TPU v7x, 32 devices: a whole 2x2x4 slice. The times are simulated.
32 devices in a mesh: blk: 8 (over z, x), ulysses: 4 (over y, core).
Axes of the slice: x: 2, y: 2, z: 4, core: 2. Of those that a mesh axis runs over, the one named last changes fastest.
Arguments:
- tokens: bfloat16 [2, 2048, 768], P(None, ('blk', 'ulysses')), may hold values from -6 to 6
- attn_gain: bfloat16 [768], P(('blk', 'ulysses')), may hold values from 0.25 to 1.75
- qkv_weight: bfloat16 [768, 2304], P(('blk', 'ulysses')), may hold values from -0.3125 to 0.3125
- attn_out_weight: bfloat16 [768, 768], P(('blk', 'ulysses')), may hold values from -1.25 to 1.25
- mlp_gain: bfloat16 [768], P(('blk', 'ulysses')), may hold values from 0.25 to 1.75
- in_weight: bfloat16 [768, 2304], P(('blk', 'ulysses')), may hold values from -0.21875 to 0.21875
- out_weight: bfloat16 [1152, 768], P(None, ('blk', 'ulysses')), may hold values from -0.1875 to 0.1875
- cotangent: bfloat16 [2, 2048, 768], P(None, ('blk', 'ulysses')), may hold values from -6 to 6
Outputs:
- layer_output: bfloat16 [2, 2048, 768], P(None, ('blk', 'ulysses'))
- input_grad: bfloat16 [2, 2048, 768], P(None, ('blk', 'ulysses'))
- attn_gain_grad: float32 [768], P(('blk', 'ulysses'))
- qkv_weight_grad: float32 [768, 2304], P(('blk', 'ulysses'))
- attn_out_weight_grad: float32 [768, 768], P(('blk', 'ulysses'))
- mlp_gain_grad: float32 [768], P(('blk', 'ulysses'))
- in_weight_grad: float32 [768, 2304], P(('blk', 'ulysses'))
- out_weight_grad: float32 [1152, 768], P(None, ('blk', 'ulysses'))
All inputs are finite; a program needn't handle non-finite values.
Results may differ from a plain program's by a relative error of at most 0.018.
The roundings to bfloat16 on the way count: a program that leaves them out, or rounds other values in their place, can miss the bound.
Values may be sent and summed in bfloat16 or wider, within the bound.
No kernel may reach another device: no remote copies, remote signals or barrier semaphores. Data moves between devices by JAX's collectives and lax.ppermute only.
A program may use at most 256 MiB of HBM per device.

v0:
```python
import jax
import jax.numpy as jnp
from jax import lax
from jax.sharding import PartitionSpec as P

HEAD = 64


EPSILON = 1e-05
THETA = 160000.0


def from_behind(value, axis, by):
    size = lax.axis_size(axis)
    return lax.ppermute(value, axis, [(i, (i + by) % size) for i in range(size)])


def normalize(values):
    center = values - jnp.mean(values, axis=-1, keepdims=True)
    inverse = lax.rsqrt(jnp.mean(center * center, axis=-1, keepdims=True) + EPSILON)
    return (center * inverse, inverse)


def norm_back(grad_normed, normed, inverse):
    first_mean = jnp.mean(grad_normed, axis=-1, keepdims=True)
    second_mean = jnp.mean(grad_normed * normed, axis=-1, keepdims=True)
    return inverse * (grad_normed - first_mean - normed * second_mean)


def rotation(first_row, row_count, head_width):
    half_width = head_width // 2
    frequency = THETA ** (-(jnp.arange(half_width, dtype=jnp.float32) * 2.0) / head_width)
    positions = (first_row + jnp.arange(row_count, dtype=jnp.int32)).astype(jnp.float32)
    angles = positions[:, None] * frequency[None, :]
    cosine_table = jnp.concatenate([jnp.cos(angles), jnp.cos(angles)], axis=-1)
    sine_table = jnp.concatenate([jnp.sin(angles), jnp.sin(angles)], axis=-1)
    return (cosine_table, sine_table)


def rotate(values, cosine_table, sine_table, direction):
    half_width = values.shape[-1] // 2
    turned = jnp.concatenate([-values[..., half_width:], values[..., :half_width]], axis=-1)
    return values * cosine_table[:, None, :] + direction * turned * sine_table[:, None, :]


def block_grads(
    query_part,
    key_part,
    value_part,
    grad_part,
    log_part,
    dots_part,
    top_part,
    total_part,
    score_scale,
):
    scores = (
        jnp.einsum("sqhd,skhd->shqk", query_part, key_part, preferred_element_type=jnp.float32)
        * score_scale
    )
    probs = jnp.exp(scores - log_part[..., None])
    grad_probs = jnp.einsum(
        "sqhd,skhd->shqk", grad_part, value_part, preferred_element_type=jnp.float32
    )
    grad_scores = (probs * (grad_probs - dots_part[..., None])).astype(jnp.bfloat16)
    weights_low = jnp.exp(scores - top_part[..., None]).astype(jnp.bfloat16)
    grad_scaled = grad_part.astype(jnp.float32) / jnp.transpose(total_part, (0, 2, 1))[..., None]
    value_term = jnp.einsum("shqk,sqhd->skhd", weights_low.astype(jnp.float32), grad_scaled)
    return (value_term, grad_scores)


def body(
    tokens, attn_gain, qkv_weight, attn_out_weight, mlp_gain, in_weight, out_weight, cotangent
):
    sequences, per_device, model_width = tokens.shape
    groups = lax.axis_size("ulysses")
    cycle_size = lax.axis_size("blk")
    group_width = model_width // groups
    heads_here = group_width // HEAD
    group_rows = per_device * groups
    score_scale = HEAD ** (-0.5)
    qkv_full, attn_full, in_full, out_full, gain_one, gain_two = (
        lax.all_gather(qkv_weight, ("blk", "ulysses"), axis=0, tiled=True),
        lax.all_gather(attn_out_weight, ("blk", "ulysses"), axis=0, tiled=True),
        lax.all_gather(in_weight, ("blk", "ulysses"), axis=0, tiled=True),
        lax.all_gather(out_weight, ("blk", "ulysses"), axis=1, tiled=True),
        lax.all_gather(attn_gain, ("blk", "ulysses"), axis=0, tiled=True),
        lax.all_gather(mlp_gain, ("blk", "ulysses"), axis=0, tiled=True),
    )
    gain_one = gain_one.astype(jnp.float32)
    gain_two = gain_two.astype(jnp.float32)
    hidden_units = out_full.shape[0]
    inputs_wide = tokens.astype(jnp.float32).reshape(sequences * per_device, model_width)
    normed_one, inverse_one = normalize(inputs_wide)
    hidden_one = (normed_one * gain_one).astype(jnp.bfloat16)
    qkv = jnp.dot(hidden_one, qkv_full, preferred_element_type=jnp.float32).astype(jnp.bfloat16)
    packed = qkv.reshape(sequences, per_device, 3, groups, group_width)
    headwise = lax.all_to_all(packed, "ulysses", split_axis=3, concat_axis=1, tiled=True)
    headwise = headwise.reshape(sequences, group_rows, 3, heads_here, HEAD)
    cosine_table, sine_table = rotation(lax.axis_index("blk") * group_rows, group_rows, HEAD)
    queries = rotate(headwise[:, :, 0].astype(jnp.float32), cosine_table, sine_table, 1.0).astype(
        jnp.bfloat16
    )
    key_rows = rotate(headwise[:, :, 1].astype(jnp.float32), cosine_table, sine_table, 1.0).astype(
        jnp.bfloat16
    )
    value_rows = headwise[:, :, 2]
    start_top = jnp.full((sequences, heads_here, group_rows), -1e30, jnp.float32)
    zeros_rows = jnp.zeros((sequences, group_rows, heads_here, HEAD), jnp.float32)
    key_piece = lax.all_gather(key_rows, "blk", axis=1, tiled=True)
    value_piece = lax.all_gather(value_rows, "blk", axis=1, tiled=True)
    scores = (
        jnp.einsum("sqhd,skhd->shqk", queries, key_piece, preferred_element_type=jnp.float32)
        * score_scale
    )
    new_top = jnp.maximum(start_top, jnp.max(scores, axis=-1))
    weights = jnp.exp(scores - new_top[..., None])
    attend_row_total = jnp.sum(weights, axis=-1)
    update = jnp.einsum(
        "shqk,skhd->sqhd",
        weights.astype(jnp.bfloat16),
        value_piece,
        preferred_element_type=jnp.float32,
    )
    weighted = update
    row_top, row_total, weighted = (new_top, attend_row_total, weighted)
    log_total = row_top + jnp.log(row_total)
    attn_wide = weighted / jnp.transpose(row_total, (0, 2, 1))[..., None]
    attn_low = attn_wide.astype(jnp.bfloat16).reshape(sequences, group_rows, 1, group_width)
    token_rows = lax.all_to_all(attn_low, "ulysses", split_axis=1, concat_axis=2, tiled=True)
    attn_cat = token_rows.reshape(sequences * per_device, model_width)
    middle = inputs_wide + jnp.dot(attn_cat, attn_full, preferred_element_type=jnp.float32)
    normed_two, inverse_two = normalize(middle)
    hidden_two = (normed_two * gain_two).astype(jnp.bfloat16)
    joint = jnp.dot(hidden_two, in_full, preferred_element_type=jnp.float32)

    def geglu(joint_pre):
        return (
            jax.nn.gelu(joint_pre[:, :hidden_units], approximate=False)
            * joint_pre[:, hidden_units:]
        )

    act_wide, geglu_back = jax.vjp(geglu, joint)
    activation = act_wide.astype(jnp.bfloat16)
    result = middle + jnp.dot(activation, out_full, preferred_element_type=jnp.float32)
    layer_output = result.astype(jnp.bfloat16).reshape(sequences, per_device, model_width)
    grad_out = cotangent.reshape(sequences * per_device, model_width)
    grad_wout = jnp.einsum("tf,td->fd", activation, grad_out, preferred_element_type=jnp.float32)
    grad_act = jnp.einsum("td,fd->tf", grad_out, out_full, preferred_element_type=jnp.float32)
    grad_joint = geglu_back(grad_act)[0].astype(jnp.bfloat16)
    grad_win = jnp.einsum("tc,tf->cf", hidden_two, grad_joint, preferred_element_type=jnp.float32)
    grad_hidden_two = jnp.einsum(
        "tf,cf->tc", grad_joint, in_full, preferred_element_type=jnp.float32
    )
    grad_gain_two = jnp.sum(grad_hidden_two * normed_two, axis=0)
    grad_middle = grad_out.astype(jnp.float32) + norm_back(
        grad_hidden_two * gain_two, normed_two, inverse_two
    )
    grad_branch = grad_middle.astype(jnp.bfloat16)
    grad_wattn = jnp.einsum("tc,td->cd", attn_cat, grad_branch, preferred_element_type=jnp.float32)
    grad_cat = jnp.einsum(
        "td,cd->tc", grad_branch, attn_full, preferred_element_type=jnp.float32
    ).astype(jnp.bfloat16)
    grad_heads_in = lax.all_to_all(
        grad_cat.reshape(sequences, per_device, groups, group_width),
        "ulysses",
        split_axis=2,
        concat_axis=1,
        tiled=True,
    )
    grad_attn = grad_heads_in.reshape(sequences, group_rows, heads_here, HEAD)
    row_dots = jnp.transpose(jnp.sum(grad_attn.astype(jnp.float32) * attn_wide, axis=-1), (0, 2, 1))

    def cycle_step(step_index, state_now):
        key_now, value_now, grad_key, grad_value, grad_query = state_now
        value_term, grad_scores = block_grads(
            queries,
            key_now,
            value_now,
            grad_attn,
            log_total,
            row_dots,
            row_top,
            row_total,
            score_scale,
        )
        grad_value = grad_value + value_term
        grad_key = grad_key + score_scale * jnp.einsum(
            "shqk,sqhd->skhd", grad_scores, queries, preferred_element_type=jnp.float32
        )
        grad_query = grad_query + score_scale * jnp.einsum(
            "shqk,skhd->sqhd", grad_scores, key_now, preferred_element_type=jnp.float32
        )
        key_now, value_now = from_behind((key_now, value_now), "blk", 1)
        grad_key, grad_value = (
            from_behind(grad_key.astype(jnp.bfloat16), "blk", 1).astype(grad_key.dtype),
            from_behind(grad_value.astype(jnp.bfloat16), "blk", 1).astype(grad_value.dtype),
        )
        return (key_now, value_now, grad_key, grad_value, grad_query)

    final_state = lax.fori_loop(
        0, cycle_size, cycle_step, (key_rows, value_rows, zeros_rows, zeros_rows, zeros_rows)
    )
    grad_key, grad_value, grad_query = (final_state[2], final_state[3], final_state[4])
    grad_query = rotate(grad_query, cosine_table, sine_table, -1.0)
    grad_key = rotate(grad_key, cosine_table, sine_table, -1.0)
    grad_stack = jnp.stack([grad_query, grad_key, grad_value], axis=2).astype(jnp.bfloat16)
    grad_stack = grad_stack.reshape(sequences, group_rows, 3, 1, group_width)
    grad_tokens = lax.all_to_all(grad_stack, "ulysses", split_axis=1, concat_axis=3, tiled=True)
    grad_qkv = grad_tokens.reshape(sequences * per_device, 3 * model_width)
    grad_wqkv = jnp.einsum("tc,tf->cf", hidden_one, grad_qkv, preferred_element_type=jnp.float32)
    grad_hidden_one = jnp.einsum(
        "tf,cf->tc", grad_qkv, qkv_full, preferred_element_type=jnp.float32
    )
    grad_gain_one = jnp.sum(grad_hidden_one * normed_one, axis=0)
    grad_input = grad_middle + norm_back(grad_hidden_one * gain_one, normed_one, inverse_one)
    input_grad = grad_input.astype(jnp.bfloat16).reshape(sequences, per_device, model_width)
    shard_qkv, shard_attn, shard_in, shard_out, shard_one, shard_two = (
        lax.psum_scatter(grad_wqkv, ("blk", "ulysses"), scatter_dimension=0, tiled=True),
        lax.psum_scatter(grad_wattn, ("blk", "ulysses"), scatter_dimension=0, tiled=True),
        lax.psum_scatter(grad_win, ("blk", "ulysses"), scatter_dimension=0, tiled=True),
        lax.psum_scatter(grad_wout, ("blk", "ulysses"), scatter_dimension=1, tiled=True),
        lax.psum_scatter(grad_gain_one, ("blk", "ulysses"), scatter_dimension=0, tiled=True),
        lax.psum_scatter(grad_gain_two, ("blk", "ulysses"), scatter_dimension=0, tiled=True),
    )
    return (
        layer_output,
        input_grad,
        shard_one,
        shard_qkv,
        shard_attn,
        shard_two,
        shard_in,
        shard_out,
    )


def solution(mesh):
    placed = (
        P(None, ("blk", "ulysses"), None),
        P(("blk", "ulysses")),
        P(("blk", "ulysses"), None),
        P(("blk", "ulysses"), None),
        P(("blk", "ulysses")),
        P(("blk", "ulysses"), None),
        P(None, ("blk", "ulysses")),
        P(None, ("blk", "ulysses"), None),
    )
    return jax.shard_map(
        body,
        mesh=mesh,
        in_specs=placed,
        out_specs=(
            P(None, ("blk", "ulysses"), None),
            P(None, ("blk", "ulysses"), None),
            P(("blk", "ulysses")),
            P(("blk", "ulysses"), None),
            P(("blk", "ulysses"), None),
            P(("blk", "ulysses")),
            P(("blk", "ulysses"), None),
            P(None, ("blk", "ulysses")),
        ),
        check_vma=False,
    )
```

profile of v0, /device:TPU:0, one launch (start us, length us, event | category | flops | bytes accessed | tf_op | source)
XLA Modules:
  0.0 867.9 jit_solution(4147596167485549714)
XLA Ops:
  9.6 42.2 %all-reduce.8 = (bf16[768]{0:T(1024)(128)(2,1)S(1)}, bf16[768]{0:T(1024)(128)(2,1)S(1)}) all-reduce(bf16[768]{0:T(1024)(128)(2,1)S(1)} %dynamic-update-slice, bf16[768]{0:T(1024)(128)(2,1)S(1)} %dynamic-update-slice.1), channel_id=1, replica_groups=mesh['blk'=8,'ulysses'=4] {'blk','ulysses'}, use_global_device_ids=true, to_apply=%add.2 | all-reduce | flops 1536 | bytes 6144
  55.8 18.1 %all-gather.8.cloned.1.call-done = bf16[768,2304]{1,0:T(8,128)(2,1)} async-done(((bf16[24,2304]{1,0:T(8,128)(2,1)}), bf16[768,2304]{1,0:T(8,128)(2,1)}) %all-gather.8.cloned.1.call-update) | async-done | bytes 3538960 | tf_op jit(solution)/shard_map/all_gather | solution.py:83
  73.8 2.6 convolution_convert_fusion
  78.3 3.5 all-to-all-start
  82.7 10.7 %all-to-all-done = bf16[2,64,3,4,192]{4,1,2,0,3:T(8,128)(2,1)S(1)} async-done(((bf16[2,64,3,4,192]{4,1,2,0,3:T(8,128)(2,1)}), bf16[2,64,3,4,192]{4,1,2,0,3:T(8,128)(2,1)S(1)}, u32[]{:S(2)}, u32[]{:S(2)}) %all-to-all-start) | async-done | bytes 589856 | tf_op jit(solution)/shard_map/all_to_all | solution.py:98
  99.1 41.7 %all-gather.10.cloned.1.call-done = bf16[2,2048,3,64]{1,3,2,0:T(8,128)(2,1)} async-done(((bf16[2,256,3,64]{1,3,2,0:T(8,128)(2,1)}), bf16[2,2048,3,64]{1,3,2,0:T(8,128)(2,1)}) %all-gather.10.cloned.1.call-update) | async-done | bytes 1572880 | tf_op jit(solution)/shard_map/all_gather | solution.py:110
  140.8 3.3 multiply_reduce_fusion
  144.2 4.5 copy-done
  148.6 2.4 fusion.11
  151.1 35.8 %all-gather.18.cloned.1.call-done = bf16[2,2048,1,3,64]{1,4,3,0,2:T(8,128)(2,1)} async-done(((bf16[2,256,1,3,64]{1,4,3,0,2:T(8,128)(2,1)}), bf16[2,2048,1,3,64]{1,4,3,0,2:T(8,128)(2,1)}) %all-gather.18.cloned.1.call-update) | async-done | bytes 1572880 | tf_op jit(solution)/shard_map/all_gather | solution.py:111
  186.9 8.2 fusion.56
  196.0 3.4 all-to-all-start.1
  199.6 5.8 all-to-all-done.1
  205.9 36.1 %all-gather.12.cloned.1.call-done = bf16[768,768]{1,0:T(8,128)(2,1)} async-done(((bf16[24,768]{1,0:T(8,128)(2,1)}), bf16[768,768]{1,0:T(8,128)(2,1)}) %all-gather.12.cloned.1.call-update) | async-done | bytes 1179664 | tf_op jit(solution)/shard_map/all_gather | solution.py:84
  244.0 59.9 %all-gather.14.cloned.1.call-done = bf16[768,2304]{1,0:T(8,128)(2,1)} async-done(((bf16[24,2304]{1,0:T(8,128)(2,1)}), bf16[768,2304]{1,0:T(8,128)(2,1)}) %all-gather.14.cloned.1.call-update) | async-done | bytes 3538960 | tf_op jit(solution)/shard_map/all_gather | solution.py:85
  303.9 2.7 fusion.54
  306.6 54.5 %all-gather.16.cloned.1.call-done = bf16[1152,768]{0,1:T(8,128)(2,1)} async-done(((bf16[1152,24]{0,1:T(8,128)(2,1)}), bf16[1152,768]{0,1:T(8,128)(2,1)}) %all-gather.16.cloned.1.call-update) | async-done | bytes 1769488 | tf_op jit(solution)/shard_map/all_gather | solution.py:86
  361.1 3.2 fusion.45
  368.8 2.5 fusion.59
  375.7 3.4 all-to-all-start.2
  379.2 4.7 fusion.49
  387.3 184.9 %while.19 = (s32[]{:T(128)}, bf16[2,256,3,64]{1,3,2,0:T(8,128)(2,1)}, bf16[2,256,3,64]{1,3,2,0:T(8,128)(2,1)}, f32[2,256,3,64]{1,3,2,0:T(8,128)}, f32[2,256,3,64...) while((s32[]{:T(128)}, ...), condition=%wide.region_10.0_spmd.clone, body=%wide.region_9.0_spmd.clone.sunk | while | flops 255787008 | bytes 18751904 | solution.py:201
  395.6 2.0 fusion.110
  399.7 7.6 collective-permute-done.2
  420.3 2.1 fusion.111
  422.4 14.6 %collective-permute-done.2 = bf16[2,256,3,64]{1,3,2,0:T(8,128)(2,1)} collective-permute-done((bf16[2,256,3,64]{1,3,2,0:T(8,128)(2,1)}, bf16[2,256,3,64]{1,3,2,0:T(8,128)(2,1)}, u32[]{:S(2)}, u32[]{:S(2)}) %collective-permute-start.2) | collective-permute-done | bytes 196640 | tf_op jit(solution)/shard_map/while/body/eval_jaxpr/ppermute | solution.py:15
  447.0 2.1 fusion.111
  449.1 12.9 %collective-permute-done.2 = bf16[2,256,3,64]{1,3,2,0:T(8,128)(2,1)} collective-permute-done((bf16[2,256,3,64]{1,3,2,0:T(8,128)(2,1)}, bf16[2,256,3,64]{1,3,2,0:T(8,128)(2,1)}, u32[]{:S(2)}, u32[]{:S(2)}) %collective-permute-start.2) | collective-permute-done | bytes 196640 | tf_op jit(solution)/shard_map/while/body/eval_jaxpr/ppermute | solution.py:15
  471.9 2.2 fusion.111
  474.0 10.6 %collective-permute-done.2 = bf16[2,256,3,64]{1,3,2,0:T(8,128)(2,1)} collective-permute-done((bf16[2,256,3,64]{1,3,2,0:T(8,128)(2,1)}, bf16[2,256,3,64]{1,3,2,0:T(8,128)(2,1)}, u32[]{:S(2)}, u32[]{:S(2)}) %collective-permute-start.2) | collective-permute-done | bytes 196640 | tf_op jit(solution)/shard_map/while/body/eval_jaxpr/ppermute | solution.py:15
  494.5 2.2 fusion.111
  496.6 8.0 collective-permute-done.2
  512.4 2.0 fusion.110
  514.4 2.9 collective-permute-start.3
  517.4 2.2 fusion.111
  519.6 4.2 collective-permute-done.2
  528.5 2.8 collective-permute-start.1
  537.0 2.2 fusion.111
  539.1 3.9 collective-permute-done.2
  556.3 2.2 fusion.111
  558.5 11.0 %collective-permute-done.2 = bf16[2,256,3,64]{1,3,2,0:T(8,128)(2,1)} collective-permute-done((bf16[2,256,3,64]{1,3,2,0:T(8,128)(2,1)}, bf16[2,256,3,64]{1,3,2,0:T(8,128)(2,1)}, u32[]{:S(2)}, u32[]{:S(2)}) %collective-permute-start.2) | collective-permute-done | bytes 196640 | tf_op jit(solution)/shard_map/while/body/eval_jaxpr/ppermute | solution.py:15
  577.6 5.3 all-to-all-start.3
  583.1 11.5 %all-to-all-done.3 = bf16[2,256,3,1,192]{4,0,3,2,1:T(2,128)(2,1)S(1)} async-done(((bf16[2,256,3,1,192]{4,0,3,2,1:T(2,128)(2,1)}), bf16[2,256,3,1,192]{4,0,3,2,1:T(2,128)(2,1)S(1)}, u32[]{:S(2)}, u32[]{:S(2)}) %all-to-all-start.3) | async-done | bytes 589856 | tf_op jit(solution)/shard_map/all_to_all | solution.py:209
  596.0 4.0 fusion.58
  603.0 3.5 multiply_reduce_fusion.2
  606.4 37.0 %all-reduce.7 = (f32[768]{0:T(1024)S(1)}, f32[768]{0:T(1024)S(1)}) all-reduce(f32[768]{0:T(1024)S(1)} %get-tuple-element.116, f32[768]{0:T(1024)S(1)} %copy-done.28), channel_id=3, replica_groups=mesh['blk'=8,'ulysses'=4] {'blk','ulysses'}, use_global_device_ids=true, to_apply=%region_14.0.clone | all-reduce | flops 1536 | bytes 12288
  645.5 91.0 %reduce-scatter.11.cloned.1.call-done = f32[24,2304]{1,0:T(8,128)} async-done(((f32[768,2304]{1,0:T(8,128)}), f32[24,2304]{1,0:T(8,128)}) %reduce-scatter.11.cloned.1.call-update) | async-done | bytes 221200 | tf_op jit(solution)/shard_map/reduce_scatter | solution.py:221
  736.5 124.6 %reduce-scatter.7.cloned.1.call-done = f32[24,2304]{1,0:T(8,128)} async-done(((f32[768,2304]{1,0:T(8,128)}), f32[24,2304]{1,0:T(8,128)}) %reduce-scatter.7.cloned.1.call-update) | async-done | bytes 221200 | tf_op jit(solution)/shard_map/reduce_scatter | solution.py:219
  (337 shorter events, 128.7 us)
Async XLA Ops:
  7.2 66.7 %all-gather.8.cloned.1.call-start = ((), (), s32[]{:S(2)}) async-start(), calls=%async_computation.8 | async-start | bytes 3649536 | tf_op jit(solution)/shard_map/all_gather | solution.py:83
  78.3 15.1 %all-to-all-start = ((bf16[2,64,3,4,192]{4,1,2,0,3:T(8,128)(2,1)}), bf16[2,64,3,4,192]{4,1,2,0,3:T(8,128)(2,1)S(1)}, u32[]{:S(2)}, u32[]{:S(2)}) async-start(bf16[2,64,3,4,192]{4,1,2,0,3:T(8,128)(2,1)} %copy.38), calls=%async_computation | async-start | bytes 1572864 | tf_op jit(solution)/shard_map/all_to_all | solution.py:98
  81.8 59.0 %all-gather.10.cloned.1.call-start = ((), (), s32[]{:S(2)}) async-start(), calls=%async_computation.9 | async-start | bytes 1769472 | tf_op jit(solution)/shard_map/all_gather | solution.py:110
  96.6 90.3 %all-gather.18.cloned.1.call-start = ((), (), s32[]{:S(2)}) async-start(), calls=%async_computation.16 | async-start | bytes 1769472 | tf_op jit(solution)/shard_map/all_gather | solution.py:111
  97.3 144.7 %all-gather.12.cloned.1.call-start = ((), (), s32[]{:S(2)}) async-start(), calls=%async_computation.10 | async-start | bytes 1216512 | tf_op jit(solution)/shard_map/all_gather | solution.py:84
  97.9 206.0 %all-gather.14.cloned.1.call-start = ((), (), s32[]{:S(2)}) async-start(), calls=%async_computation.11 | async-start | bytes 3649536 | tf_op jit(solution)/shard_map/all_gather | solution.py:85
  98.5 262.6 %all-gather.16.cloned.1.call-start = ((), (), s32[]{:S(2)}) async-start(), calls=%async_computation.12 | async-start | bytes 1824768 | tf_op jit(solution)/shard_map/all_gather | solution.py:86
  196.0 9.4 %all-to-all-start.1 = ((bf16[2,256,1,192]{3,0,2,1:T(2,128)(2,1)}), bf16[2,256,1,192]{3,0,2,1:T(2,128)(2,1)S(1)}, u32[]{:S(2)}, u32[]{:S(2)}) async-start(bf16[2,256,1,192]{3,0,2,1:T(2,128)(2,1)} %copy.43), calls=%async_computation.1 | async-start | bytes 524288 | tf_op jit(solution)/shard_map/all_to_all | solution.py:130
  199.4 446.1 %reduce-scatter.9.cloned.1.call-start = ((), (), s32[]{:S(2)}) async-start(), calls=%async_computation.14 | async-start | bytes 2433024 | tf_op jit(solution)/shard_map/reduce_scatter | solution.py:220
  243.9 122.6 %copy-start.29 = (f32[128]{0:T(128)}, f32[128]{0:T(128)S(1)}, u32[]{:S(2)}) copy-start(f32[128]{0:T(128)S(1)} %add_rsqrt_fusion.1) | copy-start | bytes 1540
  243.9 117.1 %copy-start.15 = (bf16[2,64,768]{2,1,0:T(8,128)(2,1)S(1)}, bf16[2,64,768]{2,1,0:T(8,128)(2,1)}, u32[]{:S(2)}) copy-start(bf16[2,64,768]{2,1,0:T(8,128)(2,1)} %param.17) | copy-start | bytes 589828
  368.7 276.7 %reduce-scatter.13.cloned.1.call-start = ((), (), s32[]{:S(2)}) async-start(), calls=%async_computation.17 | async-start | bytes 3649536
  375.7 9.4 %all-to-all-start.2 = ((bf16[2,64,4,192]{3,1,0,2:T(8,128)(2,1)}), bf16[2,64,4,192]{3,1,0,2:T(8,128)(2,1)S(1)}, u32[]{:S(2)}, u32[]{:S(2)}) async-start(bf16[2,64,4,192]{3,1,0,2:T(8,128)(2,1)} %copy.46), calls=%async_computation.2 | async-start | bytes 524288 | tf_op jit(solution)/shard_map/all_to_all | solution.py:164
  379.1 357.4 %reduce-scatter.11.cloned.1.call-start = ((), (), s32[]{:S(2)}) async-start(), calls=%async_computation.15 | async-start | bytes 7299072 | tf_op jit(solution)/shard_map/reduce_scatter | solution.py:221
  388.3 22.6 %collective-permute-start = (bf16[2,256,3,64]{1,3,2,0:T(8,128)(2,1)S(1)}, bf16[2,256,3,64]{1,3,2,0:T(8,128)(2,1)}, u32[]{:S(2)}, u32[]{:S(2)}) collective-permute-start(bf16[2,256,3,64]{1,3,2,0:T(8,128)(2,1)S(1)} %copy.62), channel_id=1, source_target_pairs={{0,4},{4,8},{8,12},{12,16},{16,20},{20,24},{24,28},{28,0},{1,5},{5... | collective-permute-start | bytes 589832 | tf_op jit(solution)/shard_map/while/body/eval_jaxpr/ppermute | solution.py:15
  390.6 20.3 %collective-permute-start.1 = (bf16[2,256,3,64]{1,3,2,0:T(8,128)(2,1)S(1)}, bf16[2,256,3,64]{1,3,2,0:T(8,128)(2,1)}, u32[]{:S(2)}, u32[]{:S(2)}) collective-permute-start(bf16[2,256,3,64]{1,3,2,0:T(8,128)(2,1)S(1)} %copy.63), channel_id=1, source_target_pairs={{0,4},{4,8},{8,12},{12,16},{16,20},{20,24},{24,28},{28,0},{1,5},{5... | collective-permute-start | bytes 589832 | tf_op jit(solution)/shard_map/while/body/eval_jaxpr/ppermute | solution.py:15
  394.2 13.1 %collective-permute-start.2 = (bf16[2,256,3,64]{1,3,2,0:T(8,128)(2,1)}, bf16[2,256,3,64]{1,3,2,0:T(8,128)(2,1)}, u32[]{:S(2)}, u32[]{:S(2)}) collective-permute-start(bf16[2,256,3,64]{1,3,2,0:T(8,128)(2,1)} %fusion.109), channel_id=1, source_target_pairs={{0,4},{4,8},{8,12},{12,16},{16,20},{20,24},{24,28},{28,0},{1,5},{5... | collective-permute-start | bytes 589832 | tf_op jit(solution)/shard_map/while/body/eval_jaxpr/ppermute | solution.py:15
  397.6 12.4 %collective-permute-start.3 = (bf16[2,256,3,64]{1,3,2,0:T(8,128)(2,1)}, bf16[2,256,3,64]{1,3,2,0:T(8,128)(2,1)S(1)}, u32[]{:S(2)}, u32[]{:S(2)}) collective-permute-start(bf16[2,256,3,64]{1,3,2,0:T(8,128)(2,1)} %fusion.110), channel_id=1, source_target_pairs={{0,4},{4,8},{8,12},{12,16},{16,20},{20,24},{24,28},{28,0},{1,5},{5... | collective-permute-start | bytes 589832 | tf_op jit(solution)/shard_map/while/body/eval_jaxpr/ppermute | solution.py:15
  411.8 28.1 %collective-permute-start = (bf16[2,256,3,64]{1,3,2,0:T(8,128)(2,1)S(1)}, bf16[2,256,3,64]{1,3,2,0:T(8,128)(2,1)}, u32[]{:S(2)}, u32[]{:S(2)}) collective-permute-start(bf16[2,256,3,64]{1,3,2,0:T(8,128)(2,1)S(1)} %copy.62), channel_id=1, source_target_pairs={{0,4},{4,8},{8,12},{12,16},{16,20},{20,24},{24,28},{28,0},{1,5},{5... | collective-permute-start | bytes 589832 | tf_op jit(solution)/shard_map/while/body/eval_jaxpr/ppermute | solution.py:15
  412.7 27.1 %collective-permute-start.1 = (bf16[2,256,3,64]{1,3,2,0:T(8,128)(2,1)S(1)}, bf16[2,256,3,64]{1,3,2,0:T(8,128)(2,1)}, u32[]{:S(2)}, u32[]{:S(2)}) collective-permute-start(bf16[2,256,3,64]{1,3,2,0:T(8,128)(2,1)S(1)} %copy.63), channel_id=1, source_target_pairs={{0,4},{4,8},{8,12},{12,16},{16,20},{20,24},{24,28},{28,0},{1,5},{5... | collective-permute-start | bytes 589832 | tf_op jit(solution)/shard_map/while/body/eval_jaxpr/ppermute | solution.py:15
  415.9 21.1 %collective-permute-start.2 = (bf16[2,256,3,64]{1,3,2,0:T(8,128)(2,1)}, bf16[2,256,3,64]{1,3,2,0:T(8,128)(2,1)}, u32[]{:S(2)}, u32[]{:S(2)}) collective-permute-start(bf16[2,256,3,64]{1,3,2,0:T(8,128)(2,1)} %fusion.109), channel_id=1, source_target_pairs={{0,4},{4,8},{8,12},{12,16},{16,20},{20,24},{24,28},{28,0},{1,5},{5... | collective-permute-start | bytes 589832 | tf_op jit(solution)/shard_map/while/body/eval_jaxpr/ppermute | solution.py:15
  418.5 20.6 %collective-permute-start.3 = (bf16[2,256,3,64]{1,3,2,0:T(8,128)(2,1)}, bf16[2,256,3,64]{1,3,2,0:T(8,128)(2,1)S(1)}, u32[]{:S(2)}, u32[]{:S(2)}) collective-permute-start(bf16[2,256,3,64]{1,3,2,0:T(8,128)(2,1)} %fusion.110), channel_id=1, source_target_pairs={{0,4},{4,8},{8,12},{12,16},{16,20},{20,24},{24,28},{28,0},{1,5},{5... | collective-permute-start | bytes 589832 | tf_op jit(solution)/shard_map/while/body/eval_jaxpr/ppermute | solution.py:15
  440.8 24.1 %collective-permute-start = (bf16[2,256,3,64]{1,3,2,0:T(8,128)(2,1)S(1)}, bf16[2,256,3,64]{1,3,2,0:T(8,128)(2,1)}, u32[]{:S(2)}, u32[]{:S(2)}) collective-permute-start(bf16[2,256,3,64]{1,3,2,0:T(8,128)(2,1)S(1)} %copy.62), channel_id=1, source_target_pairs={{0,4},{4,8},{8,12},{12,16},{16,20},{20,24},{24,28},{28,0},{1,5},{5... | collective-permute-start | bytes 589832 | tf_op jit(solution)/shard_map/while/body/eval_jaxpr/ppermute | solution.py:15
  441.7 23.2 %collective-permute-start.1 = (bf16[2,256,3,64]{1,3,2,0:T(8,128)(2,1)S(1)}, bf16[2,256,3,64]{1,3,2,0:T(8,128)(2,1)}, u32[]{:S(2)}, u32[]{:S(2)}) collective-permute-start(bf16[2,256,3,64]{1,3,2,0:T(8,128)(2,1)S(1)} %copy.63), channel_id=1, source_target_pairs={{0,4},{4,8},{8,12},{12,16},{16,20},{20,24},{24,28},{28,0},{1,5},{5... | collective-permute-start | bytes 589832 | tf_op jit(solution)/shard_map/while/body/eval_jaxpr/ppermute | solution.py:15
  444.8 17.3 %collective-permute-start.2 = (bf16[2,256,3,64]{1,3,2,0:T(8,128)(2,1)}, bf16[2,256,3,64]{1,3,2,0:T(8,128)(2,1)}, u32[]{:S(2)}, u32[]{:S(2)}) collective-permute-start(bf16[2,256,3,64]{1,3,2,0:T(8,128)(2,1)} %fusion.109), channel_id=1, source_target_pairs={{0,4},{4,8},{8,12},{12,16},{16,20},{20,24},{24,28},{28,0},{1,5},{5... | collective-permute-start | bytes 589832 | tf_op jit(solution)/shard_map/while/body/eval_jaxpr/ppermute | solution.py:15
  446.8 17.2 %collective-permute-start.3 = (bf16[2,256,3,64]{1,3,2,0:T(8,128)(2,1)}, bf16[2,256,3,64]{1,3,2,0:T(8,128)(2,1)S(1)}, u32[]{:S(2)}, u32[]{:S(2)}) collective-permute-start(bf16[2,256,3,64]{1,3,2,0:T(8,128)(2,1)} %fusion.110), channel_id=1, source_target_pairs={{0,4},{4,8},{8,12},{12,16},{16,20},{20,24},{24,28},{28,0},{1,5},{5... | collective-permute-start | bytes 589832 | tf_op jit(solution)/shard_map/while/body/eval_jaxpr/ppermute | solution.py:15
  465.8 21.6 %collective-permute-start = (bf16[2,256,3,64]{1,3,2,0:T(8,128)(2,1)S(1)}, bf16[2,256,3,64]{1,3,2,0:T(8,128)(2,1)}, u32[]{:S(2)}, u32[]{:S(2)}) collective-permute-start(bf16[2,256,3,64]{1,3,2,0:T(8,128)(2,1)S(1)} %copy.62), channel_id=1, source_target_pairs={{0,4},{4,8},{8,12},{12,16},{16,20},{20,24},{24,28},{28,0},{1,5},{5... | collective-permute-start | bytes 589832 | tf_op jit(solution)/shard_map/while/body/eval_jaxpr/ppermute | solution.py:15
  466.7 20.7 %collective-permute-start.1 = (bf16[2,256,3,64]{1,3,2,0:T(8,128)(2,1)S(1)}, bf16[2,256,3,64]{1,3,2,0:T(8,128)(2,1)}, u32[]{:S(2)}, u32[]{:S(2)}) collective-permute-start(bf16[2,256,3,64]{1,3,2,0:T(8,128)(2,1)S(1)} %copy.63), channel_id=1, source_target_pairs={{0,4},{4,8},{8,12},{12,16},{16,20},{20,24},{24,28},{28,0},{1,5},{5... | collective-permute-start | bytes 589832 | tf_op jit(solution)/shard_map/while/body/eval_jaxpr/ppermute | solution.py:15
  469.8 14.8 %collective-permute-start.2 = (bf16[2,256,3,64]{1,3,2,0:T(8,128)(2,1)}, bf16[2,256,3,64]{1,3,2,0:T(8,128)(2,1)}, u32[]{:S(2)}, u32[]{:S(2)}) collective-permute-start(bf16[2,256,3,64]{1,3,2,0:T(8,128)(2,1)} %fusion.109), channel_id=1, source_target_pairs={{0,4},{4,8},{8,12},{12,16},{16,20},{20,24},{24,28},{28,0},{1,5},{5... | collective-permute-start | bytes 589832 | tf_op jit(solution)/shard_map/while/body/eval_jaxpr/ppermute | solution.py:15
  471.9 14.8 %collective-permute-start.3 = (bf16[2,256,3,64]{1,3,2,0:T(8,128)(2,1)}, bf16[2,256,3,64]{1,3,2,0:T(8,128)(2,1)S(1)}, u32[]{:S(2)}, u32[]{:S(2)}) collective-permute-start(bf16[2,256,3,64]{1,3,2,0:T(8,128)(2,1)} %fusion.110), channel_id=1, source_target_pairs={{0,4},{4,8},{8,12},{12,16},{16,20},{20,24},{24,28},{28,0},{1,5},{5... | collective-permute-start | bytes 589832 | tf_op jit(solution)/shard_map/while/body/eval_jaxpr/ppermute | solution.py:15
  488.4 19.0 %collective-permute-start = (bf16[2,256,3,64]{1,3,2,0:T(8,128)(2,1)S(1)}, bf16[2,256,3,64]{1,3,2,0:T(8,128)(2,1)}, u32[]{:S(2)}, u32[]{:S(2)}) collective-permute-start(bf16[2,256,3,64]{1,3,2,0:T(8,128)(2,1)S(1)} %copy.62), channel_id=1, source_target_pairs={{0,4},{4,8},{8,12},{12,16},{16,20},{20,24},{24,28},{28,0},{1,5},{5... | collective-permute-start | bytes 589832 | tf_op jit(solution)/shard_map/while/body/eval_jaxpr/ppermute | solution.py:15
  489.3 18.1 %collective-permute-start.1 = (bf16[2,256,3,64]{1,3,2,0:T(8,128)(2,1)S(1)}, bf16[2,256,3,64]{1,3,2,0:T(8,128)(2,1)}, u32[]{:S(2)}, u32[]{:S(2)}) collective-permute-start(bf16[2,256,3,64]{1,3,2,0:T(8,128)(2,1)S(1)} %copy.63), channel_id=1, source_target_pairs={{0,4},{4,8},{8,12},{12,16},{16,20},{20,24},{24,28},{28,0},{1,5},{5... | collective-permute-start | bytes 589832 | tf_op jit(solution)/shard_map/while/body/eval_jaxpr/ppermute | solution.py:15
  492.4 12.2 %collective-permute-start.2 = (bf16[2,256,3,64]{1,3,2,0:T(8,128)(2,1)}, bf16[2,256,3,64]{1,3,2,0:T(8,128)(2,1)}, u32[]{:S(2)}, u32[]{:S(2)}) collective-permute-start(bf16[2,256,3,64]{1,3,2,0:T(8,128)(2,1)} %fusion.109), channel_id=1, source_target_pairs={{0,4},{4,8},{8,12},{12,16},{16,20},{20,24},{24,28},{28,0},{1,5},{5... | collective-permute-start | bytes 589832 | tf_op jit(solution)/shard_map/while/body/eval_jaxpr/ppermute | solution.py:15
  494.5 12.2 %collective-permute-start.3 = (bf16[2,256,3,64]{1,3,2,0:T(8,128)(2,1)}, bf16[2,256,3,64]{1,3,2,0:T(8,128)(2,1)S(1)}, u32[]{:S(2)}, u32[]{:S(2)}) collective-permute-start(bf16[2,256,3,64]{1,3,2,0:T(8,128)(2,1)} %fusion.110), channel_id=1, source_target_pairs={{0,4},{4,8},{8,12},{12,16},{16,20},{20,24},{24,28},{28,0},{1,5},{5... | collective-permute-start | bytes 589832 | tf_op jit(solution)/shard_map/while/body/eval_jaxpr/ppermute | solution.py:15
  508.4 18.2 %collective-permute-start = (bf16[2,256,3,64]{1,3,2,0:T(8,128)(2,1)S(1)}, bf16[2,256,3,64]{1,3,2,0:T(8,128)(2,1)}, u32[]{:S(2)}, u32[]{:S(2)}) collective-permute-start(bf16[2,256,3,64]{1,3,2,0:T(8,128)(2,1)S(1)} %copy.62), channel_id=1, source_target_pairs={{0,4},{4,8},{8,12},{12,16},{16,20},{20,24},{24,28},{28,0},{1,5},{5... | collective-permute-start | bytes 589832 | tf_op jit(solution)/shard_map/while/body/eval_jaxpr/ppermute | solution.py:15
  509.3 17.3 %collective-permute-start.1 = (bf16[2,256,3,64]{1,3,2,0:T(8,128)(2,1)S(1)}, bf16[2,256,3,64]{1,3,2,0:T(8,128)(2,1)}, u32[]{:S(2)}, u32[]{:S(2)}) collective-permute-start(bf16[2,256,3,64]{1,3,2,0:T(8,128)(2,1)S(1)} %copy.63), channel_id=1, source_target_pairs={{0,4},{4,8},{8,12},{12,16},{16,20},{20,24},{24,28},{28,0},{1,5},{5... | collective-permute-start | bytes 589832 | tf_op jit(solution)/shard_map/while/body/eval_jaxpr/ppermute | solution.py:15
  512.4 11.4 %collective-permute-start.2 = (bf16[2,256,3,64]{1,3,2,0:T(8,128)(2,1)}, bf16[2,256,3,64]{1,3,2,0:T(8,128)(2,1)}, u32[]{:S(2)}, u32[]{:S(2)}) collective-permute-start(bf16[2,256,3,64]{1,3,2,0:T(8,128)(2,1)} %fusion.109), channel_id=1, source_target_pairs={{0,4},{4,8},{8,12},{12,16},{16,20},{20,24},{24,28},{28,0},{1,5},{5... | collective-permute-start | bytes 589832 | tf_op jit(solution)/shard_map/while/body/eval_jaxpr/ppermute | solution.py:15
  514.4 11.3 %collective-permute-start.3 = (bf16[2,256,3,64]{1,3,2,0:T(8,128)(2,1)}, bf16[2,256,3,64]{1,3,2,0:T(8,128)(2,1)S(1)}, u32[]{:S(2)}, u32[]{:S(2)}) collective-permute-start(bf16[2,256,3,64]{1,3,2,0:T(8,128)(2,1)} %fusion.110), channel_id=1, source_target_pairs={{0,4},{4,8},{8,12},{12,16},{16,20},{20,24},{24,28},{28,0},{1,5},{5... | collective-permute-start | bytes 589832 | tf_op jit(solution)/shard_map/while/body/eval_jaxpr/ppermute | solution.py:15
  527.6 18.5 %collective-permute-start = (bf16[2,256,3,64]{1,3,2,0:T(8,128)(2,1)S(1)}, bf16[2,256,3,64]{1,3,2,0:T(8,128)(2,1)}, u32[]{:S(2)}, u32[]{:S(2)}) collective-permute-start(bf16[2,256,3,64]{1,3,2,0:T(8,128)(2,1)S(1)} %copy.62), channel_id=1, source_target_pairs={{0,4},{4,8},{8,12},{12,16},{16,20},{20,24},{24,28},{28,0},{1,5},{5... | collective-permute-start | bytes 589832 | tf_op jit(solution)/shard_map/while/body/eval_jaxpr/ppermute | solution.py:15
  528.5 17.6 %collective-permute-start.1 = (bf16[2,256,3,64]{1,3,2,0:T(8,128)(2,1)S(1)}, bf16[2,256,3,64]{1,3,2,0:T(8,128)(2,1)}, u32[]{:S(2)}, u32[]{:S(2)}) collective-permute-start(bf16[2,256,3,64]{1,3,2,0:T(8,128)(2,1)S(1)} %copy.63), channel_id=1, source_target_pairs={{0,4},{4,8},{8,12},{12,16},{16,20},{20,24},{24,28},{28,0},{1,5},{5... | collective-permute-start | bytes 589832 | tf_op jit(solution)/shard_map/while/body/eval_jaxpr/ppermute | solution.py:15
  534.4 8.7 %collective-permute-start.2 = (bf16[2,256,3,64]{1,3,2,0:T(8,128)(2,1)}, bf16[2,256,3,64]{1,3,2,0:T(8,128)(2,1)}, u32[]{:S(2)}, u32[]{:S(2)}) collective-permute-start(bf16[2,256,3,64]{1,3,2,0:T(8,128)(2,1)} %fusion.109), channel_id=1, source_target_pairs={{0,4},{4,8},{8,12},{12,16},{16,20},{20,24},{24,28},{28,0},{1,5},{5... | collective-permute-start | bytes 589832 | tf_op jit(solution)/shard_map/while/body/eval_jaxpr/ppermute | solution.py:15
  536.4 8.8 %collective-permute-start.3 = (bf16[2,256,3,64]{1,3,2,0:T(8,128)(2,1)}, bf16[2,256,3,64]{1,3,2,0:T(8,128)(2,1)S(1)}, u32[]{:S(2)}, u32[]{:S(2)}) collective-permute-start(bf16[2,256,3,64]{1,3,2,0:T(8,128)(2,1)} %fusion.110), channel_id=1, source_target_pairs={{0,4},{4,8},{8,12},{12,16},{16,20},{20,24},{24,28},{28,0},{1,5},{5... | collective-permute-start | bytes 589832 | tf_op jit(solution)/shard_map/while/body/eval_jaxpr/ppermute | solution.py:15
  547.0 25.2 %collective-permute-start = (bf16[2,256,3,64]{1,3,2,0:T(8,128)(2,1)S(1)}, bf16[2,256,3,64]{1,3,2,0:T(8,128)(2,1)}, u32[]{:S(2)}, u32[]{:S(2)}) collective-permute-start(bf16[2,256,3,64]{1,3,2,0:T(8,128)(2,1)S(1)} %copy.62), channel_id=1, source_target_pairs={{0,4},{4,8},{8,12},{12,16},{16,20},{20,24},{24,28},{28,0},{1,5},{5... | collective-permute-start | bytes 589832 | tf_op jit(solution)/shard_map/while/body/eval_jaxpr/ppermute | solution.py:15
  547.9 24.3 %collective-permute-start.1 = (bf16[2,256,3,64]{1,3,2,0:T(8,128)(2,1)S(1)}, bf16[2,256,3,64]{1,3,2,0:T(8,128)(2,1)}, u32[]{:S(2)}, u32[]{:S(2)}) collective-permute-start(bf16[2,256,3,64]{1,3,2,0:T(8,128)(2,1)S(1)} %copy.63), channel_id=1, source_target_pairs={{0,4},{4,8},{8,12},{12,16},{16,20},{20,24},{24,28},{28,0},{1,5},{5... | collective-permute-start | bytes 589832 | tf_op jit(solution)/shard_map/while/body/eval_jaxpr/ppermute | solution.py:15
  551.8 17.6 %collective-permute-start.2 = (bf16[2,256,3,64]{1,3,2,0:T(8,128)(2,1)}, bf16[2,256,3,64]{1,3,2,0:T(8,128)(2,1)}, u32[]{:S(2)}, u32[]{:S(2)}) collective-permute-start(bf16[2,256,3,64]{1,3,2,0:T(8,128)(2,1)} %fusion.109), channel_id=1, source_target_pairs={{0,4},{4,8},{8,12},{12,16},{16,20},{20,24},{24,28},{28,0},{1,5},{5... | collective-permute-start | bytes 589832 | tf_op jit(solution)/shard_map/while/body/eval_jaxpr/ppermute | solution.py:15
  554.4 17.0 %collective-permute-start.3 = (bf16[2,256,3,64]{1,3,2,0:T(8,128)(2,1)}, bf16[2,256,3,64]{1,3,2,0:T(8,128)(2,1)S(1)}, u32[]{:S(2)}, u32[]{:S(2)}) collective-permute-start(bf16[2,256,3,64]{1,3,2,0:T(8,128)(2,1)} %fusion.110), channel_id=1, source_target_pairs={{0,4},{4,8},{8,12},{12,16},{16,20},{20,24},{24,28},{28,0},{1,5},{5... | collective-permute-start | bytes 589832 | tf_op jit(solution)/shard_map/while/body/eval_jaxpr/ppermute | solution.py:15
  577.6 16.9 %all-to-all-start.3 = ((bf16[2,256,3,1,192]{4,0,3,2,1:T(2,128)(2,1)}), bf16[2,256,3,1,192]{4,0,3,2,1:T(2,128)(2,1)S(1)}, u32[]{:S(2)}, u32[]{:S(2)}) async-start(bf16[2,256,3,1,192]{4,0,3,2,1:T(2,128)(2,1)} %copy.48), calls=%async_computation.3 | async-start | bytes 1572864 | tf_op jit(solution)/shard_map/all_to_all | solution.py:209
  582.9 278.1 %reduce-scatter.7.cloned.1.call-start = ((), (), s32[]{:S(2)}) async-start(), calls=%async_computation.13 | async-start | bytes 7299072 | tf_op jit(solution)/shard_map/reduce_scatter | solution.py:219
  (64 other events, 424.4 us)
Sparse Core Ops, SparseCore 0:
  10.9 62.8 all-gather.7
  96.7 44.0 all-gather.9
  143.4 43.4 all-gather.17
  189.7 52.2 all-gather.11
  244.8 59.0 all-gather.13
  306.6 54.4 all-gather.15
  368.8 114.1 reduce-scatter.8
  489.9 121.3 reduce-scatter.12
  618.6 117.8 reduce-scatter.10
  742.6 118.4 reduce-scatter.6
where the time goes:
time: 870 us; the launch traced here: 868 us
  waiting for transfers between devices  570 us (66%)
  matrix products  99.2 us (11%)
  blocking collectives  79.2 us (9%)
  local copies, waits for them, and re-layouts  36 us (4%)
  other arithmetic  35.4 us (4%)
  starting transfers between devices  32.5 us (4%)
  between operations  14.8 us (2%)
    reduce_scatter x1, waiting for transfers between devices, body(): lax.psum_scatter(grad_wqkv, ('blk', 'ulysses'), scatter_dimension=0, tile...  125 us
    reduce_scatter x1, waiting for transfers between devices, body(): lax.psum_scatter(grad_win, ('blk', 'ulysses'), scatter_dimension=0, tiled...  91 us
    unnamed x2, blocking collectives  79.2 us
    ppermute x32, waiting for transfers between devices, from_behind(): lax.ppermute(value, axis, [(i, (i + by) % size) for i in range(size)])  76.3 us
    all_gather x1, waiting for transfers between devices, body(): lax.all_gather(in_weight, ('blk', 'ulysses'), axis=0, tiled=True)  59.9 us
    all_gather x1, waiting for transfers between devices, body(): lax.all_gather(out_weight, ('blk', 'ulysses'), axis=1, tiled=True)  54.5 us
    all_gather x1, waiting for transfers between devices, body(): key_piece = lax.all_gather(key_rows, 'blk', axis=1, tiled=True)  41.7 us
    all_gather x1, waiting for transfers between devices, body(): lax.all_gather(attn_out_weight, ('blk', 'ulysses'), axis=0, tiled=True)  36.1 us
  transfers between devices with their start and end apart: 46, of which 28 were waited for; matrix products, arithmetic and copies ran while one was open for 17% of the time, Pallas kernels for 0%

commit v1 on v0

--- a/solution.py
+++ b/solution.py
@@ -1,6 +1,8 @@
 import jax
 import jax.numpy as jnp
 from jax import lax
+from jax.experimental import pallas as pl
+from jax.experimental.pallas import tpu as pltpu
 from jax.sharding import PartitionSpec as P
 
 HEAD = 64
@@ -69,7 +71,7 @@
     return (value_term, grad_scores)
 
 
-def body(
+def ring_body(
     tokens, attn_gain, qkv_weight, attn_out_weight, mlp_gain, in_weight, out_weight, cotangent
 ):
     sequences, per_device, model_width = tokens.shape
@@ -235,6 +237,326 @@
     )
 
 
+AXES = ("blk", "ulysses")
+BF = jnp.bfloat16
+F32 = jnp.float32
+HEADS = 12
+SHARE = 3
+BLOCK = 256
+
+
+def swap(value, axis, bit):
+    size = lax.axis_size(axis)
+    return lax.ppermute(value, axis, [(i, i ^ bit) for i in range(size)])
+
+
+def my_bit(axis, bit):
+    return (lax.axis_index(axis) // bit) % 2
+
+
+def join(mine, other, side, axis):
+    first = jnp.stack([mine, other], axis=axis)
+    second = jnp.stack([other, mine], axis=axis)
+    return jnp.where(side == 0, first, second)
+
+
+def gather_sequence(tokens):
+    sequences, rows, width = tokens.shape
+    z2, z1, x = my_bit("blk", 4), my_bit("blk", 2), my_bit("blk", 1)
+    y, core = my_bit("ulysses", 2), my_bit("ulysses", 1)
+    keep = lax.dynamic_index_in_dim(tokens, z2, 0, keepdims=False)
+    give = lax.dynamic_index_in_dim(tokens, 1 - z2, 0, keepdims=False)
+    wide = join(keep, swap(give, "blk", 4), z2, 0)
+    wide = join(wide, swap(wide, "blk", 2), z1, 1)
+    wide = wide.reshape(2, 2, 2, rows // 2, width)
+    part_a, part_b = wide[:, :, 0], wide[:, :, 1]
+    from_a, from_b = swap(part_a, "blk", 1), swap(part_b, "ulysses", 2)
+    part_a = join(part_a, from_a, x, 2)
+    part_b = join(part_b, from_b, y, 2)
+    from_a, from_b = swap(part_a, "ulysses", 2), swap(part_b, "blk", 1)
+    part_a = join(part_a, from_a, y, 3)
+    part_b = join(part_b, from_b, x, 2)
+    wide = jnp.stack([part_a, part_b], axis=4)
+    wide = join(wide, swap(wide, "ulysses", 1), core, 4)
+    return wide.reshape(32 * rows, width)
+
+
+def halve(value, axis, bit, dim):
+    side = my_bit(axis, bit)
+    keep = lax.dynamic_index_in_dim(value, side, dim, keepdims=False)
+    give = lax.dynamic_index_in_dim(value, 1 - side, dim, keepdims=False)
+    got = swap(give, axis, bit)
+    return (keep.astype(F32) + got.astype(F32)).astype(BF)
+
+
+def scatter_rows(grads):
+    rows, columns = grads.shape
+    view = grads.reshape(2, 2, 2, 2, 2, rows // 32, columns)
+    view = halve(view, "ulysses", 1, 4)
+    half = columns // 256 * 128
+    part_a, part_b = view[..., :half], view[..., half:]
+    part_a = halve(part_a, "blk", 1, 2)
+    part_b = halve(part_b, "ulysses", 2, 3)
+    part_a = halve(part_a, "ulysses", 2, 2)
+    part_b = halve(part_b, "blk", 1, 2)
+    part_a, part_b = halve(part_a, "blk", 2, 1), halve(part_b, "blk", 2, 1)
+    part_a, part_b = halve(part_a, "blk", 4, 0), halve(part_b, "blk", 4, 0)
+    return jnp.concatenate([part_a, part_b], axis=-1)
+
+
+def exchange(value):
+    return lax.all_to_all(value, AXES, split_axis=0, concat_axis=0, tiled=True)
+
+
+def to_owners(by_pair):
+    sequences, heads = by_pair.shape[:2]
+    tail = by_pair.shape[2:]
+    grouped = by_pair.reshape(sequences, heads // SHARE, SHARE, *tail)
+    grouped = jnp.concatenate([grouped, grouped[:, :, -1:]], axis=2)
+    return grouped.reshape(sequences * heads // SHARE * (SHARE + 1), *tail)
+
+
+def from_owners(blocks):
+    tail = blocks.shape[1:]
+    grouped = blocks.reshape(2, HEADS // SHARE, SHARE + 1, *tail)[:, :, :SHARE]
+    return grouped.reshape(2, HEADS, *tail)
+
+
+def turn(values):
+    lane = lax.broadcasted_iota(jnp.int32, values.shape, 1) % HEAD
+    return jnp.where(
+        lane < HEAD // 2, -pltpu.roll(values, 3 * HEAD // 2, 1), pltpu.roll(values, HEAD // 2, 1)
+    )
+
+
+def project_kernel(tokens, gain, weight, cosine, sine, hidden, queries, key_rows, value_rows):
+    normed, inverse = normalize(tokens[...].astype(F32))
+    low = (normed * gain[...]).astype(BF)
+    hidden[...] = low
+    qkv = jnp.dot(low, weight[...], preferred_element_type=F32).astype(BF)
+    both = qkv[:, : 2 * HEAD].astype(F32)
+    both = both * cosine[...] + turn(both) * sine[...]
+    both = both.astype(BF)
+    queries[...] = both[:, :HEAD] * BF(HEAD**-0.5)
+    key_rows[...] = both[:, HEAD:]
+    value_rows[...] = qkv[:, 2 * HEAD :]
+
+
+def project(tokens, gain, weight, cosine, sine):
+    length, width = tokens.shape
+    by_row = lambda columns: pl.BlockSpec((BLOCK, columns), lambda i: (i, 0))
+    whole = lambda shape: pl.BlockSpec(shape, lambda i: (0, 0))
+    return pl.pallas_call(
+        project_kernel,
+        grid=(length // BLOCK,),
+        in_specs=[
+            by_row(width),
+            whole((1, width)),
+            whole(weight.shape),
+            by_row(2 * HEAD),
+            by_row(2 * HEAD),
+        ],
+        out_specs=[by_row(width), by_row(HEAD), by_row(HEAD), by_row(HEAD)],
+        out_shape=[jax.ShapeDtypeStruct((length, width), BF)]
+        + [jax.ShapeDtypeStruct((length, HEAD), BF)] * 3,
+        name="project",
+    )(tokens, gain, weight, cosine, sine)
+
+
+def attend_kernel(queries, key_rows, value_rows, weights, attn32, total):
+    scores = lax.dot_general(
+        queries[...], key_rows[...], (((1,), (1,)), ((), ())), preferred_element_type=F32
+    )
+    top = jnp.max(scores, axis=-1, keepdims=True)
+    expo = jnp.exp(scores - top)
+    row_total = jnp.sum(expo, axis=-1, keepdims=True)
+    low = expo.astype(BF)
+    weights[...] = low
+    mixed = jnp.dot(low, value_rows[...], preferred_element_type=F32)
+    attn32[...] = mixed / row_total
+    total[...] = row_total
+
+
+def attend(queries, key_rows, value_rows):
+    length = queries.shape[0]
+    by_row = lambda columns: pl.BlockSpec((BLOCK, columns), lambda i: (i, 0))
+    whole = pl.BlockSpec((length, HEAD), lambda i: (0, 0))
+    return pl.pallas_call(
+        attend_kernel,
+        grid=(length // BLOCK,),
+        in_specs=[by_row(HEAD), whole, whole],
+        out_specs=[by_row(length), by_row(HEAD), by_row(1)],
+        out_shape=[
+            jax.ShapeDtypeStruct((length, length), BF),
+            jax.ShapeDtypeStruct((length, HEAD), F32),
+            jax.ShapeDtypeStruct((length, 1), F32),
+        ],
+        name="attend",
+    )(queries, key_rows, value_rows)
+
+
+def attend_back_kernel(
+    grad, attn32, total, weights, queries, key_rows, value_rows, grad_query, grad_key, grad_value
+):
+    @pl.when(pl.program_id(0) == 0)
+    def _():
+        grad_key[...] = jnp.zeros_like(grad_key)
+        grad_value[...] = jnp.zeros_like(grad_value)
+
+    wide = grad[...].astype(F32)
+    dots = jnp.sum(wide * attn32[...], axis=-1, keepdims=True)
+    grad_probs = lax.dot_general(
+        grad[...], value_rows[...], (((1,), (1,)), ((), ())), preferred_element_type=F32
+    )
+    inverse = 1.0 / total[...]
+    low = weights[...]
+    grad_scores = ((low.astype(F32) * inverse) * (grad_probs - dots)).astype(BF)
+    grad_query[...] = HEAD**-0.5 * jnp.dot(
+        grad_scores, key_rows[...], preferred_element_type=F32
+    )
+    over_rows = (((0,), (0,)), ((), ()))
+    grad_value[...] += lax.dot_general(
+        low, (wide * inverse).astype(BF), over_rows, preferred_element_type=F32
+    )
+    grad_key[...] += lax.dot_general(
+        grad_scores, queries[...], over_rows, preferred_element_type=F32
+    )
+
+
+def attend_back(grad, attn32, total, weights, queries, key_rows, value_rows):
+    length = queries.shape[0]
+    by_row = lambda columns: pl.BlockSpec((BLOCK, columns), lambda i: (i, 0))
+    whole = pl.BlockSpec((length, HEAD), lambda i: (0, 0))
+    return pl.pallas_call(
+        attend_back_kernel,
+        grid=(length // BLOCK,),
+        in_specs=[
+            by_row(HEAD),
+            by_row(HEAD),
+            by_row(1),
+            by_row(length),
+            by_row(HEAD),
+            whole,
+            whole,
+        ],
+        out_specs=[by_row(HEAD), whole, whole],
+        out_shape=[jax.ShapeDtypeStruct((length, HEAD), F32)] * 3,
+        name="attend_back",
+    )(grad, attn32, total, weights, queries, key_rows, value_rows)
+
+
+def unturn(values, cosine_table, sine_table):
+    half_width = HEAD // 2
+    turned = jnp.concatenate([-values[:, half_width:], values[:, :half_width]], axis=-1)
+    return values * cosine_table - turned * sine_table
+
+
+def owner_body(
+    tokens, attn_gain, qkv_weight, attn_out_weight, mlp_gain, in_weight, out_weight, cotangent
+):
+    sequences, per_device, model_width = tokens.shape
+    hidden_units = out_weight.shape[0]
+    rows_here = qkv_weight.shape[0]
+    length = per_device * 32
+    late = jnp.concatenate(
+        [in_weight, attn_out_weight, jnp.transpose(out_weight)], axis=1
+    )
+    late_full = lax.all_gather(late, AXES, axis=0, tiled=True)
+    in_full = late_full[:, : 2 * hidden_units]
+    attn_full = late_full[:, 2 * hidden_units : 2 * hidden_units + model_width]
+    out_turned = late_full[:, 2 * hidden_units + model_width :]
+    by_head = qkv_weight.reshape(rows_here, 3, HEADS, HEAD).transpose(2, 0, 1, 3)
+    by_head = by_head.reshape(HEADS, rows_here, 3 * HEAD)
+    gains = jnp.concatenate([attn_gain, mlp_gain, jnp.zeros((3 * HEAD - 2 * rows_here,), BF)])
+    gain_rows = jnp.broadcast_to(gains, (HEADS, 8, 3 * HEAD))
+    packed = jnp.concatenate([by_head, gain_rows], axis=1)
+    packed = to_owners(jnp.stack([packed, packed]))
+    got = exchange(packed)
+    weight_here = got[:, :rows_here].reshape(model_width, 3 * HEAD)
+    gain_one = got[:, rows_here, :rows_here].reshape(1, model_width).astype(F32)
+    gain_two = got[:, rows_here, rows_here : 2 * rows_here].reshape(1, model_width).astype(F32)
+    sequence = gather_sequence(tokens)
+    cosine_table, sine_table = rotation(0, length, HEAD)
+    cosine_two = jnp.concatenate([cosine_table, cosine_table], axis=1)
+    sine_two = jnp.concatenate([sine_table, sine_table], axis=1)
+    hidden_one, queries, key_rows, value_rows = project(
+        sequence, gain_one, weight_here, cosine_two, sine_two
+    )
+    weights_low, attn32, row_total = attend(queries, key_rows, value_rows)
+    back = exchange(attn32.astype(BF).reshape(32, per_device, HEAD))
+    attn_cat = from_owners(back).transpose(0, 2, 1, 3)
+    attn_cat = attn_cat.reshape(sequences * per_device, model_width)
+    inputs_wide = tokens.astype(F32).reshape(sequences * per_device, model_width)
+    middle = inputs_wide + jnp.dot(attn_cat, attn_full, preferred_element_type=F32)
+    normed_two, inverse_two = normalize(middle)
+    hidden_two = (normed_two * gain_two).astype(BF)
+    joint = jnp.dot(hidden_two, in_full, preferred_element_type=F32)
+
+    def geglu(joint_pre):
+        return (
+            jax.nn.gelu(joint_pre[:, :hidden_units], approximate=False)
+            * joint_pre[:, hidden_units:]
+        )
+
+    act_wide, geglu_back = jax.vjp(geglu, joint)
+    activation = act_wide.astype(BF)
+    result = middle + jnp.einsum("tf,df->td", activation, out_turned, preferred_element_type=F32)
+    layer_output = result.astype(BF).reshape(sequences, per_device, model_width)
+    grad_out = cotangent.reshape(sequences * per_device, model_width)
+    grad_act = jnp.dot(grad_out, out_turned, preferred_element_type=F32)
+    grad_joint = geglu_back(grad_act)[0].astype(BF)
+    grad_hidden_two = jnp.einsum("tf,cf->tc", grad_joint, in_full, preferred_element_type=F32)
+    grad_middle = grad_out.astype(F32) + norm_back(
+        grad_hidden_two * gain_two, normed_two, inverse_two
+    )
+    grad_branch = grad_middle.astype(BF)
+    grad_cat = jnp.einsum(
+        "td,cd->tc", grad_branch, attn_full, preferred_element_type=F32
+    ).astype(BF)
+    by_pair = grad_cat.reshape(sequences, per_device, HEADS, HEAD).transpose(0, 2, 1, 3)
+    grad_attn = exchange(to_owners(by_pair)).reshape(length, HEAD)
+    grad_wout = jnp.einsum("td,tf->df", grad_out, activation, preferred_element_type=F32)
+    grad_win = jnp.einsum("tc,tf->cf", hidden_two, grad_joint, preferred_element_type=F32)
+    grad_wattn = jnp.einsum("tc,td->cd", attn_cat, grad_branch, preferred_element_type=F32)
+    late_grads = jnp.concatenate(
+        [grad_win.astype(BF), grad_wattn.astype(BF), grad_wout.astype(BF)], axis=1
+    )
+    shards = scatter_rows(late_grads).astype(F32)
+    shard_in = shards[:, : 2 * hidden_units]
+    shard_attn = shards[:, 2 * hidden_units : 2 * hidden_units + model_width]
+    shard_out = jnp.transpose(shards[:, 2 * hidden_units + model_width :])
+    shard_two = jnp.sum(shard_in * in_weight.astype(F32), axis=1) / mlp_gain.astype(F32)
+    qkv_full = lax.all_gather(qkv_weight, AXES, axis=0, tiled=True)
+    grad_query, grad_key, grad_value = attend_back(
+        grad_attn, attn32, row_total, weights_low, queries, key_rows, value_rows
+    )
+    grad_query = unturn(grad_query, cosine_table, sine_table)
+    grad_key = unturn(grad_key, cosine_table, sine_table)
+    grad_stack = jnp.concatenate([grad_query, grad_key, grad_value], axis=1).astype(BF)
+    grad_tokens = exchange(grad_stack.reshape(32, per_device, 3 * HEAD))
+    grad_whead = jnp.einsum("tc,tf->cf", hidden_one, grad_stack, preferred_element_type=F32)
+    grad_rows = from_owners(exchange(grad_whead.astype(BF).reshape(32, rows_here, 3 * HEAD)))
+    grad_rows = jnp.sum(grad_rows.astype(F32), axis=0).reshape(HEADS, rows_here, 3, HEAD)
+    shard_qkv = grad_rows.transpose(1, 2, 0, 3).reshape(rows_here, 3 * model_width)
+    shard_one = jnp.sum(shard_qkv * qkv_weight.astype(F32), axis=1) / attn_gain.astype(F32)
+    grad_qkv = from_owners(grad_tokens).reshape(sequences, HEADS, per_device, 3, HEAD)
+    grad_qkv = grad_qkv.transpose(0, 2, 3, 1, 4).reshape(sequences * per_device, 3 * model_width)
+    grad_hidden_one = jnp.einsum("tf,cf->tc", grad_qkv, qkv_full, preferred_element_type=F32)
+    normed_one, inverse_one = normalize(inputs_wide)
+    grad_input = grad_middle + norm_back(grad_hidden_one * gain_one, normed_one, inverse_one)
+    input_grad = grad_input.astype(BF).reshape(sequences, per_device, model_width)
+    return (
+        layer_output,
+        input_grad,
+        shard_one,
+        shard_qkv,
+        shard_attn,
+        shard_two,
+        shard_in,
+        shard_out,
+    )
+
+
 def solution(mesh):
     placed = (
         P(None, ("blk", "ulysses"), None),
@@ -246,8 +568,9 @@
         P(None, ("blk", "ulysses")),
         P(None, ("blk", "ulysses"), None),
     )
+    sizes = (mesh.shape["blk"], mesh.shape["ulysses"])
     return jax.shard_map(
-        body,
+        owner_body if sizes == (8, 4) else ring_body,
         mesh=mesh,
         in_specs=placed,
         out_specs=(

time: 870 us -> 298 us (0.34)
  waiting for transfers between devices: 570 us -> 105 us
  blocking collectives: 79.2 us -> 0 us
  matrix products: 99.2 us -> 20.4 us
  Pallas kernels: 0 us -> 35.3 us
  starting transfers between devices: 32.5 us -> 48.7 us
    all_gather x6 -> x2, waiting for transfers between devices: 246 us -> 0.02 us  [the longest x1 0.02 us: owner_body(): late_full = lax.all_gather(late, AXES, axis=0, tiled=True)]
    reduce_scatter x3 -> x0, waiting for transfers between devices: 216 us -> none  [the longest x1 125 us: body(): lax.psum_scatter(grad_wqkv, ('blk', 'ulysses'), scatter_dimension=0, tile...]
    unnamed x2 -> x0, blocking collectives: 79.2 us -> none
    dot_general x54 -> x11, matrix products: 99.2 us -> 20.4 us  [the longest x1 3.58 us: owner_body(): jnp.einsum('tf,cf->tc', grad_qkv, qkv_full, preferred_element_type=F32)]
    pallas_call x0 -> x3, Pallas kernels: none -> 35.3 us  [the longest x1 14.9 us: attend_back(): pl.pallas_call(attend_back_kernel, grid=(length // BLOCK,), in_specs=[by_...]
    ppermute x32 -> x16, waiting for transfers between devices: 76.3 us -> 54 us  [swap(): return lax.ppermute(value, axis, [(i, i ^ bit) for i in range(size)])]
    all_to_all x4 -> x5, waiting for transfers between devices: 29.2 us -> 50.2 us  [exchange(): return lax.all_to_all(value, AXES, split_axis=0, concat_axis=0, tiled=True)]
    convert_element_type x22 -> x14, other arithmetic: 23 us -> 7.33 us  [the longest x9 3.51 us: halve(): return (keep.astype(F32) + got.astype(F32)).astype(BF)]
  transfers between devices with their start and end apart: 46 -> 23, of which waited for: 28 -> 19; matrix products, arithmetic and copies ran while one was open for 17% -> 28% of each run, Pallas kernels for 0% -> 12%
where the time goes in v1:
time: 298 us; the launch traced here: 297 us
  waiting for transfers between devices  105 us (35%)
  starting transfers between devices  48.7 us (16%)
  other arithmetic  37 us (12%)
  local copies, waits for them, and re-layouts  36.1 us (12%)
  Pallas kernels  35.3 us (12%)
  matrix products  20.4 us (7%)
  between operations  14.9 us (5%)
    ppermute x16, waiting for transfers between devices, swap(): return lax.ppermute(value, axis, [(i, i ^ bit) for i in range(size)])  54 us
    all_to_all x5, waiting for transfers between devices, exchange(): return lax.all_to_all(value, AXES, split_axis=0, concat_axis=0, tiled=True)  50.2 us
    all_to_all x5, starting transfers between devices, exchange(): return lax.all_to_all(value, AXES, split_axis=0, concat_axis=0, tiled=True)  24.2 us
    ppermute x16, starting transfers between devices, swap(): return lax.ppermute(value, axis, [(i, i ^ bit) for i in range(size)])  24.2 us
    pallas_call x1, Pallas kernels, attend_back(): pl.pallas_call(attend_back_kernel, grid=(length // BLOCK,), in_specs=[by_...  14.9 us
    pallas_call x1, Pallas kernels, attend(): pl.pallas_call(attend_kernel, grid=(length // BLOCK,), in_specs=[by_row(H...  11.2 us
    unnamed x61, local copies, waits for them, and re-layouts  9.27 us
    pallas_call x1, Pallas kernels, project(): pl.pallas_call(project_kernel, grid=(length // BLOCK,), in_specs=[by_row(...  9.11 us
  transfers between devices with their start and end apart: 23, of which 19 were waited for; matrix products, arithmetic and copies ran while one was open for 28% of the time, Pallas kernels for 12%

profile of v1, /device:TPU:0, one launch (start us, length us, event | category | flops | bytes accessed | tf_op | source)
XLA Modules:
  0.0 297.0 jit_solution(9558101267854198611)
XLA Ops:
  9.9 4.1 %collective-permute-start = (bf16[64,768]{1,0:T(8,128)(2,1)S(1)}, bf16[64,768]{1,0:T(8,128)(2,1)S(1)}, u32[]{:S(2)}, u32[]{:S(2)}) collective-permute-start(bf16[64,768]{1,0:T(8,128)(2,1)S(1)} %get-tuple-element.58), channel_id=1, source_target_pairs={{0,16},{4,20},{8,24},{12,28},{16,0},{20,4},{24,8},{28,12},{1,17},{... | collective-permute-start | bytes 294920 | tf_op jit(solution)/shard_map/ppermute | solution.py:250
  14.0 4.9 %collective-permute-done = bf16[64,768]{1,0:T(8,128)(2,1)S(1)} collective-permute-done((bf16[64,768]{1,0:T(8,128)(2,1)S(1)}, bf16[64,768]{1,0:T(8,128)(2,1)S(1)}, u32[]{:S(2)}, u32[]{:S(2)}) %collective-permute-start) | collective-permute-done | bytes 98336 | tf_op jit(solution)/shard_map/ppermute | solution.py:250
  19.7 5.6 %collective-permute-done.1 = bf16[2,64,768]{2,1,0:T(8,128)(2,1)S(1)} collective-permute-done((bf16[2,64,768]{2,1,0:T(8,128)(2,1)S(1)}, bf16[2,64,768]{2,1,0:T(8,128)(2,1)S(1)}, u32[]{:S(2)}, u32[]{:S(2)}) %collective-permute-start.1) | collective-permute-done | bytes 196640 | tf_op jit(solution)/shard_map/ppermute | solution.py:250
  28.2 3.0 %collective-permute-done.4 = bf16[2,2,32,768]{3,2,1,0:T(8,128)(2,1)S(1)} collective-permute-done((bf16[2,2,32,768]{3,2,1,0:T(8,128)(2,1)S(1)}, bf16[2,2,32,768]{3,2,1,0:T(8,128)(2,1)S(1)}, u32[]{:S(2)}, u32[]{:S(2)}) %collective-permute-start.4) | collective-permute-done | bytes 196640 | tf_op jit(solution)/shard_map/ppermute | solution.py:250
  34.6 6.4 %collective-permute-done.5 = bf16[2,2,2,32,768]{4,3,2,1,0:T(8,128)(2,1)S(1)} collective-permute-done((bf16[2,2,2,32,768]{4,3,2,1,0:T(8,128)(2,1)S(1)}, bf16[2,2,2,32,768]{4,3,2,1,0:T(8,128)(2,1)S(1)}, u32[]{:S(2)}, u32[]{:S(2)}) %collective-permute-start.5) | collective-permute-done | bytes 393248 | tf_op jit(solution)/shard_map/ppermute | solution.py:250
  44.9 10.2 %all-to-all-start = ((bf16[32,32,192]{2,1,0:T(8,128)(2,1)}), bf16[32,32,192]{2,1,0:T(8,128)(2,1)S(1)}, u32[]{:S(2)}, u32[]{:S(2)}) async-start(bf16[32,32,192]{2,1,0:T(8,128)(2,1)} %bitcast.26), calls=%async_computation | async-start | bytes 1048576 | tf_op jit(solution)/shard_map/all_to_all | solution.py:308
  55.2 3.7 %multiply_sine_fusion = (f32[2048,32]{1,0:T(8,128)S(1)}, f32[2048,32]{1,0:T(8,128)S(1)}) fusion(f32[32]{0:T(128)S(1)} %multiply_power_fusion, f32[2048]{0:T(1024)S(1)} %iota_convert_fusion), kind=kLoop, calls=%fused_computation.23 | loop fusion | flops 65536 | bytes 532608 | tf_op jit(solution)/shard_map/sin | solution.py:38
  60.3 3.0 %pad_maximum_fusion.2 = (f32[2048,128]{1,0:T(8,128)}, f32[2048,128]{1,0:T(8,128)}) fusion(f32[2048,32]{1,0:T(8,128)S(1)} %get-tuple-element.60, f32[2048,32]{1,0:T(8,128)S(1)} %get-tuple-element.59), kind=kLoop, calls=%fused_computation.38 | loop fusion | flops 1572864 | bytes 2621440 | tf_op jit(solution)/shard_map/concatenate | solution.py:480
  63.4 16.0 %all-to-all-done = bf16[32,32,192]{2,1,0:T(8,128)(2,1)S(1)} async-done(((bf16[32,32,192]{2,1,0:T(8,128)(2,1)}), bf16[32,32,192]{2,1,0:T(8,128)(2,1)S(1)}, u32[]{:S(2)}, u32[]{:S(2)}) %all-to-all-start) | async-done | bytes 393248 | tf_op jit(solution)/shard_map/all_to_all | solution.py:308
  81.0 3.6 %maximum_select_fusion = bf16[2,2,2,2,2,2,32,768]{7,6,5,4,3,2,1,0:T(8,128)(2,1)} fusion(bf16[2,2,2,2,1,2,32,768]{7,6,5,4,3,2,1,0:T(8,128)(2,1)} %bitcast.23, bf16[2,2,2,2,1,2,32,768]{7,6,5,4,3,2,1,0:T(8,128)(2,1)S(1)} %get-tuple-element.44, pred[]{:T(512)S(6)} %eq.32), kind=kLoop, calls=%fused_computation.7 | loop fusion | flops 4718592 | bytes 6291457 | tf_op jit(solution)/shard_map/jit(_where)/select_n | solution.py:260
  84.6 9.1 %project.1 = (bf16[2048,768]{1,0:T(8,128)(2,1)}, bf16[2048,64]{1,0:T(8,128)(2,1)}, bf16[2048,64]{1,0:T(8,128)(2,1)}, bf16[2048,64]{1,0:T(8,128)(2,1)}) custom-call(bf16[2048,768]{1,0:T(8,128)(2,1)} %bitcast.145, f32[1,768]{1,0:T(1,128)} %reshape.663.gain, bf16[768,192]{1,0:T(8,128)(2,1)} %bitcast.162, f32[2048,128]{1,0:T(8,128)} %get-tuple-element.66.cosine, ...), custom_call_target="tpu_custom_call" | custom-call | tf_op jit(solution)/shard_map/project/pallas_call | solution.py:349
  93.7 11.2 %attend.1 = (bf16[2048,2048]{1,0:T(8,128)(2,1)}, f32[2048,64]{1,0:T(8,128)}, f32[2048,1]{1,0:T(8,128)}) custom-call(bf16[2048,64]{1,0:T(8,128)(2,1)} %get-tuple-element.18.queries, bf16[2048,64]{1,0:T(8,128)(2,1)} %get-tuple-element.19.key_rows, bf16[2048,64]{1,0:T(8,128)(2,1)} %get-tuple-element.20.value_rows), custom_call_target="tpu_custom_call" | custom-call | tf_op jit(solution)/shard_map/attend/pallas_call | solution.py:384
  107.3 3.8 %all-to-all-start.1 = ((bf16[32,2,2048]{2,1,0:T(2,128)(2,1)}), bf16[32,2,2048]{2,1,0:T(2,128)(2,1)S(1)}, u32[]{:S(2)}, u32[]{:S(2)}) async-start(bf16[32,2,2048]{2,1,0:T(2,128)(2,1)} %reshape.690), calls=%async_computation.1 | async-start | bytes 524288 | tf_op jit(solution)/shard_map/all_to_all | solution.py:308
  112.0 9.7 %all-to-all-done.1 = bf16[32,2,2048]{2,1,0:T(2,128)(2,1)S(1)} async-done(((bf16[32,2,2048]{2,1,0:T(2,128)(2,1)}), bf16[32,2,2048]{2,1,0:T(2,128)(2,1)S(1)}, u32[]{:S(2)}, u32[]{:S(2)}) %all-to-all-start.1) | async-done | bytes 262176 | tf_op jit(solution)/shard_map/all_to_all | solution.py:308
  122.8 1.9 fusion.66
  124.9 3.1 %fusion.3 = f32[128,2304]{1,0:T(8,128)S(1)} fusion(bf16[768,4224]{1,0:T(8,128)(2,1)} %all-gather.3.cloned.1.call-done, f32[128,768]{1,0:T(8,128)S(1)} %get-tuple-element.62, f32[768]{0:T(1024)S(1)} %reshape.664, f32[128]{0:T(128)S(1)} %add_rsqrt_fusion.1, f32[128]{0:T(128)S(1)} %broadcast_multiply_fusion.5), kind=kOutput, calls=%fused_computation.10 | convolution fusion | flops 453378048 | bytes 5115904 | tf_op jit(solution)/shard_map/dot_general | solution.py:493
  134.0 3.3 %all-to-all-start.2 = ((bf16[32,2,2048]{2,1,0:T(2,128)(2,1)}), bf16[32,2,2048]{2,1,0:T(2,128)(2,1)}, u32[]{:S(2)}, u32[]{:S(2)}) async-start(bf16[32,2,2048]{2,1,0:T(2,128)(2,1)} %reshape.692), calls=%async_computation.2 | async-start | bytes 524288 | tf_op jit(solution)/shard_map/all_to_all | solution.py:308
  138.5 2.3 convolution_convert_fusion
  142.1 1.9 copy.85
  144.1 5.0 %all-to-all-done.2 = bf16[32,2,2048]{2,1,0:T(2,128)(2,1)} async-done(((bf16[32,2,2048]{2,1,0:T(2,128)(2,1)}), bf16[32,2,2048]{2,1,0:T(2,128)(2,1)}, u32[]{:S(2)}, u32[]{:S(2)}) %all-to-all-start.2) | async-done | bytes 262176 | tf_op jit(solution)/shard_map/all_to_all | solution.py:308
  149.1 2.1 reshape.693
  151.2 14.9 %attend_back.1 = (f32[2048,64]{1,0:T(8,128)}, f32[2048,64]{1,0:T(8,128)}, f32[2048,64]{1,0:T(8,128)}) custom-call(bf16[2048,64]{1,0:T(8,128)(2,1)} %bitcast.155, f32[2048,64]{1,0:T(8,128)} %get-tuple-element.21.attn32, f32[2048,1]{1,0:T(8,128)} %get-tuple-element.22.total, bf16[2048,2048]{1,0:T(8,128)(2,1)} %get-tuple-element.23.weights, ...), custom_call_target="tpu_custom_call" | custom-call | tf_op jit(solution)/shard_map/attend_back/pallas_call | solution.py:430
  166.1 2.0 slice_negate_fusion.1
  172.5 2.1 convolution_convert_fusion.3
  174.5 1.9 copy.66
  176.4 3.3 %all-to-all-start.4 = ((bf16[32,24,192]{2,1,0:T(8,128)(2,1)}), bf16[32,24,192]{2,1,0:T(8,128)(2,1)}, u32[]{:S(2)}, u32[]{:S(2)}) async-start(bf16[32,24,192]{2,1,0:T(8,128)(2,1)} %bitcast.165), calls=%async_computation.4 | async-start | bytes 786432 | tf_op jit(solution)/shard_map/all_to_all | solution.py:308
  179.8 2.8 pad_maximum_fusion.6
  182.7 10.2 %all-to-all-done.4 = bf16[32,24,192]{2,1,0:T(8,128)(2,1)} async-done(((bf16[32,24,192]{2,1,0:T(8,128)(2,1)}), bf16[32,24,192]{2,1,0:T(8,128)(2,1)}, u32[]{:S(2)}, u32[]{:S(2)}) %all-to-all-start.4) | async-done | bytes 294944 | tf_op jit(solution)/shard_map/all_to_all | solution.py:308
  192.9 3.6 %all-to-all-start.3 = ((bf16[32,64,192]{2,1,0:T(8,128)(2,1)}), bf16[32,64,192]{2,1,0:T(8,128)(2,1)}, u32[]{:S(2)}, u32[]{:S(2)}) async-start(bf16[32,64,192]{2,1,0:T(8,128)(2,1)} %pad_maximum_fusion.6), calls=%async_computation.3 | async-start | bytes 2097152 | tf_op jit(solution)/shard_map/all_to_all | solution.py:308
  200.2 2.9 fusion.17
  203.1 1.8 convert_reduce_fusion
  204.9 2.0 reshape.660
  206.9 2.2 copy.67
  209.1 1.9 reshape.661
  213.2 9.3 %all-to-all-done.3 = bf16[32,64,192]{2,1,0:T(8,128)(2,1)} async-done(((bf16[32,64,192]{2,1,0:T(8,128)(2,1)}), bf16[32,64,192]{2,1,0:T(8,128)(2,1)}, u32[]{:S(2)}, u32[]{:S(2)}) %all-to-all-start.3) | async-done | bytes 786464 | tf_op jit(solution)/shard_map/all_to_all | solution.py:308
  222.5 2.5 copy.64
  226.4 2.3 copy.65
  228.7 3.3 %reshape.656 = bf16[128,2304]{0,1:T(8,128)(2,1)} reshape(bf16[2,64,3,12,64]{1,0,4,3,2:T(2,128)(2,1)} %copy.65) | data formatting | bytes 1179648 | tf_op jit(solution)/shard_map/reshape | solution.py:543
  231.9 3.6 %fusion.63 = (f32[128]{0:T(128)S(1)}, f32[128]{0:T(128)S(1)}, f32[128,768]{1,0:T(8,128)S(1)}) fusion(f32[128]{0:T(128)S(1)} %copy-done.23, f32[128]{0:T(128)S(1)} %copy-done.22, bf16[2,64,768]{2,1,0:T(8,128)(2,1)S(1)} %copy-done.7, f32[768]{0:T(1024)S(1)} %reshape.665, bf16[128,2304]{0,1:T(8,128)(2,1)} %reshape.656, ...), kind=kOutput, calls=%fused_computation.165 | convolution fusion | flops 453672704 | bytes 4723712 | tf_op jit(solution)/shard_map/tf,cf->tc/dot_general | solution.py:544
  235.5 2.7 fusion
  242.6 14.7 %collective-permute-done.8 = bf16[2,2,2,24,2048]{4,3,0,1,2:T(8,128)(2,1)S(1)} collective-permute-done((bf16[2,2,2,24,2048]{4,3,0,1,2:T(8,128)(2,1)S(1)}, bf16[2,2,2,24,2048]{4,3,0,1,2:T(8,128)(2,1)S(1)}, u32[]{:S(2)}, u32[]{:S(2)}) %collective-permute-start.8) | collective-permute-done | bytes 786464 | tf_op jit(solution)/shard_map/ppermute | solution.py:250
  257.7 2.0 collective-permute-start.9
  261.1 7.2 %collective-permute-done.9 = bf16[2,2,24,2048]{3,2,0,1:T(8,128)(2,1)S(1)} collective-permute-done((bf16[2,2,24,2048]{3,2,0,1:T(8,128)(2,1)S(1)}, bf16[2,2,24,2048]{3,2,0,1:T(8,128)(2,1)S(1)}, u32[]{:S(2)}, u32[]{:S(2)}) %collective-permute-start.9) | collective-permute-done | bytes 393248 | tf_op jit(solution)/shard_map/ppermute | solution.py:250
  270.4 2.1 collective-permute-start.14
  272.5 4.9 %collective-permute-done.10 = bf16[2,24,2048]{2,1,0:T(8,128)(2,1)S(1)} collective-permute-done((bf16[2,24,2048]{2,1,0:T(8,128)(2,1)S(1)}, bf16[2,24,2048]{2,1,0:T(8,128)(2,1)S(1)}, u32[]{:S(2)}, u32[]{:S(2)}) %collective-permute-start.10) | collective-permute-done | bytes 196640 | tf_op jit(solution)/shard_map/ppermute | solution.py:250
  279.7 3.1 %collective-permute-start.15 = (bf16[24,2176]{1,0:T(8,128)(2,1)S(1)}, bf16[24,2176]{1,0:T(8,128)(2,1)S(1)}, u32[]{:S(2)}, u32[]{:S(2)}) collective-permute-start(bf16[24,2176]{1,0:T(8,128)(2,1)S(1)} %dynamic-slice_bitcast_fusion.6), channel_id=1, source_target_pairs={{0,16},{4,20},{8,24},{12,28},{16,0},{20,4},{24,8},{28,12},{1,17},{... | collective-permute-start | bytes 313352 | tf_op jit(solution)/shard_map/ppermute | solution.py:250
  282.9 2.4 collective-permute-done.11
  285.3 2.2 collective-permute-done.15
  (172 shorter events, 54.4 us)
Async XLA Ops:
  7.2 115.6 %all-gather.3.cloned.1.call-start = ((), (), s32[]{:S(2)}) async-start(), calls=%async_computation.5 | async-start | bytes 6690816 | tf_op jit(solution)/shard_map/all_gather | solution.py:464
  9.9 9.0 %collective-permute-start = (bf16[64,768]{1,0:T(8,128)(2,1)S(1)}, bf16[64,768]{1,0:T(8,128)(2,1)S(1)}, u32[]{:S(2)}, u32[]{:S(2)}) collective-permute-start(bf16[64,768]{1,0:T(8,128)(2,1)S(1)} %get-tuple-element.58), channel_id=1, source_target_pairs={{0,16},{4,20},{8,24},{12,28},{16,0},{20,4},{24,8},{28,12},{1,17},{... | collective-permute-start | bytes 294920 | tf_op jit(solution)/shard_map/ppermute | solution.py:250
  18.9 6.4 %collective-permute-start.1 = (bf16[2,64,768]{2,1,0:T(8,128)(2,1)S(1)}, bf16[2,64,768]{2,1,0:T(8,128)(2,1)S(1)}, u32[]{:S(2)}, u32[]{:S(2)}) collective-permute-start(bf16[2,64,768]{2,1,0:T(8,128)(2,1)S(1)} %maximum_select_fusion.9), channel_id=1, source_target_pairs={{0,8},{4,12},{8,0},{12,4},{16,24},{20,28},{24,16},{28,20},{1,9},{5... | collective-permute-start | bytes 589832 | tf_op jit(solution)/shard_map/ppermute | solution.py:250
  25.5 5.7 %collective-permute-start.4 = (bf16[2,2,32,768]{3,2,1,0:T(8,128)(2,1)S(1)}, bf16[2,2,32,768]{3,2,1,0:T(8,128)(2,1)S(1)}, u32[]{:S(2)}, u32[]{:S(2)}) collective-permute-start(bf16[2,2,32,768]{3,2,1,0:T(8,128)(2,1)S(1)} %get-tuple-element.54), channel_id=1, source_target_pairs={{0,2},{1,3},{2,0},{3,1},{4,6},{5,7},{6,4},{7,5},{8,10},{9,11},{10,... | collective-permute-start | bytes 589832 | tf_op jit(solution)/shard_map/ppermute | solution.py:250
  26.9 6.5 %collective-permute-start.2 = (bf16[2,2,32,768]{3,2,1,0:T(8,128)(2,1)S(1)}, bf16[2,2,32,768]{3,2,1,0:T(8,128)(2,1)S(1)}, u32[]{:S(2)}, u32[]{:S(2)}) collective-permute-start(bf16[2,2,32,768]{3,2,1,0:T(8,128)(2,1)S(1)} %get-tuple-element.51), channel_id=1, source_target_pairs={{0,4},{4,0},{8,12},{12,8},{16,20},{20,16},{24,28},{28,24},{1,5},{5... | collective-permute-start | bytes 589832 | tf_op jit(solution)/shard_map/ppermute | solution.py:250
  31.3 9.7 %collective-permute-start.5 = (bf16[2,2,2,32,768]{4,3,2,1,0:T(8,128)(2,1)S(1)}, bf16[2,2,2,32,768]{4,3,2,1,0:T(8,128)(2,1)S(1)}, u32[]{:S(2)}, u32[]{:S(2)}) collective-permute-start(bf16[2,2,2,32,768]{4,3,2,1,0:T(8,128)(2,1)S(1)} %maximum_select_fusion.7), channel_id=1, source_target_pairs={{0,4},{4,0},{8,12},{12,8},{16,20},{20,16},{24,28},{28,24},{1,5},{5... | collective-permute-start | bytes 1179656 | tf_op jit(solution)/shard_map/ppermute | solution.py:250
  33.4 8.3 %collective-permute-start.3 = (bf16[2,2,2,32,768]{4,3,2,1,0:T(8,128)(2,1)S(1)}, bf16[2,2,2,32,768]{4,3,2,1,0:T(8,128)(2,1)S(1)}, u32[]{:S(2)}, u32[]{:S(2)}) collective-permute-start(bf16[2,2,2,32,768]{4,3,2,1,0:T(8,128)(2,1)S(1)} %maximum_select_fusion.5), channel_id=1, source_target_pairs={{0,2},{1,3},{2,0},{3,1},{4,6},{5,7},{6,4},{7,5},{8,10},{9,11},{10,... | collective-permute-start | bytes 1179656 | tf_op jit(solution)/shard_map/ppermute | solution.py:250
  41.0 2.4 copy-start.17
  41.0 2.9 copy-start.24
  41.1 2.9 copy-start.25
  43.4 37.6 %collective-permute-start.6 = (bf16[2,2,2,2,2,32,768]{6,5,4,3,2,1,0:T(8,128)(2,1)}, bf16[2,2,2,2,2,32,768]{6,5,4,3,2,1,0:T(8,128)(2,1)}, u32[]{:S(2)}, u32[]{:S(2)}) collective-permute-start(bf16[2,2,2,2,2,32,768]{6,5,4,3,2,1,0:T(8,128)(2,1)} %get-tuple-element.45), channel_id=1, source_target_pairs={{0,1},{1,0},{2,3},{3,2},{4,5},{5,4},{6,7},{7,6},{8,9},{9,8},{10,11... | collective-permute-start | bytes 4718600 | tf_op jit(solution)/shard_map/ppermute | solution.py:250
  44.9 34.5 %all-to-all-start = ((bf16[32,32,192]{2,1,0:T(8,128)(2,1)}), bf16[32,32,192]{2,1,0:T(8,128)(2,1)S(1)}, u32[]{:S(2)}, u32[]{:S(2)}) async-start(bf16[32,32,192]{2,1,0:T(8,128)(2,1)} %bitcast.26), calls=%async_computation | async-start | bytes 1048576 | tf_op jit(solution)/shard_map/all_to_all | solution.py:308
  58.9 1.0 copy-start.1
  58.9 1.4 copy-start.3
  79.4 5.2 %copy-start.14 = (bf16[32,32,192]{2,1,0:T(8,128)(2,1)}, bf16[32,32,192]{2,1,0:T(8,128)(2,1)S(1)}, u32[]{:S(2)}) copy-start(bf16[32,32,192]{2,1,0:T(8,128)(2,1)S(1)} %all-to-all-done) | copy-start | bytes 1179652
  104.9 17.8 %copy-start.7 = (bf16[2,64,768]{2,1,0:T(8,128)(2,1)S(1)}, bf16[2,64,768]{2,1,0:T(8,128)(2,1)}, u32[]{:S(2)}) copy-start(bf16[2,64,768]{2,1,0:T(8,128)(2,1)} %param.8) | copy-start | bytes 589828
  107.3 14.4 %all-to-all-start.1 = ((bf16[32,2,2048]{2,1,0:T(2,128)(2,1)}), bf16[32,2,2048]{2,1,0:T(2,128)(2,1)S(1)}, u32[]{:S(2)}, u32[]{:S(2)}) async-start(bf16[32,2,2048]{2,1,0:T(2,128)(2,1)} %reshape.690), calls=%async_computation.1 | async-start | bytes 524288 | tf_op jit(solution)/shard_map/all_to_all | solution.py:308
  111.1 120.8 %all-gather.5.cloned.1.call-start = ((), (), s32[]{:S(2)}) async-start(), calls=%async_computation.6 | async-start | bytes 3649536 | tf_op jit(solution)/shard_map/all_gather | solution.py:529
  122.7 5.2 %copy-start.10 = (bf16[768,4224]{1,0:T(8,128)(2,1)S(1)}, bf16[768,4224]{1,0:T(8,128)(2,1)}, u32[]{:S(2)}) copy-start(bf16[768,4224]{1,0:T(8,128)(2,1)} %all-gather.3.cloned.1.call-done) | copy-start | bytes 19464196
  124.6 13.9 %copy-start = (f32[128,768]{1,0:T(8,128)}, f32[128,768]{1,0:T(8,128)S(1)}, u32[]{:S(2)}) copy-start(f32[128,768]{1,0:T(8,128)S(1)} %get-tuple-element.62) | copy-start | bytes 1179652
  124.7 3.3 %copy-start.19 = (bf16[2,64,768]{2,1,0:T(8,128)(2,1)S(1)}, bf16[2,64,768]{2,1,0:T(8,128)(2,1)}, u32[]{:S(2)}) copy-start(bf16[2,64,768]{2,1,0:T(8,128)(2,1)} %param.15) | copy-start | bytes 589828
  129.5 1.8 copy-start.20
  129.8 8.0 %copy-start.15 = (bf16[128,1152]{1,0:T(8,128)(2,1)}, bf16[128,1152]{1,0:T(8,128)(2,1)S(1)}, u32[]{:S(2)}) copy-start(bf16[128,1152]{1,0:T(8,128)(2,1)S(1)} %get-tuple-element.43) | copy-start | bytes 884740
  131.5 6.3 %copy-start.8 = (f32[128,768]{1,0:T(8,128)}, f32[128,768]{1,0:T(8,128)S(1)}, u32[]{:S(2)}) copy-start(f32[128,768]{1,0:T(8,128)S(1)} %multiply_add_fusion.1) | copy-start | bytes 1179652
  134.0 15.0 %all-to-all-start.2 = ((bf16[32,2,2048]{2,1,0:T(2,128)(2,1)}), bf16[32,2,2048]{2,1,0:T(2,128)(2,1)}, u32[]{:S(2)}, u32[]{:S(2)}) async-start(bf16[32,2,2048]{2,1,0:T(2,128)(2,1)} %reshape.692), calls=%async_computation.2 | async-start | bytes 524288 | tf_op jit(solution)/shard_map/all_to_all | solution.py:308
  144.1 91.5 %collective-permute-start.7 = (bf16[2,2,2,2,24,4224]{5,4,0,1,2,3:T(8,128)(2,1)}, bf16[2,2,2,2,24,4224]{5,4,0,1,2,3:T(8,128)(2,1)}, u32[]{:S(2)}, u32[]{:S(2)}) collective-permute-start(bf16[2,2,2,2,24,4224]{5,4,0,1,2,3:T(8,128)(2,1)} %bitcast.143), channel_id=1, source_target_pairs={{0,1},{1,0},{2,3},{3,2},{4,5},{5,4},{6,7},{7,6},{8,9},{9,8},{10,11... | collective-permute-start | bytes 9732104 | tf_op jit(solution)/shard_map/ppermute | solution.py:250
  166.1 2.0 copy-start.6
  168.1 1.2 copy-start.2
  168.1 1.5 copy-start.4
  168.1 1.9 copy-start.5
  170.0 1.2 copy-start.16
  170.0 2.5 copy-start.27
  176.4 16.5 %all-to-all-start.4 = ((bf16[32,24,192]{2,1,0:T(8,128)(2,1)}), bf16[32,24,192]{2,1,0:T(8,128)(2,1)}, u32[]{:S(2)}, u32[]{:S(2)}) async-start(bf16[32,24,192]{2,1,0:T(8,128)(2,1)} %bitcast.165), calls=%async_computation.4 | async-start | bytes 786432 | tf_op jit(solution)/shard_map/all_to_all | solution.py:308
  192.9 29.6 %all-to-all-start.3 = ((bf16[32,64,192]{2,1,0:T(8,128)(2,1)}), bf16[32,64,192]{2,1,0:T(8,128)(2,1)}, u32[]{:S(2)}, u32[]{:S(2)}) async-start(bf16[32,64,192]{2,1,0:T(8,128)(2,1)} %pad_maximum_fusion.6), calls=%async_computation.3 | async-start | bytes 2097152 | tf_op jit(solution)/shard_map/all_to_all | solution.py:308
  197.9 13.1 %copy-start.18 = (bf16[24,2304]{1,0:T(8,128)(2,1)S(1)}, bf16[24,2304]{1,0:T(8,128)(2,1)}, u32[]{:S(2)}) copy-start(bf16[24,2304]{1,0:T(8,128)(2,1)} %param.10) | copy-start | bytes 331780
  225.0 6.9 %copy-start.22 = (f32[128]{0:T(128)S(1)}, f32[128]{0:T(128)}, u32[]{:S(2)}) copy-start(f32[128]{0:T(128)} %div.111) | copy-start | bytes 1540
  225.0 6.9 %copy-start.23 = (f32[128]{0:T(128)S(1)}, f32[128]{0:T(128)}, u32[]{:S(2)}) copy-start(f32[128]{0:T(128)} %rsqrt.21) | copy-start | bytes 1540
  238.4 3.4 %copy-start.9 = (f32[128,768]{1,0:T(8,128)S(1)}, f32[128,768]{1,0:T(8,128)}, u32[]{:S(2)}) copy-start(f32[128,768]{1,0:T(8,128)} %copy-done.8) | copy-start | bytes 1179652
  238.5 18.9 %collective-permute-start.8 = (bf16[2,2,2,24,2048]{4,3,0,1,2:T(8,128)(2,1)S(1)}, bf16[2,2,2,24,2048]{4,3,0,1,2:T(8,128)(2,1)S(1)}, u32[]{:S(2)}, u32[]{:S(2)}) collective-permute-start(bf16[2,2,2,24,2048]{4,3,0,1,2:T(8,128)(2,1)S(1)} %dynamic-slice_bitcast_fusion.1), channel_id=1, source_target_pairs={{0,4},{4,0},{8,12},{12,8},{16,20},{20,16},{24,28},{28,24},{1,5},{5... | collective-permute-start | bytes 2359304 | tf_op jit(solution)/shard_map/ppermute | solution.py:250
  240.2 20.2 %collective-permute-start.12 = (bf16[2,2,2,24,2176]{4,3,0,1,2:T(8,128)(2,1)S(1)}, bf16[2,2,2,24,2176]{4,3,0,1,2:T(8,128)(2,1)S(1)}, u32[]{:S(2)}, u32[]{:S(2)}) collective-permute-start(bf16[2,2,2,24,2176]{4,3,0,1,2:T(8,128)(2,1)S(1)} %dynamic-slice_bitcast_fusion), channel_id=1, source_target_pairs={{0,2},{1,3},{2,0},{3,1},{4,6},{5,7},{6,4},{7,5},{8,10},{9,11},{10,... | collective-permute-start | bytes 2506760 | tf_op jit(solution)/shard_map/ppermute | solution.py:250
  257.7 10.7 %collective-permute-start.9 = (bf16[2,2,24,2048]{3,2,0,1:T(8,128)(2,1)S(1)}, bf16[2,2,24,2048]{3,2,0,1:T(8,128)(2,1)S(1)}, u32[]{:S(2)}, u32[]{:S(2)}) collective-permute-start(bf16[2,2,24,2048]{3,2,0,1:T(8,128)(2,1)S(1)} %dynamic-slice_bitcast_fusion.3), channel_id=1, source_target_pairs={{0,2},{1,3},{2,0},{3,1},{4,6},{5,7},{6,4},{7,5},{8,10},{9,11},{10,... | collective-permute-start | bytes 1179656 | tf_op jit(solution)/shard_map/ppermute | solution.py:250
  260.6 28.2 %copy-start.21 = (bf16[24,2304]{1,0:T(8,128)(2,1)S(1)}, bf16[24,2304]{1,0:T(8,128)(2,1)}, u32[]{:S(2)}) copy-start(bf16[24,2304]{1,0:T(8,128)(2,1)} %param.13) | copy-start | bytes 331780
  260.7 9.6 %collective-permute-start.13 = (bf16[2,2,24,2176]{3,2,0,1:T(8,128)(2,1)S(1)}, bf16[2,2,24,2176]{3,2,0,1:T(8,128)(2,1)S(1)}, u32[]{:S(2)}, u32[]{:S(2)}) collective-permute-start(bf16[2,2,24,2176]{3,2,0,1:T(8,128)(2,1)S(1)} %dynamic-slice_bitcast_fusion.2), channel_id=1, source_target_pairs={{0,4},{4,0},{8,12},{12,8},{16,20},{20,16},{24,28},{28,24},{1,5},{5... | collective-permute-start | bytes 1253384 | tf_op jit(solution)/shard_map/ppermute | solution.py:250
  268.5 21.2 %copy-start.26 = (bf16[24]{0:T(256)(128)(2,1)S(1)}, bf16[24]{0:T(256)(128)(2,1)}, u32[]{:S(2)}) copy-start(bf16[24]{0:T(256)(128)(2,1)} %param.12) | copy-start | bytes 148
  268.5 8.9 %collective-permute-start.10 = (bf16[2,24,2048]{2,1,0:T(8,128)(2,1)S(1)}, bf16[2,24,2048]{2,1,0:T(8,128)(2,1)S(1)}, u32[]{:S(2)}, u32[]{:S(2)}) collective-permute-start(bf16[2,24,2048]{2,1,0:T(8,128)(2,1)S(1)} %dynamic-slice_bitcast_fusion.5), channel_id=1, source_target_pairs={{0,8},{4,12},{8,0},{12,4},{16,24},{20,28},{24,16},{28,20},{1,9},{5... | collective-permute-start | bytes 589832 | tf_op jit(solution)/shard_map/ppermute | solution.py:250
  270.4 9.3 %collective-permute-start.14 = (bf16[2,24,2176]{2,1,0:T(8,128)(2,1)S(1)}, bf16[2,24,2176]{2,1,0:T(8,128)(2,1)S(1)}, u32[]{:S(2)}, u32[]{:S(2)}) collective-permute-start(bf16[2,24,2176]{2,1,0:T(8,128)(2,1)S(1)} %dynamic-slice_bitcast_fusion.4), channel_id=1, source_target_pairs={{0,8},{4,12},{8,0},{12,4},{16,24},{20,28},{24,16},{28,20},{1,9},{5... | collective-permute-start | bytes 626696 | tf_op jit(solution)/shard_map/ppermute | solution.py:250
  277.5 7.8 %collective-permute-start.11 = (bf16[24,2048]{1,0:T(8,128)(2,1)S(1)}, bf16[24,2048]{1,0:T(8,128)(2,1)S(1)}, u32[]{:S(2)}, u32[]{:S(2)}) collective-permute-start(bf16[24,2048]{1,0:T(8,128)(2,1)S(1)} %dynamic-slice_bitcast_fusion.7), channel_id=1, source_target_pairs={{0,16},{4,20},{8,24},{12,28},{16,0},{20,4},{24,8},{28,12},{1,17},{... | collective-permute-start | bytes 294920 | tf_op jit(solution)/shard_map/ppermute | solution.py:250
  279.7 7.8 %collective-permute-start.15 = (bf16[24,2176]{1,0:T(8,128)(2,1)S(1)}, bf16[24,2176]{1,0:T(8,128)(2,1)S(1)}, u32[]{:S(2)}, u32[]{:S(2)}) collective-permute-start(bf16[24,2176]{1,0:T(8,128)(2,1)S(1)} %dynamic-slice_bitcast_fusion.6), channel_id=1, source_target_pairs={{0,16},{4,20},{8,24},{12,28},{16,0},{20,4},{24,8},{28,12},{1,17},{... | collective-permute-start | bytes 313352 | tf_op jit(solution)/shard_map/ppermute | solution.py:250
  (3 other events, 2.8 us)
Sparse Core Ops, SparseCore 0:
  11.4 78.0 all-gather.2
  114.9 62.3 all-gather.4

commit v2 on v0

--- a/solution.py
+++ b/solution.py
@@ -1,6 +1,10 @@
+import functools
+
 import jax
 import jax.numpy as jnp
 from jax import lax
+from jax.experimental import pallas as pl
+from jax.experimental.pallas import tpu as pltpu
 from jax.sharding import PartitionSpec as P
 
 HEAD = 64
@@ -69,7 +73,7 @@
     return (value_term, grad_scores)
 
 
-def body(
+def ring_body(
     tokens, attn_gain, qkv_weight, attn_out_weight, mlp_gain, in_weight, out_weight, cotangent
 ):
     sequences, per_device, model_width = tokens.shape
@@ -235,6 +239,585 @@
     )
 
 
+AXES = ("blk", "ulysses")
+BF = jnp.bfloat16
+F32 = jnp.float32
+HEADS = 12
+SHARE = 3
+BLOCK = 256
+LANES = 128
+TILE = 384
+BY_COLUMN = (((1,), (1,)), ((), ()))
+BY_ROW = (((0,), (0,)), ((), ()))
+
+
+def swap(value, axis, bit):
+    size = lax.axis_size(axis)
+    return lax.ppermute(value, axis, [(i, i ^ bit) for i in range(size)])
+
+
+def my_bit(axis, bit):
+    return (lax.axis_index(axis) // bit) % 2
+
+
+def join(mine, other, side, axis):
+    first = jnp.stack([mine, other], axis=axis)
+    second = jnp.stack([other, mine], axis=axis)
+    return jnp.where(side == 0, first, second)
+
+
+def gather_sequence(tokens, also):
+    sequences, rows, width = tokens.shape
+    z2, z1, x = my_bit("blk", 4), my_bit("blk", 2), my_bit("blk", 1)
+    y = my_bit("ulysses", 2)
+    keep = lax.dynamic_index_in_dim(tokens, z2, 0, keepdims=False)
+    give = lax.dynamic_index_in_dim(tokens, 1 - z2, 0, keepdims=False)
+    wide = join(keep, swap(give, "blk", 4), z2, 0)
+    wide = join(wide, swap(wide, "blk", 2), z1, 1)
+    wide = wide.reshape(2, 2, 2, rows // 2, width)
+    part_a, part_b = wide[:, :, 0], wide[:, :, 1]
+    from_a, from_b = swap(part_a, "blk", 1), swap(part_b, "ulysses", 2)
+    part_a = join(part_a, from_a, x, 2)
+    part_b = join(part_b, from_b, y, 2)
+    from_a, from_b = swap(part_a, "ulysses", 2), swap(part_b, "blk", 1)
+    part_a = join(part_a, from_a, y, 3)
+    part_b = join(part_b, from_b, x, 2)
+    wide = jnp.stack([part_a, part_b], axis=4).reshape(16 * rows, width)
+    wide, also = lax.optimization_barrier((wide, also))
+    return wide, swap(wide, "ulysses", 1), also
+
+
+def halve(keep, got, axis, bit, dim):
+    total = (keep.astype(F32) + got.astype(F32)).astype(BF)
+    side = my_bit(axis, bit)
+    keep = lax.dynamic_index_in_dim(total, side, dim, keepdims=False)
+    give = lax.dynamic_index_in_dim(total, 1 - side, dim, keepdims=False)
+    return keep, give
+
+
+def exchange(value):
+    return lax.all_to_all(value, AXES, split_axis=0, concat_axis=0, tiled=True)
+
+
+def owner_slot(sequence, head):
+    return sequence * 16 + head // SHARE * (SHARE + 1) + head % SHARE
+
+
+def turn(values):
+    lane = lax.broadcasted_iota(jnp.int32, values.shape, 1) % HEAD
+    return jnp.where(
+        lane < HEAD // 2,
+        -pltpu.roll(values, LANES - HEAD // 2, 1),
+        pltpu.roll(values, HEAD // 2, 1),
+    )
+
+
+def side_by_side(left, right):
+    return jnp.concatenate([left, right], axis=1)
+
+
+def smem():
+    return pl.BlockSpec(memory_space=pltpu.SMEM)
+
+
+def project_kernel(
+    core, mine, other, gain, weight, cosine, sine, hidden, queries, key_rows, value_rows
+):
+    def one(tokens, slot):
+        normed, inverse = normalize(tokens[...].astype(F32))
+        low = (normed * gain[...]).astype(BF)
+        hidden[slot] = low
+        qkv = jnp.dot(low, weight[:, : 3 * HEAD], preferred_element_type=F32).astype(BF)
+        both = qkv[:, :LANES].astype(F32)
+        both = (both * cosine[slot] + turn(both) * sine[slot]).astype(BF)
+        queries[slot] = both[:, :HEAD] * BF(HEAD**-0.5)
+        key_rows[slot] = both[:, HEAD:]
+        value_rows[slot] = qkv[:, LANES:]
+
+    one(mine, core[0])
+    one(other, 1 - core[0])
+
+
+def project(core, mine, other, gain, weight, cosine, sine):
+    length, width = mine.shape
+    by_row = pl.BlockSpec((BLOCK, width), lambda i: (i, 0))
+    by_pair = lambda columns: pl.BlockSpec((2, BLOCK, columns), lambda i: (0, i, 0))
+    whole = lambda shape: pl.BlockSpec(shape, lambda i: (0, 0))
+    return pl.pallas_call(
+        project_kernel,
+        grid=(length // BLOCK,),
+        in_specs=[
+            smem(),
+            by_row,
+            by_row,
+            whole((1, width)),
+            whole(weight.shape),
+            by_pair(LANES),
+            by_pair(LANES),
+        ],
+        out_specs=[by_pair(width), by_pair(HEAD), by_pair(HEAD), by_pair(HEAD)],
+        out_shape=[jax.ShapeDtypeStruct((2, length, width), BF)]
+        + [jax.ShapeDtypeStruct((2, length, HEAD), BF)] * 3,
+        name="project",
+    )(core, mine, other, gain, weight, cosine, sine)
+
+
+def attend_kernel(queries, key_rows, value_rows, weights, attn32, total, send):
+    scores = lax.dot_general(
+        queries[...], key_rows[...], BY_COLUMN, preferred_element_type=F32
+    )
+    top = jnp.max(scores, axis=-1, keepdims=True)
+    expo = jnp.exp(scores - top)
+    row_total = jnp.sum(expo, axis=-1, keepdims=True)
+    low = expo.astype(BF)
+    weights[...] = low
+    mixed = jnp.dot(low, value_rows[...], preferred_element_type=F32) / row_total
+    attn32[...] = mixed
+    total[...] = row_total
+    mixed = mixed.astype(BF)
+    for i in range(BLOCK // 64):
+        rows = mixed[64 * i : 64 * i + 64]
+        send[i, 0] = side_by_side(rows[:32], rows[32:])
+
+
+def attend(queries, key_rows, value_rows):
+    length = queries.shape[0]
+    by_row = lambda columns: pl.BlockSpec((BLOCK, columns), lambda i: (i, 0))
+    whole = pl.BlockSpec((length, HEAD), lambda i: (0, 0))
+    steps = length // BLOCK
+    return pl.pallas_call(
+        attend_kernel,
+        grid=(steps,),
+        in_specs=[by_row(HEAD), whole, whole],
+        out_specs=[
+            by_row(length),
+            by_row(HEAD),
+            by_row(1),
+            pl.BlockSpec(
+                (BLOCK // 64, 1, 32, LANES), lambda i: (i % (steps // 2), i // (steps // 2), 0, 0)
+            ),
+        ],
+        out_shape=[
+            jax.ShapeDtypeStruct((length, length), BF),
+            jax.ShapeDtypeStruct((length, HEAD), F32),
+            jax.ShapeDtypeStruct((length, 1), F32),
+            jax.ShapeDtypeStruct((length // 128, 2, 32, LANES), BF),
+        ],
+        name="attend",
+    )(queries, key_rows, value_rows)
+
+
+def middle_kernel(
+    got, tokens, late, gain, grad_out, layer_output, send, attn, hidden, grad_joint, activation,
+    branch, grad_middle
+):
+    width = tokens.shape[1]
+    hidden_units = activation.shape[1]
+    cut = 2 * hidden_units
+    for s in range(2):
+        for h in range(0, HEADS, 2):
+            left, right = got[owner_slot(s, h)], got[owner_slot(s, h + 1)]
+            columns = slice(h * HEAD, h * HEAD + LANES)
+            attn[64 * s : 64 * s + 32, columns] = side_by_side(left[:, :HEAD], right[:, :HEAD])
+            attn[64 * s + 32 : 64 * s + 64, columns] = side_by_side(
+                left[:, HEAD:], right[:, HEAD:]
+            )
+    attn_weight = late[:, cut : cut + width]
+    middle = tokens[...].astype(F32) + jnp.dot(
+        attn[...], attn_weight, preferred_element_type=F32
+    )
+    normed, inverse = normalize(middle)
+    low = (normed * gain[...]).astype(BF)
+    hidden[...] = low
+    first = jnp.dot(low, late[:, :hidden_units], preferred_element_type=F32)
+    gate = jnp.dot(low, late[:, hidden_units:cut], preferred_element_type=F32)
+    cumulative = 0.5 * (1.0 + lax.erf(first * (0.5**0.5)))
+    bent = first * cumulative
+    active = (bent * gate).astype(BF)
+    activation[...] = active
+    out_weight = late[:, cut + width :]
+    layer_output[...] = (
+        middle + lax.dot_general(active, out_weight, BY_COLUMN, preferred_element_type=F32)
+    ).astype(BF)
+    grad_act = jnp.dot(grad_out[...], out_weight, preferred_element_type=F32)
+    density = jnp.exp(-0.5 * first * first) * 0.3989422804014327
+    grad_joint[:, :hidden_units] = (grad_act * gate * (cumulative + first * density)).astype(BF)
+    grad_joint[:, hidden_units:] = (grad_act * bent).astype(BF)
+    grad_hidden = lax.dot_general(
+        grad_joint[...], late[:, :cut], BY_COLUMN, preferred_element_type=F32
+    )
+    total = grad_out[...].astype(F32) + norm_back(grad_hidden * gain[...], normed, inverse)
+    grad_middle[...] = total
+    branch_low = total.astype(BF)
+    branch[...] = branch_low
+    grad_cat = lax.dot_general(
+        branch_low, attn_weight, BY_COLUMN, preferred_element_type=F32
+    ).astype(BF)
+    for s in range(2):
+        for h in range(HEADS):
+            rows = grad_cat[64 * s : 64 * s + 64, h * HEAD : (h + 1) * HEAD]
+            block = side_by_side(rows[:32], rows[32:])
+            send[owner_slot(s, h)] = block
+            if h % SHARE == SHARE - 1:
+                send[owner_slot(s, h) + 1] = block
+
+
+def middle_part(got, tokens, late, gain, grad_out):
+    rows, width = tokens.shape
+    hidden_units = (late.shape[1] - width) // 3
+    shapes = [
+        ((rows, width), BF),
+        (got.shape, BF),
+        ((rows, width), BF),
+        ((rows, width), BF),
+        ((rows, 2 * hidden_units), BF),
+        ((rows, hidden_units), BF),
+        ((rows, width), BF),
+        ((rows, width), F32),
+    ]
+    return pl.pallas_call(
+        middle_kernel,
+        out_shape=[jax.ShapeDtypeStruct(shape, kind) for shape, kind in shapes],
+        name="middle_part",
+    )(got, tokens, late, gain, grad_out)
+
+
+def weight_grads_kernel(
+    core, hidden, attn, grad_out, joint, branch, active, keep, give, *, in_tiles, attn_tiles
+):
+    tile = pl.program_id(0)
+
+    def write(left, right):
+        total = lax.dot_general(left[...], right[...], BY_ROW, preferred_element_type=F32)
+        total = total.reshape(keep.shape[0], 2, *keep.shape[1:])
+        first, second = total[:, 0], total[:, 1]
+        keep[...] = jnp.where(core[0] == 0, first, second).astype(BF)
+        give[...] = jnp.where(core[0] == 0, second, first).astype(BF)
+
+    @pl.when(tile < in_tiles)
+    def _():
+        write(hidden, joint)
+
+    @pl.when((tile >= in_tiles) & (tile < in_tiles + attn_tiles))
+    def _():
+        write(attn, branch)
+
+    @pl.when(tile >= in_tiles + attn_tiles)
+    def _():
+        write(grad_out, active)
+
+
+def weight_grads(core, hidden, attn, grad_out, joint, branch, active, rows_here):
+    rows, width = hidden.shape
+    in_tiles, attn_tiles = joint.shape[1] // TILE, width // TILE
+    out_tiles = active.shape[1] // TILE
+    tiles = in_tiles + attn_tiles + out_tiles
+    whole = pl.BlockSpec((rows, width), lambda t: (0, 0))
+    part = lambda first, count: pl.BlockSpec(
+        (rows, TILE), lambda t: (0, jnp.clip(t - first, 0, count - 1))
+    )
+    pairs = width // (2 * rows_here)
+    result = pl.BlockSpec((pairs, rows_here, TILE), lambda t: (0, 0, t))
+    return pl.pallas_call(
+        functools.partial(weight_grads_kernel, in_tiles=in_tiles, attn_tiles=attn_tiles),
+        grid=(tiles,),
+        in_specs=[
+            smem(),
+            whole,
+            whole,
+            whole,
+            part(0, in_tiles),
+            part(in_tiles, attn_tiles),
+            part(in_tiles + attn_tiles, out_tiles),
+        ],
+        out_specs=[result, result],
+        out_shape=[jax.ShapeDtypeStruct((pairs, rows_here, tiles * TILE), BF)] * 2,
+        name="weight_grads",
+    )(core, hidden, attn, grad_out, joint, branch, active)
+
+
+def attend_back_kernel(
+    got, attn32, total, weights, queries, key_rows, value_rows, cosine, sine, send, grad_both,
+    grad_low, grad_query, grad_key, grad_value
+):
+    step = pl.program_id(0)
+
+    @pl.when(step == 0)
+    def _():
+        grad_key[...] = jnp.zeros_like(grad_key)
+        grad_value[...] = jnp.zeros_like(grad_value)
+
+    pieces = []
+    for i in range(BLOCK // 64):
+        block = got[i, 0]
+        pieces += [block[:, :HEAD], block[:, HEAD:]]
+    grad = jnp.concatenate(pieces, axis=0)
+    wide = grad.astype(F32)
+    dots = jnp.sum(wide * attn32[...], axis=-1, keepdims=True)
+    grad_probs = lax.dot_general(
+        grad, value_rows[...], BY_COLUMN, preferred_element_type=F32
+    )
+    inverse = 1.0 / total[...]
+    low = weights[...]
+    grad_scores = ((low.astype(F32) * inverse) * (grad_probs - dots)).astype(BF)
+    grad_query[pl.ds(step * BLOCK, BLOCK), :] = HEAD**-0.5 * jnp.dot(
+        grad_scores, key_rows[...], preferred_element_type=F32
+    )
+    grad_value[...] += lax.dot_general(
+        low, (wide * inverse).astype(BF), BY_ROW, preferred_element_type=F32
+    )
+    grad_key[...] += lax.dot_general(
+        grad_scores, queries[...], BY_ROW, preferred_element_type=F32
+    )
+
+    @pl.when(step == pl.num_programs(0) - 1)
+    def _():
+        length = grad_key.shape[0]
+        both = side_by_side(grad_query[...], grad_key[...])
+        both = (both * cosine[...] - turn(both) * sine[...]).astype(BF)
+        grad_both[...] = both
+        low = grad_value[...].astype(BF)
+        grad_low[...] = low
+        for i in range(length // 64):
+            core, pair = i // (length // 128), i % (length // 128)
+            rows = low[64 * i : 64 * i + 64]
+            send[pair, core, :64] = both[64 * i : 64 * i + 64]
+            send[pair, core, 64:] = side_by_side(rows[:32], rows[32:])
+
+
+def attend_back(got, attn32, total, weights, queries, key_rows, value_rows, cosine, sine):
+    length = queries.shape[0]
+    steps = length // BLOCK
+    by_row = lambda columns: pl.BlockSpec((BLOCK, columns), lambda i: (i, 0))
+    whole = lambda *shape: pl.BlockSpec(shape, lambda i: (0,) * len(shape))
+    send = (length // 128, 2, 96, LANES)
+    return pl.pallas_call(
+        attend_back_kernel,
+        grid=(steps,),
+        in_specs=[
+            pl.BlockSpec(
+                (BLOCK // 64, 1, 32, LANES), lambda i: (i % (steps // 2), i // (steps // 2), 0, 0)
+            ),
+            by_row(HEAD),
+            by_row(1),
+            by_row(length),
+            by_row(HEAD),
+            whole(length, HEAD),
+            whole(length, HEAD),
+            whole(length, LANES),
+            whole(length, LANES),
+        ],
+        out_specs=[whole(*send), whole(length, LANES), whole(length, HEAD)],
+        out_shape=[
+            jax.ShapeDtypeStruct(send, BF),
+            jax.ShapeDtypeStruct((length, LANES), BF),
+            jax.ShapeDtypeStruct((length, HEAD), BF),
+        ],
+        scratch_shapes=[pltpu.VMEM((length, HEAD), F32)] * 3,
+        name="attend_back",
+    )(got, attn32, total, weights, queries, key_rows, value_rows, cosine, sine)
+
+
+def head_grads_kernel(hidden, both, low, result):
+    @pl.when(pl.program_id(0) == 0)
+    def _():
+        result[...] = jnp.zeros_like(result)
+
+    result[:, :LANES] += lax.dot_general(
+        hidden[...], both[...], BY_ROW, preferred_element_type=F32
+    )
+    result[:, LANES:] += lax.dot_general(
+        hidden[...], low[...], BY_ROW, preferred_element_type=F32
+    )
+
+
+def head_grads(hidden, both, low):
+    length, width = hidden.shape
+    by_row = lambda columns: pl.BlockSpec((2 * BLOCK, columns), lambda i: (i, 0))
+    return pl.pallas_call(
+        head_grads_kernel,
+        grid=(length // (2 * BLOCK),),
+        in_specs=[by_row(width), by_row(LANES), by_row(HEAD)],
+        out_specs=pl.BlockSpec((width, 3 * HEAD), lambda i: (0, 0)),
+        out_shape=jax.ShapeDtypeStruct((width, 3 * HEAD), F32),
+        name="head_grads",
+    )(hidden, both, low)
+
+
+def last_kernel(got, weight, tokens, gain, grad_middle, result, grads):
+    width = tokens.shape[1]
+    for s in range(2):
+        for h in range(0, HEADS, 2):
+            left, right = got[owner_slot(s, h)], got[owner_slot(s, h + 1)]
+            top, end = slice(64 * s, 64 * s + 64), slice(64 * s + 64, 64 * s + 128)
+            place = lambda j: slice(j * width + h * HEAD, j * width + h * HEAD + LANES)
+            grads[top, place(0)] = side_by_side(left[:64, :HEAD], right[:64, :HEAD])
+            grads[top, place(1)] = side_by_side(left[:64, HEAD:], right[:64, HEAD:])
+            grads[64 * s : 64 * s + 32, place(2)] = side_by_side(
+                left[64:, :HEAD], right[64:, :HEAD]
+            )
+            grads[64 * s + 32 : 64 * s + 64, place(2)] = side_by_side(
+                left[64:, HEAD:], right[64:, HEAD:]
+            )
+    grad_hidden = lax.dot_general(
+        grads[...], weight[...], BY_COLUMN, preferred_element_type=F32
+    )
+    normed, inverse = normalize(tokens[...].astype(F32))
+    result[...] = (
+        grad_middle[...] + norm_back(grad_hidden * gain[...], normed, inverse)
+    ).astype(BF)
+
+
+def last_part(got, weight, tokens, gain, grad_middle):
+    return pl.pallas_call(
+        last_kernel,
+        out_shape=jax.ShapeDtypeStruct(tokens.shape, BF),
+        scratch_shapes=[pltpu.VMEM((tokens.shape[0], weight.shape[1]), BF)],
+        name="last_part",
+    )(got, weight, tokens, gain, grad_middle)
+
+
+def collect_kernel(got, weight, gain, result, gain_grad):
+    width = result.shape[1] // 3
+    for h in range(0, HEADS, 2):
+        left = got[owner_slot(0, h)].astype(F32) + got[owner_slot(1, h)].astype(F32)
+        right = got[owner_slot(0, h + 1)].astype(F32) + got[owner_slot(1, h + 1)].astype(F32)
+        for j in range(3):
+            columns = slice(j * HEAD, (j + 1) * HEAD)
+            place = slice(j * width + h * HEAD, j * width + h * HEAD + LANES)
+            result[:, place] = side_by_side(left[:, columns], right[:, columns])
+    product = result[...] * weight[...].astype(F32)
+    gain_grad[...] = jnp.sum(product, axis=1, keepdims=True) / gain[...]
+
+
+def collect(got, weight, gain):
+    rows, columns = weight.shape
+    return pl.pallas_call(
+        collect_kernel,
+        out_shape=[
+            jax.ShapeDtypeStruct((rows, columns), F32),
+            jax.ShapeDtypeStruct((rows, 1), F32),
+        ],
+        name="collect",
+    )(got, weight, gain)
+
+
+def owner_body(
+    tokens, attn_gain, qkv_weight, attn_out_weight, mlp_gain, in_weight, out_weight, cotangent
+):
+    sequences, per_device, model_width = tokens.shape
+    hidden_units = out_weight.shape[0]
+    rows_here = qkv_weight.shape[0]
+    rows = sequences * per_device
+    length = per_device * 32
+    core = my_bit("ulysses", 1).astype(jnp.int32).reshape(1)
+    late = jnp.concatenate([in_weight, attn_out_weight, jnp.transpose(out_weight)], axis=1)
+    late_full = lax.all_gather(late, AXES, axis=0, tiled=True)
+    by_head = qkv_weight.reshape(rows_here, 3, HEADS, HEAD).transpose(2, 0, 1, 3)
+    by_head = by_head.reshape(HEADS, rows_here, 3 * HEAD)
+    gains = jnp.stack([attn_gain, mlp_gain], axis=1)
+    gains = jnp.broadcast_to(jnp.pad(gains, ((0, 0), (0, HEAD - 2))), (HEADS, rows_here, HEAD))
+    packed = jnp.concatenate([by_head, gains], axis=2)
+    packed = packed.reshape(HEADS // SHARE, SHARE, rows_here, 4 * HEAD)
+    packed = jnp.concatenate([packed, packed[:, -1:]], axis=1)
+    packed = jnp.broadcast_to(packed[None], (2,) + packed.shape)
+    mixed = exchange(packed.reshape(32, rows_here, 4 * HEAD))
+    mine, other, mixed = gather_sequence(tokens, mixed)
+    weight_here = mixed.reshape(model_width, 4 * HEAD)
+    gain_one = weight_here[:, 3 * HEAD].reshape(1, model_width).astype(F32)
+    gain_two = weight_here[:, 3 * HEAD + 1].reshape(1, model_width).astype(F32)
+    cosine, sine = rotation(0, length, HEAD)
+    by_core = lambda table: jnp.tile(
+        table.reshape(length // 128, 2, 64, HEAD).transpose(1, 0, 2, 3).reshape(length, HEAD),
+        (1, 2),
+    )
+    cosine, sine = by_core(cosine), by_core(sine)
+    hidden_one, queries, key_rows, value_rows = project(
+        core,
+        mine,
+        other,
+        gain_one,
+        weight_here,
+        cosine.reshape(2, length // 2, LANES),
+        sine.reshape(2, length // 2, LANES),
+    )
+    queries, key_rows, value_rows = (
+        value.reshape(length, HEAD) for value in (queries, key_rows, value_rows)
+    )
+    weights_low, attn32, row_total, send = attend(queries, key_rows, value_rows)
+    got = exchange(send.reshape(32, 32, LANES))
+    flat_tokens = tokens.reshape(rows, model_width)
+    grad_out = cotangent.reshape(rows, model_width)
+    layer_output, send, attn_cat, hidden_two, grad_joint, activation, branch, grad_middle = (
+        middle_part(got, flat_tokens, late_full, gain_two, grad_out)
+    )
+    got = exchange(send)
+    keep, give = weight_grads(
+        core, hidden_two, attn_cat, grad_out, grad_joint, branch, activation, rows_here
+    )
+    came = swap(give, "ulysses", 1)
+    got, keep, came = lax.optimization_barrier((got, keep, came))
+    columns = keep.shape[-1]
+    half = columns // 256 * 128
+    view = (2, 2, 2, 2, rows_here)
+    cut = lambda value: (
+        value[..., :half].reshape(*view, half),
+        value[..., half:].reshape(*view, columns - half),
+    )
+    (keep_a, keep_b), (came_a, came_b) = cut(keep), cut(came)
+    keep_a, give_a = halve(keep_a, came_a, "blk", 1, 2)
+    keep_b, give_b = halve(keep_b, came_b, "ulysses", 2, 3)
+    came_a, came_b = swap(give_a, "blk", 1), swap(give_b, "ulysses", 2)
+    send, grad_both, grad_low = attend_back(
+        got.reshape(length // 128, 2, 32, LANES),
+        attn32,
+        row_total,
+        weights_low,
+        queries,
+        key_rows,
+        value_rows,
+        cosine,
+        sine,
+    )
+    qkv_full = lax.all_gather(qkv_weight, AXES, axis=0, tiled=True)
+    send, came_a, came_b = lax.optimization_barrier((send, came_a, came_b))
+    got = exchange(send.reshape(32, 96, LANES))
+    keep_a, give_a = halve(keep_a, came_a, "ulysses", 2, 2)
+    keep_b, give_b = halve(keep_b, came_b, "blk", 1, 2)
+    came_a, came_b = swap(give_a, "ulysses", 2), swap(give_b, "blk", 1)
+    head_grad = head_grads(hidden_one.reshape(length, model_width), grad_both, grad_low)
+    got, head_grad, came_a, came_b = lax.optimization_barrier((got, head_grad, came_a, came_b))
+    got_grads = exchange(head_grad.astype(BF).reshape(32, rows_here, 3 * HEAD))
+    keep_a, give_a = halve(keep_a, came_a, "blk", 2, 1)
+    keep_b, give_b = halve(keep_b, came_b, "blk", 2, 1)
+    came_a, came_b = swap(give_a, "blk", 2), swap(give_b, "blk", 2)
+    input_grad = last_part(got, qkv_full, flat_tokens, gain_one, grad_middle)
+    input_grad = input_grad.reshape(sequences, per_device, model_width)
+    keep_a, give_a = halve(keep_a, came_a, "blk", 4, 0)
+    keep_b, give_b = halve(keep_b, came_b, "blk", 4, 0)
+    came_a, came_b = swap(give_a, "blk", 4), swap(give_b, "blk", 4)
+    shard_qkv, shard_one = collect(
+        got_grads, qkv_weight, attn_gain.astype(F32).reshape(rows_here, 1)
+    )
+    part_a = keep_a.astype(F32) + came_a.astype(F32)
+    part_b = keep_b.astype(F32) + came_b.astype(F32)
+    shards = jnp.concatenate([part_a, part_b], axis=1)
+    shard_in = shards[:, : 2 * hidden_units]
+    shard_attn = shards[:, 2 * hidden_units : 2 * hidden_units + model_width]
+    shard_out = jnp.transpose(shards[:, 2 * hidden_units + model_width :])
+    shard_two = jnp.sum(shard_in * in_weight.astype(F32), axis=1) / mlp_gain.astype(F32)
+    return (
+        layer_output.reshape(sequences, per_device, model_width),
+        input_grad,
+        shard_one.reshape(rows_here),
+        shard_qkv,
+        shard_attn,
+        shard_two,
+        shard_in,
+        shard_out,
+    )
+
+
 def solution(mesh):
     placed = (
         P(None, ("blk", "ulysses"), None),
@@ -246,8 +829,9 @@
         P(None, ("blk", "ulysses")),
         P(None, ("blk", "ulysses"), None),
     )
+    sizes = (mesh.shape["blk"], mesh.shape["ulysses"])
     return jax.shard_map(
-        body,
+        owner_body if sizes == (8, 4) else ring_body,
         mesh=mesh,
         in_specs=placed,
         out_specs=(

time: 870 us -> 244 us (0.28)
  waiting for transfers between devices: 570 us -> 82 us
  matrix products: 99.2 us -> 0 us
  blocking collectives: 79.2 us -> 0 us
  Pallas kernels: 0 us -> 64.6 us
  local copies, waits for them, and re-layouts: 36 us -> 18.4 us
  other arithmetic: 35.4 us -> 18.7 us
  starting transfers between devices: 32.5 us -> 44.7 us
    all_gather x6 -> x2, waiting for transfers between devices: 246 us -> 0.01 us  [the longest x1 0.01 us: owner_body(): late_full = lax.all_gather(late, AXES, axis=0, tiled=True)]
    reduce_scatter x3 -> x0, waiting for transfers between devices: 216 us -> none  [the longest x1 125 us: body(): lax.psum_scatter(grad_wqkv, ('blk', 'ulysses'), scatter_dimension=0, tile...]
    dot_general x54 -> x0, matrix products: 99.2 us -> none  [the longest x8 16.2 us: block_grads(): jnp.einsum('shqk,sqhd->skhd', weights_low.astype(jnp.float32), grad_scaled)]
    unnamed x2 -> x0, blocking collectives: 79.2 us -> none
    pallas_call x0 -> x8, Pallas kernels: none -> 64.6 us  [the longest x1 16.4 us: attend_back(): pl.pallas_call(attend_back_kernel, grid=(steps,), in_specs=[pl.BlockSpec(...]
    while x80 -> x0, local copies, waits for them, and re-layouts: 15 us -> none
    ppermute x32 -> x16, waiting for transfers between devices: 76.3 us -> 61.3 us  [swap(): return lax.ppermute(value, axis, [(i, i ^ bit) for i in range(size)])]
    convert_element_type x22 -> x10, other arithmetic: 23 us -> 10.3 us  [the longest x8 8.04 us: halve(): total = (keep.astype(F32) + got.astype(F32)).astype(BF)]
  transfers between devices with their start and end apart: 46 -> 23, of which waited for: 28 -> 11; matrix products, arithmetic and copies ran while one was open for 17% -> 13% of each run, Pallas kernels for 0% -> 19%
where the time goes in v2:
time: 244 us; the launch traced here: 243 us
  waiting for transfers between devices  82 us (34%)
  Pallas kernels  64.6 us (26%)
  starting transfers between devices  44.7 us (18%)
  other arithmetic  18.7 us (8%)
  local copies, waits for them, and re-layouts  18.4 us (8%)
  between operations  14.5 us (6%)
    ppermute x16, waiting for transfers between devices, swap(): return lax.ppermute(value, axis, [(i, i ^ bit) for i in range(size)])  61.3 us
    all_to_all x5, starting transfers between devices, exchange(): return lax.all_to_all(value, AXES, split_axis=0, concat_axis=0, tiled=True)  23.1 us
    ppermute x16, starting transfers between devices, swap(): return lax.ppermute(value, axis, [(i, i ^ bit) for i in range(size)])  21.5 us
    all_to_all x5, waiting for transfers between devices, exchange(): return lax.all_to_all(value, AXES, split_axis=0, concat_axis=0, tiled=True)  20 us
    pallas_call x1, Pallas kernels, attend_back(): pl.pallas_call(attend_back_kernel, grid=(steps,), in_specs=[pl.BlockSpec(...  16.4 us
    pallas_call x1, Pallas kernels, attend(): pl.pallas_call(attend_kernel, grid=(steps,), in_specs=[by_row(HEAD), whol...  11.7 us
    pallas_call x1, Pallas kernels, weight_grads(): pl.pallas_call(functools.partial(weight_grads_kernel, in_tiles=in_tiles,...  9.7 us
    convert_element_type x8, other arithmetic, halve(): total = (keep.astype(F32) + got.astype(F32)).astype(BF)  8.04 us
  transfers between devices with their start and end apart: 23, of which 11 were waited for; matrix products, arithmetic and copies ran while one was open for 13% of the time, Pallas kernels for 19%

profile of v2, /device:TPU:0, one launch (start us, length us, event | category | flops | bytes accessed | tf_op | source)
XLA Modules:
  0.0 242.9 jit_solution(8053169219015042712)
XLA Ops:
  7.2 1.6 pad_maximum_fusion.3
  9.9 4.1 %collective-permute-start = (bf16[64,768]{1,0:T(8,128)(2,1)S(1)}, bf16[64,768]{1,0:T(8,128)(2,1)S(1)}, u32[]{:S(2)}, u32[]{:S(2)}) collective-permute-start(bf16[64,768]{1,0:T(8,128)(2,1)S(1)} %get-tuple-element.94), channel_id=1, source_target_pairs={{0,16},{4,20},{8,24},{12,28},{16,0},{20,4},{24,8},{28,12},{1,17},{... | collective-permute-start | bytes 294920 | tf_op jit(solution)/shard_map/ppermute | solution.py:256
  14.0 4.9 %collective-permute-done = bf16[64,768]{1,0:T(8,128)(2,1)S(1)} collective-permute-done((bf16[64,768]{1,0:T(8,128)(2,1)S(1)}, bf16[64,768]{1,0:T(8,128)(2,1)S(1)}, u32[]{:S(2)}, u32[]{:S(2)}) %collective-permute-start) | collective-permute-done | bytes 98336 | tf_op jit(solution)/shard_map/ppermute | solution.py:256
  19.7 5.6 %collective-permute-done.1 = bf16[2,64,768]{2,1,0:T(8,128)(2,1)S(1)} collective-permute-done((bf16[2,64,768]{2,1,0:T(8,128)(2,1)S(1)}, bf16[2,64,768]{2,1,0:T(8,128)(2,1)S(1)}, u32[]{:S(2)}, u32[]{:S(2)}) %collective-permute-start.1) | collective-permute-done | bytes 196640 | tf_op jit(solution)/shard_map/ppermute | solution.py:256
  25.5 1.2 collective-permute-start.4
  27.4 1.6 collective-permute-start.2
  29.9 6.3 %all-to-all-start = ((bf16[32,24,256]{2,1,0:T(8,128)(2,1)}), bf16[32,24,256]{2,1,0:T(8,128)(2,1)S(1)}, u32[]{:S(2)}, u32[]{:S(2)}) async-start(bf16[32,24,256]{2,1,0:T(8,128)(2,1)} %bitcast.26), calls=%async_computation | async-start | bytes 786432 | tf_op jit(solution)/shard_map/all_to_all | solution.py:299
  36.2 1.8 collective-permute-start.5
  38.2 1.5 collective-permute-start.3
  39.8 17.6 %collective-permute-done.5 = bf16[2,2,2,32,768]{4,3,2,1,0:T(8,128)(2,1)S(1)} collective-permute-done((bf16[2,2,2,32,768]{4,3,2,1,0:T(8,128)(2,1)S(1)}, bf16[2,2,2,32,768]{4,3,2,1,0:T(8,128)(2,1)S(1)}, u32[]{:S(2)}, u32[]{:S(2)}) %collective-permute-start.5) | collective-permute-done | bytes 393248 | tf_op jit(solution)/shard_map/ppermute | solution.py:256
  57.5 1.4 pad_maximum_fusion
  59.0 1.9 multiply_sine_fusion
  62.5 1.3 copy.56.cosine
  65.2 1.3 copy.57.sine
  67.4 7.2 %project.1 = (bf16[2,1024,768]{2,1,0:T(8,128)(2,1)}, bf16[2,1024,64]{2,1,0:T(8,128)(2,1)}, bf16[2,1024,64]{2,1,0:T(8,128)(2,1)}, bf16[2,1024,64]{2,1,0:T(8,128)(2,1)}) custom-call(s32[1]{0:T(128)} %bitcast.core, bf16[1024,768]{1,0:T(8,128)(2,1)} %bitcast.22.mine, bf16[1024,768]{1,0:T(8,128)(2,1)} %collective-permute-done.6.other, f32[1,768]{1,0:T(1,128)} %reshape.641.gain, ...), custom_call_target="tpu_custom_call" | custom-call | tf_op jit(solution)/shard_map/project/pallas_call | solution.py:346
  74.6 11.7 %attend.1 = (bf16[2048,2048]{1,0:T(8,128)(2,1)}, f32[2048,64]{1,0:T(8,128)}, f32[2048,1]{1,0:T(8,128)}, bf16[16,2,32,128]{3,2,1,0:T(8,128)(2,1)}) custom-call(bf16[2048,64]{1,0:T(8,128)(2,1)} %bitcast.126, bf16[2048,64]{1,0:T(8,128)(2,1)} %bitcast.128, bf16[2048,64]{1,0:T(8,128)(2,1)} %bitcast.130), custom_call_target="tpu_custom_call" | custom-call | tf_op jit(solution)/shard_map/attend/pallas_call | solution.py:388
  86.3 5.4 %all-to-all-start.1 = ((bf16[32,32,128]{2,1,0:T(8,128)(2,1)}), bf16[32,32,128]{2,1,0:T(8,128)(2,1)S(1)}, u32[]{:S(2)}, u32[]{:S(2)}) async-start(bf16[32,32,128]{2,1,0:T(8,128)(2,1)} %bitcast.149), calls=%async_computation.1 | async-start | bytes 524288 | tf_op jit(solution)/shard_map/all_to_all | solution.py:299
  92.2 9.8 %all-to-all-done.1.got = bf16[32,32,128]{2,1,0:T(8,128)(2,1)S(1)} async-done(((bf16[32,32,128]{2,1,0:T(8,128)(2,1)}), bf16[32,32,128]{2,1,0:T(8,128)(2,1)S(1)}, u32[]{:S(2)}, u32[]{:S(2)}) %all-to-all-start.1) | async-done | bytes 262176 | tf_op jit(solution)/shard_map/all_to_all | solution.py:299
  102.8 8.0 %middle_part.1 = (bf16[128,768]{1,0:T(8,128)(2,1)}, bf16[32,32,128]{2,1,0:T(8,128)(2,1)}, bf16[128,768]{1,0:T(8,128)(2,1)}, bf16[128,768]{1,0:T(8,128)(2,1)}, bf...) custom-call(bf16[32,32,128]{2,1,0:T(8,128)(2,1)} %copy-done.4, ...), custom_call_target="tpu_custom_call" | custom-call | tf_op jit(solution)/shard_map/middle_part/pallas_call | solution.py:478
  110.7 9.7 %weight_grads.1 = (bf16[16,24,4224]{2,1,0:T(8,128)(2,1)}, bf16[16,24,4224]{2,1,0:T(8,128)(2,1)}) custom-call(s32[1]{0:T(128)} %bitcast.core, bf16[128,768]{1,0:T(8,128)(2,1)} %get-tuple-element.51.hidden, bf16[128,768]{1,0:T(8,128)(2,1)} %get-tuple-element.52.attn, bf16[128,768]{1,0:T(8,128)(2,1)} %bitcast.141, bf16[128,2304]{1,0:T(8,128)(2,1)} %get-tuple-element.53.joint, ...), custom_call_target="tpu_custom_call" | custom-call | tf_op jit(solution)/shard_map/weight_grads/pallas_call | solution.py:521
  120.4 2.6 %all-to-all-start.2 = ((bf16[32,32,128]{2,1,0:T(8,128)(2,1)}), bf16[32,32,128]{2,1,0:T(8,128)(2,1)S(1)}, u32[]{:S(2)}, u32[]{:S(2)}) async-start(bf16[32,32,128]{2,1,0:T(8,128)(2,1)} %get-tuple-element.50), calls=%async_computation.2 | async-start | bytes 524288 | tf_op jit(solution)/shard_map/all_to_all | solution.py:299
  123.8 9.8 %all-to-all-done.2 = bf16[32,32,128]{2,1,0:T(8,128)(2,1)S(1)} async-done(((bf16[32,32,128]{2,1,0:T(8,128)(2,1)}), bf16[32,32,128]{2,1,0:T(8,128)(2,1)S(1)}, u32[]{:S(2)}, u32[]{:S(2)}) %all-to-all-start.2) | async-done | bytes 262176 | tf_op jit(solution)/shard_map/all_to_all | solution.py:299
  133.6 2.4 add_convert_fusion
  137.5 2.5 %add_convert_fusion.1 = bf16[16,24,2048]{2,1,0:T(8,128)(2,1)S(1)} fusion(bf16[16,24,4224]{2,1,0:T(8,128)(2,1)} %collective-permute-done.7, bf16[16,24,4224]{2,1,0:T(8,128)(2,1)} %get-tuple-element.63), kind=kLoop, calls=%fused_computation.1 | loop fusion | flops 3145728 | bytes 4718592 | tf_op jit(solution)/shard_map/convert_element_type | solution.py:291
  140.0 1.0 constant_dynamic-slice_fusion.1
  141.0 1.0 copy.81
  142.0 1.5 collective-permute-start.8
  143.5 1.4 copy.58.cosine
  144.8 1.3 copy.59.sine
  146.1 16.4 %attend_back.1 = (bf16[16,2,96,128]{3,2,1,0:T(8,128)(2,1)}, bf16[2048,128]{1,0:T(8,128)(2,1)}, bf16[2048,64]{1,0:T(8,128)(2,1)}) custom-call(bf16[16,2,32,128]{3,2,1,0:T(8,128)(2,1)} %bitcast.138, f32[2048,64]{1,0:T(8,128)} %get-tuple-element.59.attn32, f32[2048,1]{1,0:T(8,128)} %get-tuple-element.60.total, bf16[2048,2048]{1,0:T(8,128)(2,1)} %get-tuple-element.61.weights, ...), custom_call_target="tpu_custom_call" | custom-call | tf_op jit(solution)/shard_map/attend_back/pallas_call | solution.py:594
  162.5 2.7 %collective-permute-done.8 = bf16[2,2,2,24,2048]{4,3,0,1,2:T(8,128)(2,1)} collective-permute-done((bf16[2,2,2,24,2048]{4,3,0,1,2:T(8,128)(2,1)}, bf16[2,2,2,24,2048]{4,3,0,1,2:T(8,128)(2,1)}, u32[]{:S(2)}, u32[]{:S(2)}) %collective-permute-start.8) | collective-permute-done | bytes 786464 | tf_op jit(solution)/shard_map/ppermute | solution.py:256
  165.2 3.4 %all-to-all-start.3 = ((bf16[32,96,128]{2,1,0:T(8,128)(2,1)}), bf16[32,96,128]{2,1,0:T(8,128)(2,1)}, u32[]{:S(2)}, u32[]{:S(2)}) async-start(bf16[32,96,128]{2,1,0:T(8,128)(2,1)} %bitcast.142), calls=%async_computation.3 | async-start | bytes 1572864 | tf_op jit(solution)/shard_map/all_to_all | solution.py:299
  168.6 1.4 fusion
  170.0 1.6 collective-permute-start.11
  171.7 1.4 fusion.1
  173.1 1.6 collective-permute-start.10
  175.4 5.3 %head_grads.1 = f32[768,192]{1,0:T(8,128)} custom-call(bf16[2048,768]{1,0:T(8,128)(2,1)} %bitcast.125, bf16[2048,128]{1,0:T(8,128)(2,1)} %get-tuple-element.67.both, bf16[2048,64]{1,0:T(8,128)(2,1)} %get-tuple-element.68.low), custom_call_target="tpu_custom_call" | custom-call | tf_op jit(solution)/shard_map/head_grads/pallas_call | solution.py:637
  180.7 14.5 %collective-permute-done.10 = bf16[2,2,24,2048]{3,2,0,1:T(8,128)(2,1)S(1)} collective-permute-done((bf16[2,2,24,2048]{3,2,0,1:T(8,128)(2,1)S(1)}, bf16[2,2,24,2048]{3,2,0,1:T(8,128)(2,1)S(1)}, u32[]{:S(2)}, u32[]{:S(2)}) %collective-permute-start.10) | collective-permute-done | bytes 393248 | tf_op jit(solution)/shard_map/ppermute | solution.py:256
  195.5 1.9 convert_element_type.174
  197.4 5.5 %all-to-all-start.4 = ((bf16[32,24,192]{2,1,0:T(8,128)(2,1)}), bf16[32,24,192]{2,1,0:T(8,128)(2,1)S(1)}, u32[]{:S(2)}, u32[]{:S(2)}) async-start(bf16[32,24,192]{2,1,0:T(8,128)(2,1)} %bitcast.52), calls=%async_computation.4 | async-start | bytes 786432 | tf_op jit(solution)/shard_map/all_to_all | solution.py:299
  203.1 1.8 collective-permute-start.14
  205.4 4.5 %last_part.1 = bf16[128,768]{1,0:T(8,128)(2,1)} custom-call(bf16[32,96,128]{2,1,0:T(8,128)(2,1)} %all-to-all-done.3.got, bf16[768,2304]{1,0:T(8,128)(2,1)} %all-gather.5.cloned.1.call-done.weight, bf16[128,768]{1,0:T(8,128)(2,1)} %bitcast.133, f32[1,768]{1,0:T(1,128)} %reshape.641.gain, f32[128,768]{1,0:T(8,128)} %get-tuple-element.72.grad_middle), custom_call_target="tpu_custom_call" | custom-call | tf_op jit(solution)/shard_map/last_part/pallas_call | solution.py:672
  209.9 6.9 %collective-permute-done.14 = bf16[2,24,2048]{2,1,0:T(8,128)(2,1)S(1)} collective-permute-done((bf16[2,24,2048]{2,1,0:T(8,128)(2,1)S(1)}, bf16[2,24,2048]{2,1,0:T(8,128)(2,1)S(1)}, u32[]{:S(2)}, u32[]{:S(2)}) %collective-permute-start.14) | collective-permute-done | bytes 196640 | tf_op jit(solution)/shard_map/ppermute | solution.py:256
  216.9 2.5 %collective-permute-start.15 = (bf16[24,2048]{1,0:T(8,128)(2,1)S(1)}, bf16[24,2048]{1,0:T(8,128)(2,1)S(1)}, u32[]{:S(2)}, u32[]{:S(2)}) collective-permute-start(bf16[24,2048]{1,0:T(8,128)(2,1)S(1)} %dynamic-slice_bitcast_fusion.5), channel_id=1, source_target_pairs={{0,16},{4,20},{8,24},{12,28},{16,0},{20,4},{24,8},{28,12},{1,17},{... | collective-permute-start | bytes 294920 | tf_op jit(solution)/shard_map/ppermute | solution.py:256
  219.4 3.6 %collective-permute-done.12 = bf16[2,24,2176]{2,1,0:T(8,128)(2,1)S(1)} collective-permute-done((bf16[2,24,2176]{2,1,0:T(8,128)(2,1)S(1)}, bf16[2,24,2176]{2,1,0:T(8,128)(2,1)S(1)}, u32[]{:S(2)}, u32[]{:S(2)}) %collective-permute-start.12) | collective-permute-done | bytes 208928 | tf_op jit(solution)/shard_map/ppermute | solution.py:256
  223.9 5.5 %collective-permute-done.13 = bf16[24,2176]{1,0:T(8,128)(2,1)S(1)} collective-permute-done((bf16[24,2176]{1,0:T(8,128)(2,1)S(1)}, bf16[24,2176]{1,0:T(8,128)(2,1)S(1)}, u32[]{:S(2)}, u32[]{:S(2)}) %collective-permute-start.13) | collective-permute-done | bytes 104480 | tf_op jit(solution)/shard_map/ppermute | solution.py:256
  232.8 1.9 collect.1
  234.7 1.3 reduce.2
  (92 shorter events, 17.2 us)
Async XLA Ops:
  7.2 94.9 %all-gather.3.cloned.1.call-start = ((), (), s32[]{:S(2)}) async-start(), calls=%async_computation.5 | async-start | bytes 6690816 | tf_op jit(solution)/shard_map/all_gather | solution.py:715
  9.9 9.0 %collective-permute-start = (bf16[64,768]{1,0:T(8,128)(2,1)S(1)}, bf16[64,768]{1,0:T(8,128)(2,1)S(1)}, u32[]{:S(2)}, u32[]{:S(2)}) collective-permute-start(bf16[64,768]{1,0:T(8,128)(2,1)S(1)} %get-tuple-element.94), channel_id=1, source_target_pairs={{0,16},{4,20},{8,24},{12,28},{16,0},{20,4},{24,8},{28,12},{1,17},{... | collective-permute-start | bytes 294920 | tf_op jit(solution)/shard_map/ppermute | solution.py:256
  18.9 7.8 %copy-start.7 = (bf16[24]{0:T(256)(128)(2,1)S(1)}, bf16[24]{0:T(256)(128)(2,1)}, u32[]{:S(2)}) copy-start(bf16[24]{0:T(256)(128)(2,1)} %param.9) | copy-start | bytes 148
  18.9 7.8 %copy-start.8 = (bf16[24]{0:T(256)(128)(2,1)S(1)}, bf16[24]{0:T(256)(128)(2,1)}, u32[]{:S(2)}) copy-start(bf16[24]{0:T(256)(128)(2,1)} %param.12) | copy-start | bytes 148
  18.9 7.9 %copy-start.5 = (bf16[24,2304]{1,0:T(8,128)(2,1)S(1)}, bf16[24,2304]{1,0:T(8,128)(2,1)}, u32[]{:S(2)}) copy-start(bf16[24,2304]{1,0:T(8,128)(2,1)} %weight.1) | copy-start | bytes 331780
  18.9 6.4 %collective-permute-start.1 = (bf16[2,64,768]{2,1,0:T(8,128)(2,1)S(1)}, bf16[2,64,768]{2,1,0:T(8,128)(2,1)S(1)}, u32[]{:S(2)}, u32[]{:S(2)}) collective-permute-start(bf16[2,64,768]{2,1,0:T(8,128)(2,1)S(1)} %maximum_select_fusion.8), channel_id=1, source_target_pairs={{0,8},{4,12},{8,0},{12,4},{16,24},{20,28},{24,16},{28,20},{1,9},{5... | collective-permute-start | bytes 589832 | tf_op jit(solution)/shard_map/ppermute | solution.py:256
  25.5 10.7 %collective-permute-start.4 = (bf16[2,2,32,768]{3,2,1,0:T(8,128)(2,1)S(1)}, bf16[2,2,32,768]{3,2,1,0:T(8,128)(2,1)S(1)}, u32[]{:S(2)}, u32[]{:S(2)}) collective-permute-start(bf16[2,2,32,768]{3,2,1,0:T(8,128)(2,1)S(1)} %get-tuple-element.90), channel_id=1, source_target_pairs={{0,2},{1,3},{2,0},{3,1},{4,6},{5,7},{6,4},{7,5},{8,10},{9,11},{10,... | collective-permute-start | bytes 589832 | tf_op jit(solution)/shard_map/ppermute | solution.py:256
  27.4 10.7 %collective-permute-start.2 = (bf16[2,2,32,768]{3,2,1,0:T(8,128)(2,1)S(1)}, bf16[2,2,32,768]{3,2,1,0:T(8,128)(2,1)S(1)}, u32[]{:S(2)}, u32[]{:S(2)}) collective-permute-start(bf16[2,2,32,768]{3,2,1,0:T(8,128)(2,1)S(1)} %get-tuple-element.87), channel_id=1, source_target_pairs={{0,4},{4,0},{8,12},{12,8},{16,20},{20,16},{24,28},{28,24},{1,5},{5... | collective-permute-start | bytes 589832 | tf_op jit(solution)/shard_map/ppermute | solution.py:256
  29.9 29.1 %all-to-all-start = ((bf16[32,24,256]{2,1,0:T(8,128)(2,1)}), bf16[32,24,256]{2,1,0:T(8,128)(2,1)S(1)}, u32[]{:S(2)}, u32[]{:S(2)}) async-start(bf16[32,24,256]{2,1,0:T(8,128)(2,1)} %bitcast.26), calls=%async_computation | async-start | bytes 786432 | tf_op jit(solution)/shard_map/all_to_all | solution.py:299
  36.2 21.2 %collective-permute-start.5 = (bf16[2,2,2,32,768]{4,3,2,1,0:T(8,128)(2,1)S(1)}, bf16[2,2,2,32,768]{4,3,2,1,0:T(8,128)(2,1)S(1)}, u32[]{:S(2)}, u32[]{:S(2)}) collective-permute-start(bf16[2,2,2,32,768]{4,3,2,1,0:T(8,128)(2,1)S(1)} %maximum_select_fusion.6), channel_id=1, source_target_pairs={{0,4},{4,0},{8,12},{12,8},{16,20},{20,16},{24,28},{28,24},{1,5},{5... | collective-permute-start | bytes 1179656 | tf_op jit(solution)/shard_map/ppermute | solution.py:256
  38.2 19.3 %collective-permute-start.3 = (bf16[2,2,2,32,768]{4,3,2,1,0:T(8,128)(2,1)S(1)}, bf16[2,2,2,32,768]{4,3,2,1,0:T(8,128)(2,1)S(1)}, u32[]{:S(2)}, u32[]{:S(2)}) collective-permute-start(bf16[2,2,2,32,768]{4,3,2,1,0:T(8,128)(2,1)S(1)} %maximum_select_fusion.4), channel_id=1, source_target_pairs={{0,2},{1,3},{2,0},{3,1},{4,6},{5,7},{6,4},{7,5},{8,10},{9,11},{10,... | collective-permute-start | bytes 1179656 | tf_op jit(solution)/shard_map/ppermute | solution.py:256
  58.9 7.5 %copy-start = (bf16[32,24,256]{2,1,0:T(8,128)(2,1)}, bf16[32,24,256]{2,1,0:T(8,128)(2,1)S(1)}, u32[]{:S(2)}) copy-start(bf16[32,24,256]{2,1,0:T(8,128)(2,1)S(1)} %all-to-all-done) | copy-start | bytes 1179652
  58.9 8.4 %collective-permute-start.6 = (bf16[1024,768]{1,0:T(8,128)(2,1)}, bf16[1024,768]{1,0:T(8,128)(2,1)}, u32[]{:S(2)}, u32[]{:S(2)}) collective-permute-start(bf16[1024,768]{1,0:T(8,128)(2,1)} %bitcast.22.mine), channel_id=1, source_target_pairs={{0,1},{1,0},{2,3},{3,2},{4,5},{5,4},{6,7},{7,6},{8,9},{9,8},{10,11... | collective-permute-start | bytes 4718600 | tf_op jit(solution)/shard_map/ppermute | solution.py:256
  86.3 15.8 %all-to-all-start.1 = ((bf16[32,32,128]{2,1,0:T(8,128)(2,1)}), bf16[32,32,128]{2,1,0:T(8,128)(2,1)S(1)}, u32[]{:S(2)}, u32[]{:S(2)}) async-start(bf16[32,32,128]{2,1,0:T(8,128)(2,1)} %bitcast.149), calls=%async_computation.1 | async-start | bytes 524288 | tf_op jit(solution)/shard_map/all_to_all | solution.py:299
  102.1 0.7 copy-start.4
  120.4 13.2 %collective-permute-start.7 = (bf16[16,24,4224]{2,1,0:T(8,128)(2,1)}, bf16[16,24,4224]{2,1,0:T(8,128)(2,1)}, u32[]{:S(2)}, u32[]{:S(2)}) collective-permute-start(bf16[16,24,4224]{2,1,0:T(8,128)(2,1)} %get-tuple-element.57), channel_id=1, source_target_pairs={{0,1},{1,0},{2,3},{3,2},{4,5},{5,4},{6,7},{7,6},{8,9},{9,8},{10,11... | collective-permute-start | bytes 9732104 | tf_op jit(solution)/shard_map/ppermute | solution.py:256
  120.4 13.2 %all-to-all-start.2 = ((bf16[32,32,128]{2,1,0:T(8,128)(2,1)}), bf16[32,32,128]{2,1,0:T(8,128)(2,1)S(1)}, u32[]{:S(2)}, u32[]{:S(2)}) async-start(bf16[32,32,128]{2,1,0:T(8,128)(2,1)} %get-tuple-element.50), calls=%async_computation.2 | async-start | bytes 524288 | tf_op jit(solution)/shard_map/all_to_all | solution.py:299
  123.0 82.4 %all-gather.5.cloned.1.call-start = ((), (), s32[]{:S(2)}) async-start(), calls=%async_computation.6 | async-start | bytes 3649536 | tf_op jit(solution)/shard_map/all_gather | solution.py:782
  133.6 2.4 %copy-start.3 = (bf16[32,32,128]{2,1,0:T(8,128)(2,1)}, bf16[32,32,128]{2,1,0:T(8,128)(2,1)S(1)}, u32[]{:S(2)}) copy-start(bf16[32,32,128]{2,1,0:T(8,128)(2,1)S(1)} %all-to-all-done.2) | copy-start | bytes 786436
  137.2 27.9 %collective-permute-start.9 = (bf16[2,2,2,24,2176]{4,3,0,1,2:T(8,128)(2,1)}, bf16[2,2,2,24,2176]{4,3,0,1,2:T(8,128)(2,1)}, u32[]{:S(2)}, u32[]{:S(2)}) collective-permute-start(bf16[2,2,2,24,2176]{4,3,0,1,2:T(8,128)(2,1)} %bitcast.117), channel_id=1, source_target_pairs={{0,2},{1,3},{2,0},{3,1},{4,6},{5,7},{6,4},{7,5},{8,10},{9,11},{10,... | collective-permute-start | bytes 2506760 | tf_op jit(solution)/shard_map/ppermute | solution.py:256
  142.0 23.2 %collective-permute-start.8 = (bf16[2,2,2,24,2048]{4,3,0,1,2:T(8,128)(2,1)}, bf16[2,2,2,24,2048]{4,3,0,1,2:T(8,128)(2,1)}, u32[]{:S(2)}, u32[]{:S(2)}) collective-permute-start(bf16[2,2,2,24,2048]{4,3,0,1,2:T(8,128)(2,1)} %bitcast.118), channel_id=1, source_target_pairs={{0,4},{4,0},{8,12},{12,8},{16,20},{20,16},{24,28},{28,24},{1,5},{5... | collective-permute-start | bytes 2359304 | tf_op jit(solution)/shard_map/ppermute | solution.py:256
  165.2 30.3 %all-to-all-start.3 = ((bf16[32,96,128]{2,1,0:T(8,128)(2,1)}), bf16[32,96,128]{2,1,0:T(8,128)(2,1)}, u32[]{:S(2)}, u32[]{:S(2)}) async-start(bf16[32,96,128]{2,1,0:T(8,128)(2,1)} %bitcast.142), calls=%async_computation.3 | async-start | bytes 1572864 | tf_op jit(solution)/shard_map/all_to_all | solution.py:299
  168.6 3.1 %copy-start.1 = (bf16[2,2,1,2,24,2048]{5,4,3,2,1,0:T(8,128)(2,1)S(1)}, bf16[2,2,1,2,24,2048]{5,4,3,2,1,0:T(8,128)(2,1)}, u32[]{:S(2)}) copy-start(bf16[2,2,1,2,24,2048]{5,4,3,2,1,0:T(8,128)(2,1)} %get-tuple-element.84) | copy-start | bytes 2359300
  170.0 25.2 %collective-permute-start.11 = (bf16[2,2,24,2176]{3,2,0,1:T(8,128)(2,1)S(1)}, bf16[2,2,24,2176]{3,2,0,1:T(8,128)(2,1)S(1)}, u32[]{:S(2)}, u32[]{:S(2)}) collective-permute-start(bf16[2,2,24,2176]{3,2,0,1:T(8,128)(2,1)S(1)} %dynamic-slice_bitcast_fusion), channel_id=1, source_target_pairs={{0,4},{4,0},{8,12},{12,8},{16,20},{20,16},{24,28},{28,24},{1,5},{5... | collective-permute-start | bytes 1253384 | tf_op jit(solution)/shard_map/ppermute | solution.py:256
  173.1 22.1 %collective-permute-start.10 = (bf16[2,2,24,2048]{3,2,0,1:T(8,128)(2,1)S(1)}, bf16[2,2,24,2048]{3,2,0,1:T(8,128)(2,1)S(1)}, u32[]{:S(2)}, u32[]{:S(2)}) collective-permute-start(bf16[2,2,24,2048]{3,2,0,1:T(8,128)(2,1)S(1)} %dynamic-slice_bitcast_fusion.1), channel_id=1, source_target_pairs={{0,2},{1,3},{2,0},{3,1},{4,6},{5,7},{6,4},{7,5},{8,10},{9,11},{10,... | collective-permute-start | bytes 1179656 | tf_op jit(solution)/shard_map/ppermute | solution.py:256
  197.4 34.7 %all-to-all-start.4 = ((bf16[32,24,192]{2,1,0:T(8,128)(2,1)}), bf16[32,24,192]{2,1,0:T(8,128)(2,1)S(1)}, u32[]{:S(2)}, u32[]{:S(2)}) async-start(bf16[32,24,192]{2,1,0:T(8,128)(2,1)} %bitcast.52), calls=%async_computation.4 | async-start | bytes 786432 | tf_op jit(solution)/shard_map/all_to_all | solution.py:299
  203.1 13.7 %collective-permute-start.14 = (bf16[2,24,2048]{2,1,0:T(8,128)(2,1)S(1)}, bf16[2,24,2048]{2,1,0:T(8,128)(2,1)S(1)}, u32[]{:S(2)}, u32[]{:S(2)}) collective-permute-start(bf16[2,24,2048]{2,1,0:T(8,128)(2,1)S(1)} %dynamic-slice_bitcast_fusion.3), channel_id=1, source_target_pairs={{0,8},{4,12},{8,0},{12,4},{16,24},{20,28},{24,16},{28,20},{1,9},{5... | collective-permute-start | bytes 589832 | tf_op jit(solution)/shard_map/ppermute | solution.py:256
  205.1 17.9 %collective-permute-start.12 = (bf16[2,24,2176]{2,1,0:T(8,128)(2,1)S(1)}, bf16[2,24,2176]{2,1,0:T(8,128)(2,1)S(1)}, u32[]{:S(2)}, u32[]{:S(2)}) collective-permute-start(bf16[2,24,2176]{2,1,0:T(8,128)(2,1)S(1)} %dynamic-slice_bitcast_fusion.2), channel_id=1, source_target_pairs={{0,8},{4,12},{8,0},{12,4},{16,24},{20,28},{24,16},{28,20},{1,9},{5... | collective-permute-start | bytes 626696 | tf_op jit(solution)/shard_map/ppermute | solution.py:256
  209.9 20.2 %copy-start.6 = (bf16[24,2304]{1,0:T(8,128)(2,1)S(1)}, bf16[24,2304]{1,0:T(8,128)(2,1)}, u32[]{:S(2)}) copy-start(bf16[24,2304]{1,0:T(8,128)(2,1)} %param.13) | copy-start | bytes 331780
  216.9 7.0 %collective-permute-start.15 = (bf16[24,2048]{1,0:T(8,128)(2,1)S(1)}, bf16[24,2048]{1,0:T(8,128)(2,1)S(1)}, u32[]{:S(2)}, u32[]{:S(2)}) collective-permute-start(bf16[24,2048]{1,0:T(8,128)(2,1)S(1)} %dynamic-slice_bitcast_fusion.5), channel_id=1, source_target_pairs={{0,16},{4,20},{8,24},{12,28},{16,0},{20,4},{24,8},{28,12},{1,17},{... | collective-permute-start | bytes 294920 | tf_op jit(solution)/shard_map/ppermute | solution.py:256
  223.0 6.4 %collective-permute-start.13 = (bf16[24,2176]{1,0:T(8,128)(2,1)S(1)}, bf16[24,2176]{1,0:T(8,128)(2,1)S(1)}, u32[]{:S(2)}, u32[]{:S(2)}) collective-permute-start(bf16[24,2176]{1,0:T(8,128)(2,1)S(1)} %dynamic-slice_bitcast_fusion.4), channel_id=1, source_target_pairs={{0,16},{4,20},{8,24},{12,28},{16,0},{20,4},{24,8},{28,12},{1,17},{... | collective-permute-start | bytes 313352 | tf_op jit(solution)/shard_map/ppermute | solution.py:256
  232.1 0.7 copy-start.2
Sparse Core Ops, SparseCore 0:
  11.4 80.1 all-gather.2
  126.8 73.8 all-gather.4

commit v3 on v2

--- a/solution.py
+++ b/solution.py
@@ -272,9 +272,9 @@
     y = my_bit("ulysses", 2)
     keep = lax.dynamic_index_in_dim(tokens, z2, 0, keepdims=False)
     give = lax.dynamic_index_in_dim(tokens, 1 - z2, 0, keepdims=False)
-    wide = join(keep, swap(give, "blk", 4), z2, 0)
-    wide = join(wide, swap(wide, "blk", 2), z1, 1)
-    wide = wide.reshape(2, 2, 2, rows // 2, width)
+    near = join(keep, swap(keep, "blk", 2), z1, 0)
+    far = join(swap(give, "blk", 4), swap(give, "blk", 6), z1, 0)
+    wide = join(near, far, z2, 0).reshape(2, 2, 2, rows // 2, width)
     part_a, part_b = wide[:, :, 0], wide[:, :, 1]
     from_a, from_b = swap(part_a, "blk", 1), swap(part_b, "ulysses", 2)
     part_a = join(part_a, from_a, x, 2)
@@ -293,6 +293,16 @@
     keep = lax.dynamic_index_in_dim(total, side, dim, keepdims=False)
     give = lax.dynamic_index_in_dim(total, 1 - side, dim, keepdims=False)
     return keep, give
+
+
+def turned_tables(rows):
+    lane = jnp.arange(LANES, dtype=jnp.int32) % (HEAD // 2)
+    frequency = THETA ** (-(lane.astype(F32) * 2.0) / HEAD)
+    row = jnp.arange(rows, dtype=jnp.int32)
+    half = rows // 2
+    position = row % half // 64 * 128 + row // half * 64 + row % 64
+    angles = position.astype(F32)[:, None] * frequency[None, :]
+    return jnp.cos(angles), jnp.sin(angles)
 
 
 def exchange(value):
@@ -403,17 +413,26 @@
             jax.ShapeDtypeStruct((length, 1), F32),
             jax.ShapeDtypeStruct((length // 128, 2, 32, LANES), BF),
         ],
+        cost_estimate=pl.CostEstimate(
+            flops=4 * length * length * HEAD * 4,
+            bytes_accessed=2 * length * length,
+            transcendentals=length * length,
+        ),
         name="attend",
     )(queries, key_rows, value_rows)
 
 
 def middle_kernel(
-    got, tokens, late, gain, grad_out, layer_output, send, attn, hidden, grad_joint, activation,
-    branch, grad_middle
+    got, tokens, late, gain, grad_out, layer_output, send, acts, grad_middle
 ):
     width = tokens.shape[1]
-    hidden_units = activation.shape[1]
+    hidden_units = (late.shape[1] - width) // 3
     cut = 2 * hidden_units
+    attn, hidden = acts.at[:, :width], acts.at[:, width : 2 * width]
+    acts[:, 2 * width : 3 * width] = grad_out[...]
+    grad_joint = acts.at[:, 3 * width : 3 * width + cut]
+    activation = acts.at[:, 3 * width + cut : 3 * width + cut + hidden_units]
+    branch = acts.at[:, 3 * width + cut + hidden_units :]
     for s in range(2):
         for h in range(0, HEADS, 2):
             left, right = got[owner_slot(s, h)], got[owner_slot(s, h + 1)]
@@ -468,11 +487,7 @@
     shapes = [
         ((rows, width), BF),
         (got.shape, BF),
-        ((rows, width), BF),
-        ((rows, width), BF),
-        ((rows, 2 * hidden_units), BF),
-        ((rows, hidden_units), BF),
-        ((rows, width), BF),
+        ((rows, 4 * width + 3 * hidden_units), BF),
         ((rows, width), F32),
     ]
     return pl.pallas_call(
@@ -483,57 +498,73 @@
 
 
 def weight_grads_kernel(
-    core, hidden, attn, grad_out, joint, branch, active, keep, give, *, in_tiles, attn_tiles
+    place, hidden, attn, grad_out, right, hidden_too, attn_too, grad_out_too, right_too,
+    keep_a, give_a, keep_b, give_b, total, *, in_tiles, attn_tiles
 ):
     tile = pl.program_id(0)
-
-    def write(left, right):
-        total = lax.dot_general(left[...], right[...], BY_ROW, preferred_element_type=F32)
-        total = total.reshape(keep.shape[0], 2, *keep.shape[1:])
-        first, second = total[:, 0], total[:, 1]
-        keep[...] = jnp.where(core[0] == 0, first, second).astype(BF)
-        give[...] = jnp.where(core[0] == 0, second, first).astype(BF)
+    x, y, core = place[0], place[1], place[2]
+
+    def multiply(left, left_too):
+        product = lax.dot_general(
+            left[...], right[...], BY_ROW, preferred_element_type=F32
+        ) + lax.dot_general(left_too[...], right_too[...], BY_ROW, preferred_element_type=F32)
+        total[...] = product.reshape(total.shape)
+
+    def write_b():
+        keep_b[...] = total[:, :, y, core].astype(BF)
+        give_b[...] = total[:, :, 1 - y, core].astype(BF)
 
     @pl.when(tile < in_tiles)
     def _():
-        write(hidden, joint)
+        multiply(hidden, hidden_too)
+        keep_a[...] = total[:, x, :, core].astype(BF)
+        give_a[...] = total[:, 1 - x, :, core].astype(BF)
 
     @pl.when((tile >= in_tiles) & (tile < in_tiles + attn_tiles))
     def _():
-        write(attn, branch)
+        multiply(attn, attn_too)
+        write_b()
 
     @pl.when(tile >= in_tiles + attn_tiles)
     def _():
-        write(grad_out, active)
-
-
-def weight_grads(core, hidden, attn, grad_out, joint, branch, active, rows_here):
-    rows, width = hidden.shape
-    in_tiles, attn_tiles = joint.shape[1] // TILE, width // TILE
-    out_tiles = active.shape[1] // TILE
+        multiply(grad_out, grad_out_too)
+        write_b()
+
+
+def weight_grads(place, acts, acts_too, width, hidden_units, rows_here):
+    rows = acts.shape[0]
+    in_tiles, attn_tiles = 2 * hidden_units // TILE, width // TILE
+    out_tiles = hidden_units // TILE
+    first = 3 * width // TILE
+    last = first + in_tiles + out_tiles
+    whole = lambda i: pl.BlockSpec((rows, width), lambda t: (0, i))
+
+    def source(t):
+        rest = t - in_tiles - attn_tiles
+        late = jnp.where(rest < 0, last + t - in_tiles, first + in_tiles + rest)
+        return 0, jnp.where(t < in_tiles, first + t, late)
+
+    sides = [whole(1), whole(0), whole(2), pl.BlockSpec((rows, TILE), source)]
+    zs = width // (8 * rows_here)
+    block = (zs, 2, rows_here, TILE)
+    out_a = pl.BlockSpec(block, lambda t: (0, 0, 0, jnp.minimum(t, in_tiles - 1)))
+    out_b = pl.BlockSpec(block, lambda t: (0, 0, 0, jnp.maximum(t - in_tiles, 0)))
+    shape = lambda tiles: jax.ShapeDtypeStruct((zs, 2, rows_here, tiles * TILE), BF)
     tiles = in_tiles + attn_tiles + out_tiles
-    whole = pl.BlockSpec((rows, width), lambda t: (0, 0))
-    part = lambda first, count: pl.BlockSpec(
-        (rows, TILE), lambda t: (0, jnp.clip(t - first, 0, count - 1))
-    )
-    pairs = width // (2 * rows_here)
-    result = pl.BlockSpec((pairs, rows_here, TILE), lambda t: (0, 0, t))
     return pl.pallas_call(
         functools.partial(weight_grads_kernel, in_tiles=in_tiles, attn_tiles=attn_tiles),
         grid=(tiles,),
-        in_specs=[
-            smem(),
-            whole,
-            whole,
-            whole,
-            part(0, in_tiles),
-            part(in_tiles, attn_tiles),
-            part(in_tiles + attn_tiles, out_tiles),
-        ],
-        out_specs=[result, result],
-        out_shape=[jax.ShapeDtypeStruct((pairs, rows_here, tiles * TILE), BF)] * 2,
+        in_specs=[smem()] + sides + sides,
+        out_specs=[out_a, out_a, out_b, out_b],
+        out_shape=[shape(in_tiles)] * 2 + [shape(attn_tiles + out_tiles)] * 2,
+        scratch_shapes=[pltpu.VMEM((zs, 2, 2, 2, rows_here, TILE), F32)],
+        cost_estimate=pl.CostEstimate(
+            flops=4 * rows * width * tiles * TILE,
+            bytes_accessed=4 * acts.size + 2 * width * tiles * TILE,
+            transcendentals=0,
+        ),
         name="weight_grads",
-    )(core, hidden, attn, grad_out, joint, branch, active)
+    )(place, *[acts] * 4, *[acts_too] * 4)
 
 
 def attend_back_kernel(
@@ -614,21 +645,32 @@
             jax.ShapeDtypeStruct((length, HEAD), BF),
         ],
         scratch_shapes=[pltpu.VMEM((length, HEAD), F32)] * 3,
+        cost_estimate=pl.CostEstimate(
+            flops=14 * length * length * HEAD * 4,
+            bytes_accessed=2 * length * length,
+            transcendentals=0,
+        ),
         name="attend_back",
     )(got, attn32, total, weights, queries, key_rows, value_rows, cosine, sine)
 
 
-def head_grads_kernel(hidden, both, low, result):
-    @pl.when(pl.program_id(0) == 0)
+def head_grads_kernel(hidden, both, low, result, total):
+    step = pl.program_id(0)
+
+    @pl.when(step == 0)
     def _():
-        result[...] = jnp.zeros_like(result)
-
-    result[:, :LANES] += lax.dot_general(
+        total[...] = jnp.zeros_like(total)
+
+    total[:, :LANES] += lax.dot_general(
         hidden[...], both[...], BY_ROW, preferred_element_type=F32
     )
-    result[:, LANES:] += lax.dot_general(
+    total[:, LANES:] += lax.dot_general(
         hidden[...], low[...], BY_ROW, preferred_element_type=F32
     )
+
+    @pl.when(step == pl.num_programs(0) - 1)
+    def _():
+        result[...] = total[...].astype(BF)
 
 
 def head_grads(hidden, both, low):
@@ -639,7 +681,13 @@
         grid=(length // (2 * BLOCK),),
         in_specs=[by_row(width), by_row(LANES), by_row(HEAD)],
         out_specs=pl.BlockSpec((width, 3 * HEAD), lambda i: (0, 0)),
-        out_shape=jax.ShapeDtypeStruct((width, 3 * HEAD), F32),
+        out_shape=jax.ShapeDtypeStruct((width, 3 * HEAD), BF),
+        scratch_shapes=[pltpu.VMEM((width, 3 * HEAD), F32)],
+        cost_estimate=pl.CostEstimate(
+            flops=6 * HEAD * length * width,
+            bytes_accessed=2 * length * (width + 3 * HEAD),
+            transcendentals=0,
+        ),
         name="head_grads",
     )(hidden, both, low)
 
@@ -711,6 +759,8 @@
     rows = sequences * per_device
     length = per_device * 32
     core = my_bit("ulysses", 1).astype(jnp.int32).reshape(1)
+    place = jnp.stack([my_bit("blk", 1), my_bit("ulysses", 2), my_bit("ulysses", 1)])
+    place = place.astype(jnp.int32)
     late = jnp.concatenate([in_weight, attn_out_weight, jnp.transpose(out_weight)], axis=1)
     late_full = lax.all_gather(late, AXES, axis=0, tiled=True)
     by_head = qkv_weight.reshape(rows_here, 3, HEADS, HEAD).transpose(2, 0, 1, 3)
@@ -722,16 +772,10 @@
     packed = jnp.concatenate([packed, packed[:, -1:]], axis=1)
     packed = jnp.broadcast_to(packed[None], (2,) + packed.shape)
     mixed = exchange(packed.reshape(32, rows_here, 4 * HEAD))
-    mine, other, mixed = gather_sequence(tokens, mixed)
+    mine, other, (mixed, cosine, sine) = gather_sequence(tokens, (mixed, *turned_tables(length)))
     weight_here = mixed.reshape(model_width, 4 * HEAD)
     gain_one = weight_here[:, 3 * HEAD].reshape(1, model_width).astype(F32)
     gain_two = weight_here[:, 3 * HEAD + 1].reshape(1, model_width).astype(F32)
-    cosine, sine = rotation(0, length, HEAD)
-    by_core = lambda table: jnp.tile(
-        table.reshape(length // 128, 2, 64, HEAD).transpose(1, 0, 2, 3).reshape(length, HEAD),
-        (1, 2),
-    )
-    cosine, sine = by_core(cosine), by_core(sine)
     hidden_one, queries, key_rows, value_rows = project(
         core,
         mine,
@@ -748,25 +792,16 @@
     got = exchange(send.reshape(32, 32, LANES))
     flat_tokens = tokens.reshape(rows, model_width)
     grad_out = cotangent.reshape(rows, model_width)
-    layer_output, send, attn_cat, hidden_two, grad_joint, activation, branch, grad_middle = (
-        middle_part(got, flat_tokens, late_full, gain_two, grad_out)
+    layer_output, send, acts, grad_middle = middle_part(
+        got, flat_tokens, late_full, gain_two, grad_out
     )
     got = exchange(send)
-    keep, give = weight_grads(
-        core, hidden_two, attn_cat, grad_out, grad_joint, branch, activation, rows_here
-    )
-    came = swap(give, "ulysses", 1)
-    got, keep, came = lax.optimization_barrier((got, keep, came))
-    columns = keep.shape[-1]
-    half = columns // 256 * 128
-    view = (2, 2, 2, 2, rows_here)
-    cut = lambda value: (
-        value[..., :half].reshape(*view, half),
-        value[..., half:].reshape(*view, columns - half),
-    )
-    (keep_a, keep_b), (came_a, came_b) = cut(keep), cut(came)
-    keep_a, give_a = halve(keep_a, came_a, "blk", 1, 2)
-    keep_b, give_b = halve(keep_b, came_b, "ulysses", 2, 3)
+    acts_too = swap(acts, "ulysses", 1)
+    parts = weight_grads(place, acts, acts_too, model_width, hidden_units, rows_here)
+    got, parts = lax.optimization_barrier((got, parts))
+    keep_a, give_a, keep_b, give_b = (
+        part.reshape(2, 2, *part.shape[1:]) for part in parts
+    )
     came_a, came_b = swap(give_a, "blk", 1), swap(give_b, "ulysses", 2)
     send, grad_both, grad_low = attend_back(
         got.reshape(length // 128, 2, 32, LANES),
@@ -786,22 +821,29 @@
     keep_b, give_b = halve(keep_b, came_b, "blk", 1, 2)
     came_a, came_b = swap(give_a, "ulysses", 2), swap(give_b, "blk", 1)
     head_grad = head_grads(hidden_one.reshape(length, model_width), grad_both, grad_low)
-    got, head_grad, came_a, came_b = lax.optimization_barrier((got, head_grad, came_a, came_b))
-    got_grads = exchange(head_grad.astype(BF).reshape(32, rows_here, 3 * HEAD))
-    keep_a, give_a = halve(keep_a, came_a, "blk", 2, 1)
-    keep_b, give_b = halve(keep_b, came_b, "blk", 2, 1)
-    came_a, came_b = swap(give_a, "blk", 2), swap(give_b, "blk", 2)
+    got, head_grad, came_a, came_b, qkv_full = lax.optimization_barrier(
+        (got, head_grad, came_a, came_b, qkv_full)
+    )
+    got_grads = exchange(head_grad.reshape(32, rows_here, 3 * HEAD))
+    total = [
+        (keep.astype(F32) + came.astype(F32)).astype(BF).reshape(4, rows_here, -1)
+        for keep, came in ((keep_a, came_a), (keep_b, came_b))
+    ]
+    z = lax.axis_index("blk") // 2
+
+    def rows_of(owner):
+        return jnp.concatenate(
+            [lax.dynamic_index_in_dim(part, owner, 0, keepdims=False) for part in total], axis=1
+        )
+
+    shards = rows_of(z).astype(F32)
+    for step in (2, 3, 1):
+        shards = shards + swap(rows_of(z ^ step), "blk", 2 * step).astype(F32)
     input_grad = last_part(got, qkv_full, flat_tokens, gain_one, grad_middle)
     input_grad = input_grad.reshape(sequences, per_device, model_width)
-    keep_a, give_a = halve(keep_a, came_a, "blk", 4, 0)
-    keep_b, give_b = halve(keep_b, came_b, "blk", 4, 0)
-    came_a, came_b = swap(give_a, "blk", 4), swap(give_b, "blk", 4)
     shard_qkv, shard_one = collect(
         got_grads, qkv_weight, attn_gain.astype(F32).reshape(rows_here, 1)
     )
-    part_a = keep_a.astype(F32) + came_a.astype(F32)
-    part_b = keep_b.astype(F32) + came_b.astype(F32)
-    shards = jnp.concatenate([part_a, part_b], axis=1)
     shard_in = shards[:, : 2 * hidden_units]
     shard_attn = shards[:, 2 * hidden_units : 2 * hidden_units + model_width]
     shard_out = jnp.transpose(shards[:, 2 * hidden_units + model_width :])

time: 244 us -> 218 us (0.89)
  waiting for transfers between devices: 82 us -> 67.5 us
  local copies, waits for them, and re-layouts: 18.4 us -> 10.8 us
  other arithmetic: 18.7 us -> 13.5 us
    ppermute x16, waiting for transfers between devices: 61.3 us -> 42.6 us  [swap(): return lax.ppermute(value, axis, [(i, i ^ bit) for i in range(size)])]
    another operation x10 -> x0, local copies, waits for them, and re-layouts: 7.96 us -> none  [owner_body(): jnp.tile(table.reshape(length // 128, 2, 64, HEAD).transpose(1, 0, 2, 3)....]
    convert_element_type x8 -> x2, other arithmetic: 8.04 us -> 0.38 us  [halve(): total = (keep.astype(F32) + got.astype(F32)).astype(BF)]
    sin x1, other arithmetic: 1.89 us -> 5.59 us  [turned_tables(): return (jnp.cos(angles), jnp.sin(angles))]
    dynamic_slice x4 -> x0, local copies, waits for them, and re-layouts: 3.16 us -> none  [the longest x2 1.93 us: halve(): give = lax.dynamic_index_in_dim(total, 1 - side, dim, keepdims=False)]
    all_to_all x5, waiting for transfers between devices: 20 us -> 23 us  [exchange(): return lax.all_to_all(value, AXES, split_axis=0, concat_axis=0, tiled=True)]
  transfers between devices with their start and end apart: 23 -> 23, of which waited for: 11 -> 13; matrix products, arithmetic and copies ran while one was open for 13% -> 8% of each run, Pallas kernels for 19% -> 30%
where the time goes in v3:
time: 218 us; the launch traced here: 217 us
  waiting for transfers between devices  67.5 us (31%)
  Pallas kernels  66.5 us (31%)
  starting transfers between devices  43.7 us (20%)
  between operations  14.5 us (7%)
  other arithmetic  13.5 us (6%)
  local copies, waits for them, and re-layouts  10.8 us (5%)
    ppermute x16, waiting for transfers between devices, swap(): return lax.ppermute(value, axis, [(i, i ^ bit) for i in range(size)])  42.6 us
    all_to_all x5, waiting for transfers between devices, exchange(): return lax.all_to_all(value, AXES, split_axis=0, concat_axis=0, tiled=True)  23 us
    all_to_all x5, starting transfers between devices, exchange(): return lax.all_to_all(value, AXES, split_axis=0, concat_axis=0, tiled=True)  22.3 us
    ppermute x16, starting transfers between devices, swap(): return lax.ppermute(value, axis, [(i, i ^ bit) for i in range(size)])  21.4 us
    pallas_call x1, Pallas kernels, attend_back(): pl.pallas_call(attend_back_kernel, grid=(steps,), in_specs=[pl.BlockSpec(...  16.4 us
    pallas_call x1, Pallas kernels, attend(): pl.pallas_call(attend_kernel, grid=(steps,), in_specs=[by_row(HEAD), whol...  11.7 us
    pallas_call x1, Pallas kernels, weight_grads(): pl.pallas_call(functools.partial(weight_grads_kernel, in_tiles=in_tiles,...  11 us
    pallas_call x1, Pallas kernels, middle_part(): pl.pallas_call(middle_kernel, out_shape=[jax.ShapeDtypeStruct(shape, kind...  8.51 us
  transfers between devices with their start and end apart: 23, of which 13 were waited for; matrix products, arithmetic and copies ran while one was open for 8% of the time, Pallas kernels for 30%

profile of v3, /device:TPU:0, one launch (start us, length us, event | category | flops | bytes accessed | tf_op | source)
XLA Modules:
  0.0 216.6 jit_solution(15160669869642270045)
XLA Ops:
  7.2 1.6 pad_maximum_fusion.2
  8.9 1.0 constant_dynamic-slice_fusion
  9.9 4.1 %collective-permute-start.1 = (bf16[64,768]{1,0:T(8,128)(2,1)S(1)}, bf16[64,768]{1,0:T(8,128)(2,1)S(1)}, u32[]{:S(2)}, u32[]{:S(2)}) collective-permute-start(bf16[64,768]{1,0:T(8,128)(2,1)S(1)} %get-tuple-element.104), channel_id=1, source_target_pairs={{0,16},{4,20},{8,24},{12,28},{16,0},{20,4},{24,8},{28,12},{1,17},{... | collective-permute-start | bytes 294920 | tf_op jit(solution)/shard_map/ppermute | solution.py:256
  14.0 1.3 collective-permute-start.2
  15.6 1.1 reshape.683
  17.3 0.8 broadcast_in_dim.5
  18.1 5.2 %all-to-all-start = ((bf16[32,24,256]{2,1,0:T(8,128)(2,1)}), bf16[32,24,256]{2,1,0:T(8,128)(2,1)S(1)}, u32[]{:S(2)}, u32[]{:S(2)}) async-start(bf16[32,24,256]{2,1,0:T(8,128)(2,1)} %bitcast.25), calls=%async_computation | async-start | bytes 786432 | tf_op jit(solution)/shard_map/all_to_all | solution.py:309
  23.7 1.8 collective-permute-start.3
  25.5 1.5 collective-permute-start.5
  27.1 7.5 %collective-permute-done.3 = bf16[2,2,32,768]{3,2,1,0:T(8,128)(2,1)S(1)} collective-permute-done((bf16[2,2,32,768]{3,2,1,0:T(8,128)(2,1)S(1)}, bf16[2,2,32,768]{3,2,1,0:T(8,128)(2,1)S(1)}, u32[]{:S(2)}, u32[]{:S(2)}) %collective-permute-start.3) | collective-permute-done | bytes 196640 | tf_op jit(solution)/shard_map/ppermute | solution.py:256
  34.7 1.0 collective-permute-start.4
  35.7 0.9 collective-permute-start.6
  36.6 5.6 %multiply_sine_fusion = (f32[2048,128]{1,0:T(8,128)}, f32[2048,128]{1,0:T(8,128)}) fusion(f32[128]{0:T(128)S(1)} %fusion.35, f32[2048]{0:T(1024)S(1)} %fusion.23), kind=kLoop, calls=%fused_computation.3 | loop fusion | flops 262144 | bytes 2105856 | tf_op jit(solution)/shard_map/sin | solution.py:305
  42.3 7.6 %collective-permute-done.6 = bf16[2,2,2,32,768]{4,3,2,1,0:T(8,128)(2,1)S(1)} collective-permute-done((bf16[2,2,2,32,768]{4,3,2,1,0:T(8,128)(2,1)S(1)}, bf16[2,2,2,32,768]{4,3,2,1,0:T(8,128)(2,1)S(1)}, u32[]{:S(2)}, u32[]{:S(2)}) %collective-permute-start.6) | collective-permute-done | bytes 393248 | tf_op jit(solution)/shard_map/ppermute | solution.py:256
  50.7 0.8 reshape.706.gain
  51.5 2.3 %collective-permute-done.7.other = bf16[1024,768]{1,0:T(8,128)(2,1)S(1)} collective-permute-done((bf16[1024,768]{1,0:T(8,128)(2,1)S(1)}, bf16[1024,768]{1,0:T(8,128)(2,1)S(1)}, u32[]{:S(2)}, u32[]{:S(2)}) %collective-permute-start.7) | collective-permute-done | bytes 1572896 | tf_op jit(solution)/shard_map/ppermute | solution.py:256
  53.8 1.2 copy-done.5
  54.9 7.2 %project.1 = (bf16[2,1024,768]{2,1,0:T(8,128)(2,1)}, bf16[2,1024,64]{2,1,0:T(8,128)(2,1)}, bf16[2,1024,64]{2,1,0:T(8,128)(2,1)}, bf16[2,1024,64]{2,1,0:T(8,128)(2,1)}) custom-call(s32[1]{0:T(128)} %bitcast.core, bf16[1024,768]{1,0:T(8,128)(2,1)} %bitcast.91, bf16[1024,768]{1,0:T(8,128)(2,1)} %copy-done.5, f32[1,768]{1,0:T(1,128)} %reshape.706.gain, ...), custom_call_target="tpu_custom_call" | custom-call | tf_op jit(solution)/shard_map/project/pallas_call | solution.py:356
  62.1 11.7 %attend.1 = (bf16[2048,2048]{1,0:T(8,128)(2,1)}, f32[2048,64]{1,0:T(8,128)}, f32[2048,1]{1,0:T(8,128)}, bf16[16,2,32,128]{3,2,1,0:T(8,128)(2,1)}) custom-call(bf16[2048,64]{1,0:T(8,128)(2,1)} %bitcast.124, bf16[2048,64]{1,0:T(8,128)(2,1)} %bitcast.126, bf16[2048,64]{1,0:T(8,128)(2,1)} %bitcast.128), custom_call_target="tpu_custom_call" | custom-call | flops 4294967296 | bytes 8388608 | tf_op jit(solution)/shard_map/attend/pallas_call | solution.py:398
  73.8 4.7 %all-to-all-start.1 = ((bf16[32,32,128]{2,1,0:T(8,128)(2,1)}), bf16[32,32,128]{2,1,0:T(8,128)(2,1)S(1)}, u32[]{:S(2)}, u32[]{:S(2)}) async-start(bf16[32,32,128]{2,1,0:T(8,128)(2,1)} %bitcast.115), calls=%async_computation.1 | async-start | bytes 524288 | tf_op jit(solution)/shard_map/all_to_all | solution.py:309
  79.1 13.7 %all-to-all-done.1.got = bf16[32,32,128]{2,1,0:T(8,128)(2,1)S(1)} async-done(((bf16[32,32,128]{2,1,0:T(8,128)(2,1)}), bf16[32,32,128]{2,1,0:T(8,128)(2,1)S(1)}, u32[]{:S(2)}, u32[]{:S(2)}) %all-to-all-start.1) | async-done | bytes 262176 | tf_op jit(solution)/shard_map/all_to_all | solution.py:309
  92.8 1.9 all-gather.3.cloned.1.call-done.late
  94.7 8.5 %middle_part.1 = (bf16[128,768]{1,0:T(8,128)(2,1)}, bf16[32,32,128]{2,1,0:T(8,128)(2,1)}, bf16[128,6528]{1,0:T(8,128)(2,1)}, f32[128,768]{1,0:T(8,128)}) custom-call(bf16[32,32,128]{2,1,0:T(8,128)(2,1)} %copy-done.6, bf16[128,768]{1,0:T(8,128)(2,1)} %bitcast.97, bf16[768,4224]{1,0:T(8,128)(2,1)} %all-gather.3.cloned.1.call-done.late, ...), custom_call_target="tpu_custom_call" | custom-call | tf_op jit(solution)/shard_map/middle_part/pallas_call | solution.py:493
  103.5 2.8 %all-to-all-start.2 = ((bf16[32,32,128]{2,1,0:T(8,128)(2,1)}), bf16[32,32,128]{2,1,0:T(8,128)(2,1)S(1)}, u32[]{:S(2)}, u32[]{:S(2)}) async-start(bf16[32,32,128]{2,1,0:T(8,128)(2,1)} %get-tuple-element.55), calls=%async_computation.2 | async-start | bytes 524288 | tf_op jit(solution)/shard_map/all_to_all | solution.py:309
  107.0 1.2 copy-done
  108.2 11.0 %weight_grads.1 = (bf16[4,2,24,2304]{3,2,1,0:T(8,128)(2,1)}, bf16[4,2,24,2304]{3,2,1,0:T(8,128)(2,1)}, bf16[4,2,24,1920]{3,2,1,0:T(8,128)(2,1)}, bf16[4,2,24,1920]{3,2,1,0:T(8,128)(2,1)}) custom-call(s32[3]{0:T(128)} %pad_add_fusion.place, bf16[128,6528]{1,0:T(8,128)(2,1)} %get-tuple-element.56.hidden.attn.grad_out.right, ...), custom_call_target="tpu_custom_call" | custom-call | flops 1660944384 | bytes 9830400 | tf_op jit(solution)/shard_map/weight_grads/pallas_call | solution.py:554
  119.2 1.6 collective-permute-start.9
  120.8 1.5 collective-permute-start.10
  122.3 16.4 %attend_back.1 = (bf16[16,2,96,128]{3,2,1,0:T(8,128)(2,1)}, bf16[2048,128]{1,0:T(8,128)(2,1)}, bf16[2048,64]{1,0:T(8,128)(2,1)}) custom-call(bf16[16,2,32,128]{3,2,1,0:T(8,128)(2,1)} %bitcast.114, f32[2048,64]{1,0:T(8,128)} %get-tuple-element.62.attn32, f32[2048,1]{1,0:T(8,128)} %get-tuple-element.63.total, bf16[2048,2048]{1,0:T(8,128)(2,1)} %get-tuple-element.64.weights, ...), custom_call_target="tpu_custom_call" | custom-call | flops 15032385536 | bytes 8388608 | tf_op jit(solution)/shard_map/attend_back/pallas_call | solution.py:625
  138.7 2.2 %collective-permute-done.10 = bf16[2,2,2,24,1920]{4,3,2,1,0:T(8,128)(2,1)S(1)} collective-permute-done((bf16[2,2,2,24,1920]{4,3,2,1,0:T(8,128)(2,1)}, bf16[2,2,2,24,1920]{4,3,2,1,0:T(8,128)(2,1)S(1)}, u32[]{:S(2)}, u32[]{:S(2)}) %collective-permute-start.10) | collective-permute-done | bytes 737312 | tf_op jit(solution)/shard_map/ppermute | solution.py:256
  140.9 5.3 %collective-permute-done.9 = bf16[2,2,2,24,2304]{4,3,2,1,0:T(8,128)(2,1)S(1)} collective-permute-done((bf16[2,2,2,24,2304]{4,3,2,1,0:T(8,128)(2,1)}, bf16[2,2,2,24,2304]{4,3,2,1,0:T(8,128)(2,1)S(1)}, u32[]{:S(2)}, u32[]{:S(2)}) %collective-permute-start.9) | collective-permute-done | bytes 884768 | tf_op jit(solution)/shard_map/ppermute | solution.py:256
  146.2 6.1 %all-to-all-start.3 = ((bf16[32,96,128]{2,1,0:T(8,128)(2,1)}), bf16[32,96,128]{2,1,0:T(8,128)(2,1)S(1)}, u32[]{:S(2)}, u32[]{:S(2)}) async-start(bf16[32,96,128]{2,1,0:T(8,128)(2,1)} %bitcast.106), calls=%async_computation.3 | async-start | bytes 1572864 | tf_op jit(solution)/shard_map/all_to_all | solution.py:309
  152.6 1.8 collective-permute-start.11
  154.6 0.8 dynamic-slice_bitcast_fusion.1
  155.4 1.5 collective-permute-start.12
  156.9 5.3 %head_grads.1 = bf16[768,192]{1,0:T(8,128)(2,1)} custom-call(bf16[2048,768]{1,0:T(8,128)(2,1)} %bitcast.96, bf16[2048,128]{1,0:T(8,128)(2,1)} %get-tuple-element.70.both, bf16[2048,64]{1,0:T(8,128)(2,1)} %get-tuple-element.71.low), custom_call_target="tpu_custom_call" | custom-call | flops 603979776 | bytes 3932160 | tf_op jit(solution)/shard_map/head_grads/pallas_call | solution.py:679
  162.1 9.1 %collective-permute-done.12 = bf16[2,2,24,1920]{3,2,1,0:T(8,128)(2,1)} collective-permute-done((bf16[2,2,24,1920]{3,2,1,0:T(8,128)(2,1)}, bf16[2,2,24,1920]{3,2,1,0:T(8,128)(2,1)}, u32[]{:S(2)}, u32[]{:S(2)}) %collective-permute-start.12) | collective-permute-done | bytes 368672 | tf_op jit(solution)/shard_map/ppermute | solution.py:256
  171.9 2.8 %all-to-all-done.3.got = bf16[32,96,128]{2,1,0:T(8,128)(2,1)S(1)} async-done(((bf16[32,96,128]{2,1,0:T(8,128)(2,1)}), bf16[32,96,128]{2,1,0:T(8,128)(2,1)S(1)}, u32[]{:S(2)}, u32[]{:S(2)}) %all-to-all-start.3) | async-done | bytes 786464 | tf_op jit(solution)/shard_map/all_to_all | solution.py:309
  174.9 1.3 fusion.3
  177.0 2.8 %collective-permute-start.14 = (bf16[24,4224]{1,0:T(8,128)(2,1)S(1)}, bf16[24,4224]{1,0:T(8,128)(2,1)S(1)}, u32[]{:S(2)}, u32[]{:S(2)}) collective-permute-start(bf16[24,4224]{1,0:T(8,128)(2,1)S(1)} %pad_maximum_fusion.4), channel_id=1, source_target_pairs={{0,24},{4,28},{8,16},{12,20},{16,8},{20,12},{24,0},{28,4},{1,25},{... | collective-permute-start | bytes 608264 | tf_op jit(solution)/shard_map/ppermute | solution.py:256
  180.7 3.5 %all-to-all-start.4 = ((bf16[32,24,192]{2,1,0:T(8,128)(2,1)}), bf16[32,24,192]{2,1,0:T(8,128)(2,1)S(1)}, u32[]{:S(2)}, u32[]{:S(2)}) async-start(bf16[32,24,192]{2,1,0:T(8,128)(2,1)} %bitcast.49), calls=%async_computation.4 | async-start | bytes 786432 | tf_op jit(solution)/shard_map/all_to_all | solution.py:309
  184.2 4.6 %last_part.1 = bf16[128,768]{1,0:T(8,128)(2,1)} custom-call(bf16[32,96,128]{2,1,0:T(8,128)(2,1)} %copy-done.3, bf16[768,2304]{1,0:T(8,128)(2,1)} %all-gather.5.cloned.1.call-done.weight, bf16[128,768]{1,0:T(8,128)(2,1)} %bitcast.98, f32[1,768]{1,0:T(1,128)} %reshape.706.gain, f32[128,768]{1,0:T(8,128)} %get-tuple-element.78.grad_middle), custom_call_target="tpu_custom_call" | custom-call | tf_op jit(solution)/shard_map/last_part/pallas_call | solution.py:720
  188.7 5.1 %collective-permute-done.13 = bf16[24,4224]{1,0:T(8,128)(2,1)S(1)} collective-permute-done((bf16[24,4224]{1,0:T(8,128)(2,1)S(1)}, bf16[24,4224]{1,0:T(8,128)(2,1)S(1)}, u32[]{:S(2)}, u32[]{:S(2)}) %collective-permute-start.13) | collective-permute-done | bytes 202784 | tf_op jit(solution)/shard_map/ppermute | solution.py:256
  193.8 2.8 %collective-permute-done.15 = bf16[24,4224]{1,0:T(8,128)(2,1)S(1)} collective-permute-done((bf16[24,4224]{1,0:T(8,128)(2,1)S(1)}, bf16[24,4224]{1,0:T(8,128)(2,1)S(1)}, u32[]{:S(2)}, u32[]{:S(2)}) %collective-permute-start.15) | collective-permute-done | bytes 202784 | tf_op jit(solution)/shard_map/ppermute | solution.py:256
  196.7 0.8 multiply_reduce_fusion
  199.4 6.4 %all-to-all-done.4.got = bf16[32,24,192]{2,1,0:T(8,128)(2,1)S(1)} async-done(((bf16[32,24,192]{2,1,0:T(8,128)(2,1)}), bf16[32,24,192]{2,1,0:T(8,128)(2,1)S(1)}, u32[]{:S(2)}, u32[]{:S(2)}) %all-to-all-start.4) | async-done | bytes 294944 | tf_op jit(solution)/shard_map/all_to_all | solution.py:309
  206.5 1.9 collect.1
  208.4 1.3 reduce.2
  (85 shorter events, 9.3 us)
Async XLA Ops:
  7.2 9.9 %copy-start.13 = (bf16[24]{0:T(256)(128)(2,1)S(1)}, bf16[24]{0:T(256)(128)(2,1)}, u32[]{:S(2)}) copy-start(bf16[24]{0:T(256)(128)(2,1)} %param.9) | copy-start | bytes 148
  7.2 9.9 %copy-start.14 = (bf16[24]{0:T(256)(128)(2,1)S(1)}, bf16[24]{0:T(256)(128)(2,1)}, u32[]{:S(2)}) copy-start(bf16[24]{0:T(256)(128)(2,1)} %param.12) | copy-start | bytes 148
  7.2 87.5 %all-gather.3.cloned.1.call-start = ((), (), s32[]{:S(2)}) async-start(), calls=%async_computation.5 | async-start | bytes 6690816 | tf_op jit(solution)/shard_map/all_gather | solution.py:765
  9.9 13.5 %collective-permute-start.1 = (bf16[64,768]{1,0:T(8,128)(2,1)S(1)}, bf16[64,768]{1,0:T(8,128)(2,1)S(1)}, u32[]{:S(2)}, u32[]{:S(2)}) collective-permute-start(bf16[64,768]{1,0:T(8,128)(2,1)S(1)} %get-tuple-element.104), channel_id=1, source_target_pairs={{0,16},{4,20},{8,24},{12,28},{16,0},{20,4},{24,8},{28,12},{1,17},{... | collective-permute-start | bytes 294920 | tf_op jit(solution)/shard_map/ppermute | solution.py:256
  14.0 9.4 %collective-permute-start.2 = (bf16[64,768]{1,0:T(8,128)(2,1)S(1)}, bf16[64,768]{1,0:T(8,128)(2,1)S(1)}, u32[]{:S(2)}, u32[]{:S(2)}) collective-permute-start(bf16[64,768]{1,0:T(8,128)(2,1)S(1)} %get-tuple-element.104), channel_id=1, source_target_pairs={{0,24},{4,28},{8,16},{12,20},{16,8},{20,12},{24,0},{28,4},{1,25},{... | collective-permute-start | bytes 294920 | tf_op jit(solution)/shard_map/ppermute | solution.py:256
  15.4 8.0 %collective-permute-start = (bf16[64,768]{1,0:T(8,128)(2,1)S(1)}, bf16[64,768]{1,0:T(8,128)(2,1)S(1)}, u32[]{:S(2)}, u32[]{:S(2)}) collective-permute-start(bf16[64,768]{1,0:T(8,128)(2,1)S(1)} %bitcast.111), channel_id=1, source_target_pairs={{0,8},{4,12},{8,0},{12,4},{16,24},{20,28},{24,16},{28,20},{1,9},{5... | collective-permute-start | bytes 294920 | tf_op jit(solution)/shard_map/ppermute | solution.py:256
  18.1 32.2 %all-to-all-start = ((bf16[32,24,256]{2,1,0:T(8,128)(2,1)}), bf16[32,24,256]{2,1,0:T(8,128)(2,1)S(1)}, u32[]{:S(2)}, u32[]{:S(2)}) async-start(bf16[32,24,256]{2,1,0:T(8,128)(2,1)} %bitcast.25), calls=%async_computation | async-start | bytes 786432 | tf_op jit(solution)/shard_map/all_to_all | solution.py:309
  23.3 138.9 %all-gather.5.cloned.1.call-start = ((), (), s32[]{:S(2)}) async-start(), calls=%async_computation.6 | async-start | bytes 3649536 | tf_op jit(solution)/shard_map/all_gather | solution.py:817
  23.7 10.9 %collective-permute-start.3 = (bf16[2,2,32,768]{3,2,1,0:T(8,128)(2,1)S(1)}, bf16[2,2,32,768]{3,2,1,0:T(8,128)(2,1)S(1)}, u32[]{:S(2)}, u32[]{:S(2)}) collective-permute-start(bf16[2,2,32,768]{3,2,1,0:T(8,128)(2,1)S(1)} %get-tuple-element.93), channel_id=1, source_target_pairs={{0,4},{4,0},{8,12},{12,8},{16,20},{20,16},{24,28},{28,24},{1,5},{5... | collective-permute-start | bytes 589832 | tf_op jit(solution)/shard_map/ppermute | solution.py:256
  25.5 10.2 %collective-permute-start.5 = (bf16[2,2,32,768]{3,2,1,0:T(8,128)(2,1)S(1)}, bf16[2,2,32,768]{3,2,1,0:T(8,128)(2,1)S(1)}, u32[]{:S(2)}, u32[]{:S(2)}) collective-permute-start(bf16[2,2,32,768]{3,2,1,0:T(8,128)(2,1)S(1)} %get-tuple-element.96), channel_id=1, source_target_pairs={{0,2},{1,3},{2,0},{3,1},{4,6},{5,7},{6,4},{7,5},{8,10},{9,11},{10,... | collective-permute-start | bytes 589832 | tf_op jit(solution)/shard_map/ppermute | solution.py:256
  34.7 15.3 %collective-permute-start.4 = (bf16[2,2,2,32,768]{4,3,2,1,0:T(8,128)(2,1)S(1)}, bf16[2,2,2,32,768]{4,3,2,1,0:T(8,128)(2,1)S(1)}, u32[]{:S(2)}, u32[]{:S(2)}) collective-permute-start(bf16[2,2,2,32,768]{4,3,2,1,0:T(8,128)(2,1)S(1)} %maximum_select_fusion.4), channel_id=1, source_target_pairs={{0,2},{1,3},{2,0},{3,1},{4,6},{5,7},{6,4},{7,5},{8,10},{9,11},{10,... | collective-permute-start | bytes 1179656 | tf_op jit(solution)/shard_map/ppermute | solution.py:256
  35.7 14.2 %collective-permute-start.6 = (bf16[2,2,2,32,768]{4,3,2,1,0:T(8,128)(2,1)S(1)}, bf16[2,2,2,32,768]{4,3,2,1,0:T(8,128)(2,1)S(1)}, u32[]{:S(2)}, u32[]{:S(2)}) collective-permute-start(bf16[2,2,2,32,768]{4,3,2,1,0:T(8,128)(2,1)S(1)} %maximum_select_fusion.6), channel_id=1, source_target_pairs={{0,4},{4,0},{8,12},{12,8},{16,20},{20,16},{24,28},{28,24},{1,5},{5... | collective-permute-start | bytes 1179656 | tf_op jit(solution)/shard_map/ppermute | solution.py:256
  50.3 3.5 %copy-start.1 = (bf16[2,2,2,2,2,32,768]{6,5,4,3,2,1,0:T(8,128)(2,1)}, bf16[2,2,2,2,2,32,768]{6,5,4,3,2,1,0:T(8,128)(2,1)S(1)}, u32[]{:S(2)}) copy-start(bf16[2,2,2,2,2,32,768]{6,5,4,3,2,1,0:T(8,128)(2,1)S(1)} %pad_maximum_fusion) | copy-start | bytes 4718596
  50.3 3.5 %copy-start.2 = (bf16[32,24,256]{2,1,0:T(8,128)(2,1)}, bf16[32,24,256]{2,1,0:T(8,128)(2,1)S(1)}, u32[]{:S(2)}) copy-start(bf16[32,24,256]{2,1,0:T(8,128)(2,1)S(1)} %all-to-all-done) | copy-start | bytes 1179652
  50.3 3.5 %collective-permute-start.7 = (bf16[1024,768]{1,0:T(8,128)(2,1)S(1)}, bf16[1024,768]{1,0:T(8,128)(2,1)S(1)}, u32[]{:S(2)}, u32[]{:S(2)}) collective-permute-start(bf16[1024,768]{1,0:T(8,128)(2,1)S(1)} %bitcast.90), channel_id=1, source_target_pairs={{0,1},{1,0},{2,3},{3,2},{4,5},{5,4},{6,7},{7,6},{8,9},{9,8},{10,11... | collective-permute-start | bytes 4718600 | tf_op jit(solution)/shard_map/ppermute | solution.py:256
  53.8 1.2 copy-start.5
  73.8 19.0 %all-to-all-start.1 = ((bf16[32,32,128]{2,1,0:T(8,128)(2,1)}), bf16[32,32,128]{2,1,0:T(8,128)(2,1)S(1)}, u32[]{:S(2)}, u32[]{:S(2)}) async-start(bf16[32,32,128]{2,1,0:T(8,128)(2,1)} %bitcast.115), calls=%async_computation.1 | async-start | bytes 524288 | tf_op jit(solution)/shard_map/all_to_all | solution.py:309
  92.8 1.9 copy-start.6
  103.2 3.8 %collective-permute-start.8 = (bf16[128,6528]{1,0:T(8,128)(2,1)}, bf16[128,6528]{1,0:T(8,128)(2,1)S(1)}, u32[]{:S(2)}, u32[]{:S(2)}) collective-permute-start(bf16[128,6528]{1,0:T(8,128)(2,1)} %get-tuple-element.56.hidden.attn.grad_out.right), channel_id=1, source_target_pairs={{0,1},{1,0},{2,3},{3,2},{4,5},{5,4},{6,7},{7,6},{8,9},{9,8},{10,11... | collective-permute-start | bytes 5013512 | tf_op jit(solution)/shard_map/ppermute | solution.py:256
  103.5 15.7 %all-to-all-start.2 = ((bf16[32,32,128]{2,1,0:T(8,128)(2,1)}), bf16[32,32,128]{2,1,0:T(8,128)(2,1)S(1)}, u32[]{:S(2)}, u32[]{:S(2)}) async-start(bf16[32,32,128]{2,1,0:T(8,128)(2,1)} %get-tuple-element.55), calls=%async_computation.2 | async-start | bytes 524288 | tf_op jit(solution)/shard_map/all_to_all | solution.py:309
  107.0 1.2 copy-start
  119.2 3.1 %copy-start.12 = (bf16[32,32,128]{2,1,0:T(8,128)(2,1)}, bf16[32,32,128]{2,1,0:T(8,128)(2,1)S(1)}, u32[]{:S(2)}) copy-start(bf16[32,32,128]{2,1,0:T(8,128)(2,1)S(1)} %all-to-all-done.2) | copy-start | bytes 786436
  119.2 27.0 %collective-permute-start.9 = (bf16[2,2,2,24,2304]{4,3,2,1,0:T(8,128)(2,1)}, bf16[2,2,2,24,2304]{4,3,2,1,0:T(8,128)(2,1)S(1)}, u32[]{:S(2)}, u32[]{:S(2)}) collective-permute-start(bf16[2,2,2,24,2304]{4,3,2,1,0:T(8,128)(2,1)} %bitcast.122), channel_id=1, source_target_pairs={{0,4},{4,0},{8,12},{12,8},{16,20},{20,16},{24,28},{28,24},{1,5},{5... | collective-permute-start | bytes 2654216 | tf_op jit(solution)/shard_map/ppermute | solution.py:256
  120.8 20.0 %collective-permute-start.10 = (bf16[2,2,2,24,1920]{4,3,2,1,0:T(8,128)(2,1)}, bf16[2,2,2,24,1920]{4,3,2,1,0:T(8,128)(2,1)S(1)}, u32[]{:S(2)}, u32[]{:S(2)}) collective-permute-start(bf16[2,2,2,24,1920]{4,3,2,1,0:T(8,128)(2,1)} %bitcast.123), channel_id=1, source_target_pairs={{0,2},{1,3},{2,0},{3,1},{4,6},{5,7},{6,4},{7,5},{8,10},{9,11},{10,... | collective-permute-start | bytes 2211848 | tf_op jit(solution)/shard_map/ppermute | solution.py:256
  138.7 13.6 %copy-start.7 = (bf16[4,2,24,2304]{3,2,1,0:T(8,128)(2,1)S(1)}, bf16[4,2,24,2304]{3,2,1,0:T(8,128)(2,1)}, u32[]{:S(2)}) copy-start(bf16[4,2,24,2304]{3,2,1,0:T(8,128)(2,1)} %get-tuple-element.72) | copy-start | bytes 2654212
  140.9 5.3 %copy-start.9 = (bf16[2,2,2,24,1920]{4,3,2,1,0:T(8,128)(2,1)}, bf16[2,2,2,24,1920]{4,3,2,1,0:T(8,128)(2,1)S(1)}, u32[]{:S(2)}) copy-start(bf16[2,2,2,24,1920]{4,3,2,1,0:T(8,128)(2,1)S(1)} %collective-permute-done.10) | copy-start | bytes 2211844
  146.2 28.5 %all-to-all-start.3 = ((bf16[32,96,128]{2,1,0:T(8,128)(2,1)}), bf16[32,96,128]{2,1,0:T(8,128)(2,1)S(1)}, u32[]{:S(2)}, u32[]{:S(2)}) async-start(bf16[32,96,128]{2,1,0:T(8,128)(2,1)} %bitcast.106), calls=%async_computation.3 | async-start | bytes 1572864 | tf_op jit(solution)/shard_map/all_to_all | solution.py:309
  152.3 2.1 copy-start.8
  152.3 2.1 copy-start.10
  152.6 19.3 %collective-permute-start.11 = (bf16[2,2,24,2304]{3,2,1,0:T(8,128)(2,1)S(1)}, bf16[2,2,24,2304]{3,2,1,0:T(8,128)(2,1)S(1)}, u32[]{:S(2)}, u32[]{:S(2)}) collective-permute-start(bf16[2,2,24,2304]{3,2,1,0:T(8,128)(2,1)S(1)} %dynamic-slice_bitcast_fusion), channel_id=1, source_target_pairs={{0,2},{1,3},{2,0},{3,1},{4,6},{5,7},{6,4},{7,5},{8,10},{9,11},{10,... | collective-permute-start | bytes 1327112 | tf_op jit(solution)/shard_map/ppermute | solution.py:256
  155.4 15.8 %collective-permute-start.12 = (bf16[2,2,24,1920]{3,2,1,0:T(8,128)(2,1)}, bf16[2,2,24,1920]{3,2,1,0:T(8,128)(2,1)}, u32[]{:S(2)}, u32[]{:S(2)}) collective-permute-start(bf16[2,2,24,1920]{3,2,1,0:T(8,128)(2,1)} %dynamic-slice_bitcast_fusion.1), channel_id=1, source_target_pairs={{0,4},{4,0},{8,12},{12,8},{16,20},{20,16},{24,28},{28,24},{1,5},{5... | collective-permute-start | bytes 1105928 | tf_op jit(solution)/shard_map/ppermute | solution.py:256
  174.8 1.5 copy-start.3
  176.3 17.6 %collective-permute-start.13 = (bf16[24,4224]{1,0:T(8,128)(2,1)S(1)}, bf16[24,4224]{1,0:T(8,128)(2,1)S(1)}, u32[]{:S(2)}, u32[]{:S(2)}) collective-permute-start(bf16[24,4224]{1,0:T(8,128)(2,1)S(1)} %pad_maximum_fusion.3), channel_id=1, source_target_pairs={{0,16},{4,20},{8,24},{12,28},{16,0},{20,4},{24,8},{28,12},{1,17},{... | collective-permute-start | bytes 608264 | tf_op jit(solution)/shard_map/ppermute | solution.py:256
  177.0 16.8 %collective-permute-start.14 = (bf16[24,4224]{1,0:T(8,128)(2,1)S(1)}, bf16[24,4224]{1,0:T(8,128)(2,1)S(1)}, u32[]{:S(2)}, u32[]{:S(2)}) collective-permute-start(bf16[24,4224]{1,0:T(8,128)(2,1)S(1)} %pad_maximum_fusion.4), channel_id=1, source_target_pairs={{0,24},{4,28},{8,16},{12,20},{16,8},{20,12},{24,0},{28,4},{1,25},{... | collective-permute-start | bytes 608264 | tf_op jit(solution)/shard_map/ppermute | solution.py:256
  179.9 16.8 %collective-permute-start.15 = (bf16[24,4224]{1,0:T(8,128)(2,1)S(1)}, bf16[24,4224]{1,0:T(8,128)(2,1)S(1)}, u32[]{:S(2)}, u32[]{:S(2)}) collective-permute-start(bf16[24,4224]{1,0:T(8,128)(2,1)S(1)} %pad_maximum_fusion.5), channel_id=1, source_target_pairs={{0,8},{4,12},{8,0},{12,4},{16,24},{20,28},{24,16},{28,20},{1,9},{5... | collective-permute-start | bytes 608264 | tf_op jit(solution)/shard_map/ppermute | solution.py:256
  180.7 25.1 %all-to-all-start.4 = ((bf16[32,24,192]{2,1,0:T(8,128)(2,1)}), bf16[32,24,192]{2,1,0:T(8,128)(2,1)S(1)}, u32[]{:S(2)}, u32[]{:S(2)}) async-start(bf16[32,24,192]{2,1,0:T(8,128)(2,1)} %bitcast.49), calls=%async_computation.4 | async-start | bytes 786432 | tf_op jit(solution)/shard_map/all_to_all | solution.py:309
  184.2 12.5 %copy-start.11 = (bf16[24,2304]{1,0:T(8,128)(2,1)S(1)}, bf16[24,2304]{1,0:T(8,128)(2,1)}, u32[]{:S(2)}) copy-start(bf16[24,2304]{1,0:T(8,128)(2,1)} %param.13) | copy-start | bytes 331780
  205.8 0.7 copy-start.4
Sparse Core Ops, SparseCore 0:
  11.4 83.2 all-gather.2
  97.6 63.0 all-gather.4

commit v4 on v3

--- a/solution.py
+++ b/solution.py
@@ -247,8 +247,13 @@
 BLOCK = 256
 LANES = 128
 TILE = 384
+SENT = 136
 BY_COLUMN = (((1,), (1,)), ((), ()))
 BY_ROW = (((0,), (0,)), ((), ()))
+
+
+def pick(value, index):
+    return lax.dynamic_index_in_dim(value, index, 0, keepdims=False)
 
 
 def swap(value, axis, bit):
@@ -498,83 +503,92 @@
 
 
 def weight_grads_kernel(
-    place, hidden, attn, grad_out, right, hidden_too, attn_too, grad_out_too, right_too,
-    keep_a, give_a, keep_b, give_b, total, *, in_tiles, attn_tiles
+    place, acts, acts_too, keep_a, give_a, keep_b, give_b, own_c, give_c, total, turned, *,
+    width, hidden_units
 ):
-    tile = pl.program_id(0)
-    x, y, core = place[0], place[1], place[2]
-
-    def multiply(left, left_too):
-        product = lax.dot_general(
-            left[...], right[...], BY_ROW, preferred_element_type=F32
-        ) + lax.dot_general(left_too[...], right_too[...], BY_ROW, preferred_element_type=F32)
+    x, y, core, z = place[0], place[1], place[2], place[3]
+    rows = acts.shape[0]
+    joint = 3 * width
+    active = joint + 2 * hidden_units
+    branch = active + hidden_units
+
+    def turn_rows(i):
+        columns = slice(i * width, (i + 1) * width)
+        turned[:, :rows] = jnp.transpose(acts[:, columns])
+        turned[:, rows:] = jnp.transpose(acts_too[:, columns])
+
+    def multiply(start):
+        right = jnp.concatenate(
+            [acts[:, start : start + TILE], acts_too[:, start : start + TILE]], axis=0
+        )
+        product = jnp.dot(turned[...], right, preferred_element_type=F32)
         total[...] = product.reshape(total.shape)
 
-    def write_b():
-        keep_b[...] = total[:, :, y, core].astype(BF)
-        give_b[...] = total[:, :, 1 - y, core].astype(BF)
-
-    @pl.when(tile < in_tiles)
-    def _():
-        multiply(hidden, hidden_too)
-        keep_a[...] = total[:, x, :, core].astype(BF)
-        give_a[...] = total[:, 1 - x, :, core].astype(BF)
-
-    @pl.when((tile >= in_tiles) & (tile < in_tiles + attn_tiles))
-    def _():
-        multiply(attn, attn_too)
-        write_b()
-
-    @pl.when(tile >= in_tiles + attn_tiles)
-    def _():
-        multiply(grad_out, grad_out_too)
-        write_b()
+    def write_b(i):
+        columns = slice(i * TILE, (i + 1) * TILE)
+        keep_b[..., columns] = total[:, :, y, core].astype(BF)
+        give_b[..., columns] = total[:, :, 1 - y, core].astype(BF)
+
+    turn_rows(0)
+    for i in range(width // TILE):
+        columns = slice(i * TILE, (i + 1) * TILE)
+        multiply(branch + i * TILE)
+        own_c[..., columns] = total[z, :, :, core].astype(BF)
+        for k in (1, 2, 3):
+            other = z + k - 2 * ((z % 2) * (k % 2) + (z // 2) * (k // 2) * 2)
+            give_c[k - 1, ..., columns] = total[other, :, :, core].astype(BF)
+    turn_rows(1)
+    tiles_a = keep_a.shape[-1] // TILE
+    for i in range(2 * hidden_units // TILE):
+        columns = slice(i * TILE, (i + 1) * TILE)
+        multiply(joint + i * TILE)
+        if i < tiles_a:
+            keep_a[..., columns] = total[:, x, :, core].astype(BF)
+            give_a[..., columns] = total[:, 1 - x, :, core].astype(BF)
+        else:
+            write_b(i - tiles_a)
+    turn_rows(2)
+    for i in range(hidden_units // TILE):
+        multiply(active + i * TILE)
+        write_b(2 * hidden_units // TILE - tiles_a + i)
 
 
 def weight_grads(place, acts, acts_too, width, hidden_units, rows_here):
     rows = acts.shape[0]
-    in_tiles, attn_tiles = 2 * hidden_units // TILE, width // TILE
-    out_tiles = hidden_units // TILE
-    first = 3 * width // TILE
-    last = first + in_tiles + out_tiles
-    whole = lambda i: pl.BlockSpec((rows, width), lambda t: (0, i))
-
-    def source(t):
-        rest = t - in_tiles - attn_tiles
-        late = jnp.where(rest < 0, last + t - in_tiles, first + in_tiles + rest)
-        return 0, jnp.where(t < in_tiles, first + t, late)
-
-    sides = [whole(1), whole(0), whole(2), pl.BlockSpec((rows, TILE), source)]
     zs = width // (8 * rows_here)
-    block = (zs, 2, rows_here, TILE)
-    out_a = pl.BlockSpec(block, lambda t: (0, 0, 0, jnp.minimum(t, in_tiles - 1)))
-    out_b = pl.BlockSpec(block, lambda t: (0, 0, 0, jnp.maximum(t - in_tiles, 0)))
-    shape = lambda tiles: jax.ShapeDtypeStruct((zs, 2, rows_here, tiles * TILE), BF)
-    tiles = in_tiles + attn_tiles + out_tiles
+    columns = 3 * hidden_units + width
+    columns_a = 5 * (2 * hidden_units // TILE) // 6 * TILE
+    columns_b = 3 * hidden_units - columns_a
+    full = lambda *dims: jax.ShapeDtypeStruct(dims, BF)
     return pl.pallas_call(
-        functools.partial(weight_grads_kernel, in_tiles=in_tiles, attn_tiles=attn_tiles),
-        grid=(tiles,),
-        in_specs=[smem()] + sides + sides,
-        out_specs=[out_a, out_a, out_b, out_b],
-        out_shape=[shape(in_tiles)] * 2 + [shape(attn_tiles + out_tiles)] * 2,
-        scratch_shapes=[pltpu.VMEM((zs, 2, 2, 2, rows_here, TILE), F32)],
+        functools.partial(weight_grads_kernel, width=width, hidden_units=hidden_units),
+        in_specs=[smem()] + [pl.BlockSpec(memory_space=pltpu.VMEM)] * 2,
+        out_shape=[full(zs, 2, rows_here, columns_a)] * 2
+        + [full(zs, 2, rows_here, columns_b)] * 2
+        + [full(2, 2, rows_here, width), full(3, 2, 2, rows_here, width)],
+        scratch_shapes=[
+            pltpu.VMEM((zs, 2, 2, 2, rows_here, TILE), F32),
+            pltpu.VMEM((width, 2 * rows), BF),
+        ],
         cost_estimate=pl.CostEstimate(
-            flops=4 * rows * width * tiles * TILE,
-            bytes_accessed=4 * acts.size + 2 * width * tiles * TILE,
+            flops=4 * rows * width * columns,
+            bytes_accessed=4 * acts.size + 2 * width * columns,
             transcendentals=0,
         ),
         name="weight_grads",
-    )(place, *[acts] * 4, *[acts_too] * 4)
+    )(place, acts, acts_too)
 
 
 def attend_back_kernel(
-    got, attn32, total, weights, queries, key_rows, value_rows, cosine, sine, send, grad_both,
-    grad_low, grad_query, grad_key, grad_value
+    got, attn32, total, weights, queries, key_rows, value_rows, cosine, sine, hidden, send,
+    grad_query, grad_key, grad_value, held, copied
 ):
     step = pl.program_id(0)
+    copy = pltpu.make_async_copy(hidden, held, copied)
 
     @pl.when(step == 0)
     def _():
+        copy.start()
         grad_key[...] = jnp.zeros_like(grad_key)
         grad_value[...] = jnp.zeros_like(grad_value)
 
@@ -606,22 +620,33 @@
         length = grad_key.shape[0]
         both = side_by_side(grad_query[...], grad_key[...])
         both = (both * cosine[...] - turn(both) * sine[...]).astype(BF)
-        grad_both[...] = both
         low = grad_value[...].astype(BF)
-        grad_low[...] = low
+        copy.wait()
+        head_grad = jnp.transpose(
+            lax.dot_general(
+                side_by_side(both, low), held[...], BY_ROW, preferred_element_type=F32
+            )
+        )
+        for i in range(length // 64):
+            rows = head_grad[24 * i : 24 * i + 24].astype(BF)
+            send[i // 2, i % 2, 96:120] = rows[:, :LANES]
+            send[i // 2, i % 2, 120:136, :HEAD] = rows[:16, LANES:]
+            send[i // 2, i % 2, 120:128, HEAD:] = rows[16:, LANES:]
         for i in range(length // 64):
             core, pair = i // (length // 128), i % (length // 128)
             rows = low[64 * i : 64 * i + 64]
             send[pair, core, :64] = both[64 * i : 64 * i + 64]
-            send[pair, core, 64:] = side_by_side(rows[:32], rows[32:])
-
-
-def attend_back(got, attn32, total, weights, queries, key_rows, value_rows, cosine, sine):
+            send[pair, core, 64:96] = side_by_side(rows[:32], rows[32:])
+
+
+def attend_back(
+    got, attn32, total, weights, queries, key_rows, value_rows, cosine, sine, hidden
+):
     length = queries.shape[0]
     steps = length // BLOCK
     by_row = lambda columns: pl.BlockSpec((BLOCK, columns), lambda i: (i, 0))
     whole = lambda *shape: pl.BlockSpec(shape, lambda i: (0,) * len(shape))
-    send = (length // 128, 2, 96, LANES)
+    send = (length // 128, 2, SENT, LANES)
     return pl.pallas_call(
         attend_back_kernel,
         grid=(steps,),
@@ -637,75 +662,38 @@
             whole(length, HEAD),
             whole(length, LANES),
             whole(length, LANES),
+            pl.BlockSpec(memory_space=pl.ANY),
         ],
-        out_specs=[whole(*send), whole(length, LANES), whole(length, HEAD)],
-        out_shape=[
-            jax.ShapeDtypeStruct(send, BF),
-            jax.ShapeDtypeStruct((length, LANES), BF),
-            jax.ShapeDtypeStruct((length, HEAD), BF),
-        ],
-        scratch_shapes=[pltpu.VMEM((length, HEAD), F32)] * 3,
+        out_specs=whole(*send),
+        out_shape=jax.ShapeDtypeStruct(send, BF),
+        scratch_shapes=[pltpu.VMEM((length, HEAD), F32)] * 3
+        + [pltpu.VMEM(hidden.shape, BF), pltpu.SemaphoreType.DMA],
         cost_estimate=pl.CostEstimate(
             flops=14 * length * length * HEAD * 4,
             bytes_accessed=2 * length * length,
             transcendentals=0,
         ),
         name="attend_back",
-    )(got, attn32, total, weights, queries, key_rows, value_rows, cosine, sine)
-
-
-def head_grads_kernel(hidden, both, low, result, total):
-    step = pl.program_id(0)
-
-    @pl.when(step == 0)
-    def _():
-        total[...] = jnp.zeros_like(total)
-
-    total[:, :LANES] += lax.dot_general(
-        hidden[...], both[...], BY_ROW, preferred_element_type=F32
-    )
-    total[:, LANES:] += lax.dot_general(
-        hidden[...], low[...], BY_ROW, preferred_element_type=F32
-    )
-
-    @pl.when(step == pl.num_programs(0) - 1)
-    def _():
-        result[...] = total[...].astype(BF)
-
-
-def head_grads(hidden, both, low):
-    length, width = hidden.shape
-    by_row = lambda columns: pl.BlockSpec((2 * BLOCK, columns), lambda i: (i, 0))
-    return pl.pallas_call(
-        head_grads_kernel,
-        grid=(length // (2 * BLOCK),),
-        in_specs=[by_row(width), by_row(LANES), by_row(HEAD)],
-        out_specs=pl.BlockSpec((width, 3 * HEAD), lambda i: (0, 0)),
-        out_shape=jax.ShapeDtypeStruct((width, 3 * HEAD), BF),
-        scratch_shapes=[pltpu.VMEM((width, 3 * HEAD), F32)],
-        cost_estimate=pl.CostEstimate(
-            flops=6 * HEAD * length * width,
-            bytes_accessed=2 * length * (width + 3 * HEAD),
-            transcendentals=0,
-        ),
-        name="head_grads",
-    )(hidden, both, low)
-
-
-def last_kernel(got, weight, tokens, gain, grad_middle, result, grads):
+    )(got, attn32, total, weights, queries, key_rows, value_rows, cosine, sine, hidden)
+
+
+def last_kernel(
+    got, weight, tokens, gain, grad_middle, own_weight, own_gain, result, grad_weight, gain_grad,
+    grads
+):
     width = tokens.shape[1]
+    place = lambda j, h: slice(j * width + h * HEAD, j * width + h * HEAD + LANES)
     for s in range(2):
         for h in range(0, HEADS, 2):
             left, right = got[owner_slot(s, h)], got[owner_slot(s, h + 1)]
-            top, end = slice(64 * s, 64 * s + 64), slice(64 * s + 64, 64 * s + 128)
-            place = lambda j: slice(j * width + h * HEAD, j * width + h * HEAD + LANES)
-            grads[top, place(0)] = side_by_side(left[:64, :HEAD], right[:64, :HEAD])
-            grads[top, place(1)] = side_by_side(left[:64, HEAD:], right[:64, HEAD:])
-            grads[64 * s : 64 * s + 32, place(2)] = side_by_side(
-                left[64:, :HEAD], right[64:, :HEAD]
+            top = slice(64 * s, 64 * s + 64)
+            grads[top, place(0, h)] = side_by_side(left[:64, :HEAD], right[:64, :HEAD])
+            grads[top, place(1, h)] = side_by_side(left[:64, HEAD:], right[:64, HEAD:])
+            grads[64 * s : 64 * s + 32, place(2, h)] = side_by_side(
+                left[64:96, :HEAD], right[64:96, :HEAD]
             )
-            grads[64 * s + 32 : 64 * s + 64, place(2)] = side_by_side(
-                left[64:, HEAD:], right[64:, HEAD:]
+            grads[64 * s + 32 : 64 * s + 64, place(2, h)] = side_by_side(
+                left[64:96, HEAD:], right[64:96, HEAD:]
             )
     grad_hidden = lax.dot_general(
         grads[...], weight[...], BY_COLUMN, preferred_element_type=F32
@@ -715,39 +703,34 @@
         grad_middle[...] + norm_back(grad_hidden * gain[...], normed, inverse)
     ).astype(BF)
 
-
-def last_part(got, weight, tokens, gain, grad_middle):
+    def both(head, rows):
+        return (
+            got[owner_slot(0, head), rows].astype(F32) + got[owner_slot(1, head), rows].astype(F32)
+        )
+
+    for h in range(0, HEADS, 2):
+        left, right = both(h, slice(96, 120)), both(h + 1, slice(96, 120))
+        grad_weight[:, place(0, h)] = side_by_side(left[:, :HEAD], right[:, :HEAD])
+        grad_weight[:, place(1, h)] = side_by_side(left[:, HEAD:], right[:, HEAD:])
+        left, right = both(h, slice(120, 136)), both(h + 1, slice(120, 136))
+        grad_weight[:16, place(2, h)] = side_by_side(left[:, :HEAD], right[:, :HEAD])
+        grad_weight[16:, place(2, h)] = side_by_side(left[:8, HEAD:], right[:8, HEAD:])
+    sums = jnp.sum(grad_weight[...] * own_weight[...].astype(F32), axis=1, keepdims=True)
+    sums = jnp.transpose(jnp.broadcast_to(sums, (sums.shape[0], LANES)))[:8]
+    gain_grad[...] = sums / own_gain[...]
+
+
+def last_part(got, weight, tokens, gain, grad_middle, own_weight, own_gain):
     return pl.pallas_call(
         last_kernel,
-        out_shape=jax.ShapeDtypeStruct(tokens.shape, BF),
+        out_shape=[
+            jax.ShapeDtypeStruct(tokens.shape, BF),
+            jax.ShapeDtypeStruct(own_weight.shape, F32),
+            jax.ShapeDtypeStruct((8, own_weight.shape[0]), F32),
+        ],
         scratch_shapes=[pltpu.VMEM((tokens.shape[0], weight.shape[1]), BF)],
         name="last_part",
-    )(got, weight, tokens, gain, grad_middle)
-
-
-def collect_kernel(got, weight, gain, result, gain_grad):
-    width = result.shape[1] // 3
-    for h in range(0, HEADS, 2):
-        left = got[owner_slot(0, h)].astype(F32) + got[owner_slot(1, h)].astype(F32)
-        right = got[owner_slot(0, h + 1)].astype(F32) + got[owner_slot(1, h + 1)].astype(F32)
-        for j in range(3):
-            columns = slice(j * HEAD, (j + 1) * HEAD)
-            place = slice(j * width + h * HEAD, j * width + h * HEAD + LANES)
-            result[:, place] = side_by_side(left[:, columns], right[:, columns])
-    product = result[...] * weight[...].astype(F32)
-    gain_grad[...] = jnp.sum(product, axis=1, keepdims=True) / gain[...]
-
-
-def collect(got, weight, gain):
-    rows, columns = weight.shape
-    return pl.pallas_call(
-        collect_kernel,
-        out_shape=[
-            jax.ShapeDtypeStruct((rows, columns), F32),
-            jax.ShapeDtypeStruct((rows, 1), F32),
-        ],
-        name="collect",
-    )(got, weight, gain)
+    )(got, weight, tokens, gain, grad_middle, own_weight, own_gain)
 
 
 def owner_body(
@@ -759,8 +742,9 @@
     rows = sequences * per_device
     length = per_device * 32
     core = my_bit("ulysses", 1).astype(jnp.int32).reshape(1)
-    place = jnp.stack([my_bit("blk", 1), my_bit("ulysses", 2), my_bit("ulysses", 1)])
-    place = place.astype(jnp.int32)
+    x, y = my_bit("blk", 1), my_bit("ulysses", 2)
+    z = lax.axis_index("blk") // 2
+    place = jnp.stack([x, y, my_bit("ulysses", 1), z]).astype(jnp.int32)
     late = jnp.concatenate([in_weight, attn_out_weight, jnp.transpose(out_weight)], axis=1)
     late_full = lax.all_gather(late, AXES, axis=0, tiled=True)
     by_head = qkv_weight.reshape(rows_here, 3, HEADS, HEAD).transpose(2, 0, 1, 3)
@@ -799,11 +783,13 @@
     acts_too = swap(acts, "ulysses", 1)
     parts = weight_grads(place, acts, acts_too, model_width, hidden_units, rows_here)
     got, parts = lax.optimization_barrier((got, parts))
+    *parts, own_c, give_c = parts
     keep_a, give_a, keep_b, give_b = (
         part.reshape(2, 2, *part.shape[1:]) for part in parts
     )
     came_a, came_b = swap(give_a, "blk", 1), swap(give_b, "ulysses", 2)
-    send, grad_both, grad_low = attend_back(
+    came_c = [swap(give_c[k - 1], "blk", 2 * k) for k in (1, 2, 3)]
+    send = attend_back(
         got.reshape(length // 128, 2, 32, LANES),
         attn32,
         row_total,
@@ -813,45 +799,55 @@
         value_rows,
         cosine,
         sine,
+        hidden_one.reshape(length, model_width),
     )
     qkv_full = lax.all_gather(qkv_weight, AXES, axis=0, tiled=True)
-    send, came_a, came_b = lax.optimization_barrier((send, came_a, came_b))
-    got = exchange(send.reshape(32, 96, LANES))
+    send, came_a, came_b, came_c = lax.optimization_barrier((send, came_a, came_b, came_c))
+    got = exchange(send.reshape(32, SENT, LANES))
     keep_a, give_a = halve(keep_a, came_a, "ulysses", 2, 2)
     keep_b, give_b = halve(keep_b, came_b, "blk", 1, 2)
     came_a, came_b = swap(give_a, "ulysses", 2), swap(give_b, "blk", 1)
-    head_grad = head_grads(hidden_one.reshape(length, model_width), grad_both, grad_low)
-    got, head_grad, came_a, came_b, qkv_full = lax.optimization_barrier(
-        (got, head_grad, came_a, came_b, qkv_full)
-    )
-    got_grads = exchange(head_grad.reshape(32, rows_here, 3 * HEAD))
+    total_c = own_c.astype(F32)
+    for part in came_c:
+        total_c = total_c + part.astype(F32)
+    total_c = total_c.astype(BF).reshape(4, rows_here, model_width)
+    side = x * 2 + y
+    shard_attn = [pick(total_c, side)]
+    shard_attn.append(swap(pick(total_c, side ^ 2), "blk", 1))
+    shard_attn.append(swap(pick(total_c, side ^ 1), "ulysses", 2))
+    shard_attn.append(swap(pick(total_c, side ^ 3), AXES, 6))
+    came_a, came_b, qkv_full = lax.optimization_barrier((came_a, came_b, qkv_full))
     total = [
         (keep.astype(F32) + came.astype(F32)).astype(BF).reshape(4, rows_here, -1)
         for keep, came in ((keep_a, came_a), (keep_b, came_b))
     ]
-    z = lax.axis_index("blk") // 2
 
     def rows_of(owner):
-        return jnp.concatenate(
-            [lax.dynamic_index_in_dim(part, owner, 0, keepdims=False) for part in total], axis=1
-        )
-
-    shards = rows_of(z).astype(F32)
-    for step in (2, 3, 1):
-        shards = shards + swap(rows_of(z ^ step), "blk", 2 * step).astype(F32)
-    input_grad = last_part(got, qkv_full, flat_tokens, gain_one, grad_middle)
+        return jnp.concatenate([pick(part, owner) for part in total], axis=1)
+
+    shards = [rows_of(z)] + [swap(rows_of(z ^ k), "blk", 2 * k) for k in (2, 3, 1)]
+    last = last_part(
+        got,
+        qkv_full,
+        flat_tokens,
+        gain_one,
+        grad_middle,
+        qkv_weight,
+        attn_gain.astype(F32).reshape(1, rows_here),
+    )
+    (input_grad, shard_qkv, shard_one), shards, shard_attn = lax.optimization_barrier(
+        (last, shards, shard_attn)
+    )
     input_grad = input_grad.reshape(sequences, per_device, model_width)
-    shard_qkv, shard_one = collect(
-        got_grads, qkv_weight, attn_gain.astype(F32).reshape(rows_here, 1)
-    )
+    shard_attn = sum(part.astype(F32) for part in shard_attn)
+    shards = sum(part.astype(F32) for part in shards)
     shard_in = shards[:, : 2 * hidden_units]
-    shard_attn = shards[:, 2 * hidden_units : 2 * hidden_units + model_width]
-    shard_out = jnp.transpose(shards[:, 2 * hidden_units + model_width :])
+    shard_out = jnp.transpose(shards[:, 2 * hidden_units :])
     shard_two = jnp.sum(shard_in * in_weight.astype(F32), axis=1) / mlp_gain.astype(F32)
     return (
         layer_output.reshape(sequences, per_device, model_width),
         input_grad,
-        shard_one.reshape(rows_here),
+        shard_one[0],
         shard_qkv,
         shard_attn,
         shard_two,

time: 218 us -> 212 us (0.972)
  Pallas kernels: 66.5 us -> 55.3 us
  waiting for transfers between devices: 67.5 us -> 71.5 us
    ppermute x16 -> x22, waiting for transfers between devices: 42.6 us -> 18.4 us  [swap(): return lax.ppermute(value, axis, [(i, i ^ bit) for i in range(size)])]
    all_gather x1, waiting for transfers between devices: 0.01 us -> 19.6 us  [owner_body(): qkv_full = lax.all_gather(qkv_weight, AXES, axis=0, tiled=True)]
    pallas_call x4 -> x2, Pallas kernels: 22.7 us -> 10.8 us  [the longest x1 6.07 us: weight_grads(): pl.pallas_call(functools.partial(weight_grads_kernel, width=width, hidden...]
    all_to_all x5 -> x4, waiting for transfers between devices: 23 us -> 31.6 us  [exchange(): return lax.all_to_all(value, AXES, split_axis=0, concat_axis=0, tiled=True)]
    all_to_all x5 -> x4, starting transfers between devices: 22.3 us -> 15.3 us  [exchange(): return lax.all_to_all(value, AXES, split_axis=0, concat_axis=0, tiled=True)]
    ppermute x16 -> x22, starting transfers between devices: 21.4 us -> 28.1 us  [swap(): return lax.ppermute(value, axis, [(i, i ^ bit) for i in range(size)])]
    squeeze x2 -> x5, local copies, waits for them, and re-layouts: 0.11 us -> 2.39 us  [the longest x1 1.2 us: owner_body(): shard_one[0]]
  transfers between devices with their start and end apart: 23 -> 28, of which waited for: 13 -> 9; matrix products, arithmetic and copies ran while one was open for 8% -> 7% of each run, Pallas kernels for 30% -> 26%
where the time goes in v4:
time: 212 us; the launch traced here: 211 us
  waiting for transfers between devices  71.5 us (34%)
  Pallas kernels  55.3 us (26%)
  starting transfers between devices  43.5 us (21%)
  between operations  14.7 us (7%)
  other arithmetic  13.9 us (7%)
  local copies, waits for them, and re-layouts  12 us (6%)
    all_to_all x4, waiting for transfers between devices, exchange(): return lax.all_to_all(value, AXES, split_axis=0, concat_axis=0, tiled=True)  31.6 us
    ppermute x22, starting transfers between devices, swap(): return lax.ppermute(value, axis, [(i, i ^ bit) for i in range(size)])  28.1 us
    all_gather x1, waiting for transfers between devices, owner_body(): qkv_full = lax.all_gather(qkv_weight, AXES, axis=0, tiled=True)  19.6 us
    ppermute x22, waiting for transfers between devices, swap(): return lax.ppermute(value, axis, [(i, i ^ bit) for i in range(size)])  18.4 us
    pallas_call x1, Pallas kernels, attend_back(): pl.pallas_call(attend_back_kernel, grid=(steps,), in_specs=[pl.BlockSpec(...  17.1 us
    all_to_all x4, starting transfers between devices, exchange(): return lax.all_to_all(value, AXES, split_axis=0, concat_axis=0, tiled=True)  15.3 us
    pallas_call x1, Pallas kernels, attend(): pl.pallas_call(attend_kernel, grid=(steps,), in_specs=[by_row(HEAD), whol...  11.7 us
    pallas_call x1, Pallas kernels, middle_part(): pl.pallas_call(middle_kernel, out_shape=[jax.ShapeDtypeStruct(shape, kind...  8.5 us
  transfers between devices with their start and end apart: 28, of which 9 were waited for; matrix products, arithmetic and copies ran while one was open for 7% of the time, Pallas kernels for 26%

profile of v4, /device:TPU:0, one launch (start us, length us, event | category | flops | bytes accessed | tf_op | source)
XLA Modules:
  0.0 211.0 jit_solution(2498451471252097177)
XLA Ops:
  7.2 1.6 pad_maximum_fusion.2
  8.9 1.0 constant_dynamic-slice_fusion
  9.9 4.1 %collective-permute-start.1 = (bf16[64,768]{1,0:T(8,128)(2,1)S(1)}, bf16[64,768]{1,0:T(8,128)(2,1)S(1)}, u32[]{:S(2)}, u32[]{:S(2)}) collective-permute-start(bf16[64,768]{1,0:T(8,128)(2,1)S(1)} %get-tuple-element.135), channel_id=1, source_target_pairs={{0,16},{4,20},{8,24},{12,28},{16,0},{20,4},{24,8},{28,12},{1,17},{... | collective-permute-start | bytes 294920 | tf_op jit(solution)/shard_map/ppermute | solution.py:261
  14.0 1.3 collective-permute-start.2
  15.6 1.1 reshape.682
  17.3 0.8 broadcast_in_dim.5
  18.1 5.2 %all-to-all-start = ((bf16[32,24,256]{2,1,0:T(8,128)(2,1)}), bf16[32,24,256]{2,1,0:T(8,128)(2,1)S(1)}, u32[]{:S(2)}, u32[]{:S(2)}) async-start(bf16[32,24,256]{2,1,0:T(8,128)(2,1)} %bitcast.25), calls=%async_computation | async-start | bytes 786432 | tf_op jit(solution)/shard_map/all_to_all | solution.py:314
  23.7 1.8 collective-permute-start.3
  25.5 1.5 collective-permute-start.5
  27.1 7.5 %collective-permute-done.3 = bf16[2,2,32,768]{3,2,1,0:T(8,128)(2,1)S(1)} collective-permute-done((bf16[2,2,32,768]{3,2,1,0:T(8,128)(2,1)S(1)}, bf16[2,2,32,768]{3,2,1,0:T(8,128)(2,1)S(1)}, u32[]{:S(2)}, u32[]{:S(2)}) %collective-permute-start.3) | collective-permute-done | bytes 196640 | tf_op jit(solution)/shard_map/ppermute | solution.py:261
  34.7 1.0 collective-permute-start.4
  35.7 0.9 collective-permute-start.6
  36.6 5.6 %multiply_sine_fusion = (f32[2048,128]{1,0:T(8,128)}, f32[2048,128]{1,0:T(8,128)}) fusion(f32[128]{0:T(128)S(1)} %fusion.35, f32[2048]{0:T(1024)S(1)} %fusion.23), kind=kLoop, calls=%fused_computation.1 | loop fusion | flops 262144 | bytes 2105856 | tf_op jit(solution)/shard_map/sin | solution.py:310
  42.3 7.6 %collective-permute-done.6 = bf16[2,2,2,32,768]{4,3,2,1,0:T(8,128)(2,1)S(1)} collective-permute-done((bf16[2,2,2,32,768]{4,3,2,1,0:T(8,128)(2,1)S(1)}, bf16[2,2,2,32,768]{4,3,2,1,0:T(8,128)(2,1)S(1)}, u32[]{:S(2)}, u32[]{:S(2)}) %collective-permute-start.6) | collective-permute-done | bytes 393248 | tf_op jit(solution)/shard_map/ppermute | solution.py:261
  50.7 0.8 reshape.705.gain
  51.5 2.3 %collective-permute-done.7.other = bf16[1024,768]{1,0:T(8,128)(2,1)S(1)} collective-permute-done((bf16[1024,768]{1,0:T(8,128)(2,1)S(1)}, bf16[1024,768]{1,0:T(8,128)(2,1)S(1)}, u32[]{:S(2)}, u32[]{:S(2)}) %collective-permute-start.7) | collective-permute-done | bytes 1572896 | tf_op jit(solution)/shard_map/ppermute | solution.py:261
  53.8 1.1 copy-done.3
  54.9 7.3 %project.1 = (bf16[2,1024,768]{2,1,0:T(8,128)(2,1)}, bf16[2,1024,64]{2,1,0:T(8,128)(2,1)}, bf16[2,1024,64]{2,1,0:T(8,128)(2,1)}, bf16[2,1024,64]{2,1,0:T(8,128)(2,1)}) custom-call(s32[1]{0:T(128)} %bitcast.core, bf16[1024,768]{1,0:T(8,128)(2,1)} %bitcast.110, bf16[1024,768]{1,0:T(8,128)(2,1)} %copy-done.3, f32[1,768]{1,0:T(1,128)} %reshape.705.gain, ...), custom_call_target="tpu_custom_call" | custom-call | tf_op jit(solution)/shard_map/project/pallas_call | solution.py:361
  62.2 11.7 %attend.1 = (bf16[2048,2048]{1,0:T(8,128)(2,1)}, f32[2048,64]{1,0:T(8,128)}, f32[2048,1]{1,0:T(8,128)}, bf16[16,2,32,128]{3,2,1,0:T(8,128)(2,1)}) custom-call(bf16[2048,64]{1,0:T(8,128)(2,1)} %bitcast.142, bf16[2048,64]{1,0:T(8,128)(2,1)} %bitcast.144, bf16[2048,64]{1,0:T(8,128)(2,1)} %bitcast.146), custom_call_target="tpu_custom_call" | custom-call | flops 4294967296 | bytes 8388608 | tf_op jit(solution)/shard_map/attend/pallas_call | solution.py:403
  73.8 4.7 %all-to-all-start.1 = ((bf16[32,32,128]{2,1,0:T(8,128)(2,1)}), bf16[32,32,128]{2,1,0:T(8,128)(2,1)S(1)}, u32[]{:S(2)}, u32[]{:S(2)}) async-start(bf16[32,32,128]{2,1,0:T(8,128)(2,1)} %bitcast.133), calls=%async_computation.1 | async-start | bytes 524288 | tf_op jit(solution)/shard_map/all_to_all | solution.py:314
  79.1 13.8 %all-to-all-done.1.got = bf16[32,32,128]{2,1,0:T(8,128)(2,1)S(1)} async-done(((bf16[32,32,128]{2,1,0:T(8,128)(2,1)}), bf16[32,32,128]{2,1,0:T(8,128)(2,1)S(1)}, u32[]{:S(2)}, u32[]{:S(2)}) %all-to-all-start.1) | async-done | bytes 262176 | tf_op jit(solution)/shard_map/all_to_all | solution.py:314
  92.8 1.9 all-gather.3.cloned.1.call-done.late
  94.7 8.5 %middle_part.1 = (bf16[128,768]{1,0:T(8,128)(2,1)}, bf16[32,32,128]{2,1,0:T(8,128)(2,1)}, bf16[128,6528]{1,0:T(8,128)(2,1)}, f32[128,768]{1,0:T(8,128)}) custom-call(bf16[32,32,128]{2,1,0:T(8,128)(2,1)} %copy-done.4, bf16[128,768]{1,0:T(8,128)(2,1)} %bitcast.115, bf16[768,4224]{1,0:T(8,128)(2,1)} %all-gather.3.cloned.1.call-done.late, ...), custom_call_target="tpu_custom_call" | custom-call | tf_op jit(solution)/shard_map/middle_part/pallas_call | solution.py:498
  103.5 2.8 %all-to-all-start.2 = ((bf16[32,32,128]{2,1,0:T(8,128)(2,1)}), bf16[32,32,128]{2,1,0:T(8,128)(2,1)S(1)}, u32[]{:S(2)}, u32[]{:S(2)}) async-start(bf16[32,32,128]{2,1,0:T(8,128)(2,1)} %get-tuple-element.69), calls=%async_computation.2 | async-start | bytes 524288 | tf_op jit(solution)/shard_map/all_to_all | solution.py:314
  107.5 1.2 copy-done.14
  108.7 6.1 %weight_grads.1 = (bf16[4,2,24,1920]{3,2,1,0:T(8,128)(2,1)}, bf16[4,2,24,1920]{3,2,1,0:T(8,128)(2,1)}, bf16[4,2,24,1536]{3,2,1,0:T(8,128)(2,1)}, bf16[4,2,24,153...) custom-call(s32[4]{0:T(128)} %pad_add_fusion.place, ...), custom_call_target="tpu_custom_call" | custom-call | flops 1660944384 | bytes 9830400 | tf_op jit(solution)/shard_map/weight_grads/pallas_call | solution.py:563
  114.8 3.7 %all-to-all-done.2 = bf16[32,32,128]{2,1,0:T(8,128)(2,1)S(1)} async-done(((bf16[32,32,128]{2,1,0:T(8,128)(2,1)}), bf16[32,32,128]{2,1,0:T(8,128)(2,1)S(1)}, u32[]{:S(2)}, u32[]{:S(2)}) %all-to-all-start.2) | async-done | bytes 262176 | tf_op jit(solution)/shard_map/all_to_all | solution.py:314
  119.2 1.1 slice_bitcast_fusion
  121.0 0.8 collective-permute-start.12
  121.8 2.9 %collective-permute-start.13 = (bf16[2,2,24,768]{3,2,1,0:T(8,128)(2,1)S(1)}, bf16[2,2,24,768]{3,2,1,0:T(8,128)(2,1)S(1)}, u32[]{:S(2)}, u32[]{:S(2)}) collective-permute-start(bf16[2,2,24,768]{3,2,1,0:T(8,128)(2,1)S(1)} %get-tuple-element.116), channel_id=1, source_target_pairs={{0,24},{4,28},{8,16},{12,20},{16,8},{20,12},{24,0},{28,4},{1,25},{... | collective-permute-start | bytes 442376 | tf_op jit(solution)/shard_map/ppermute | solution.py:261
  124.8 0.9 collective-permute-start.10
  125.6 17.1 %attend_back.1 = bf16[16,2,136,128]{3,2,1,0:T(8,128)(2,1)} custom-call(bf16[16,2,32,128]{3,2,1,0:T(8,128)(2,1)} %bitcast.132, f32[2048,64]{1,0:T(8,128)} %get-tuple-element.78.attn32, f32[2048,1]{1,0:T(8,128)} %get-tuple-element.79.total, bf16[2048,2048]{1,0:T(8,128)(2,1)} %get-tuple-element.80.weights, bf16[2048,64]{1,0:T(8,128)(2,1)} %bitcast.143, ...), custom_call_target="tpu_custom_call" | custom-call | flops 15032385536 | bytes 8388608 | tf_op jit(solution)/shard_map/attend_back/pallas_call | solution.py:650
  143.8 1.2 collective-permute-start.14
  145.2 1.3 collective-permute-start.15
  146.6 0.8 collective-permute-start.19
  147.5 0.9 collective-permute-start.20
  148.3 1.9 collective-permute-start.21
  150.2 2.6 %all-to-all-start.3 = ((bf16[32,136,128]{2,1,0:T(8,128)(2,1)}), bf16[32,136,128]{2,1,0:T(8,128)(2,1)S(1)}, u32[]{:S(2)}, u32[]{:S(2)}) async-start(bf16[32,136,128]{2,1,0:T(8,128)(2,1)} %bitcast.47), calls=%async_computation.3 | async-start | bytes 2228224 | tf_op jit(solution)/shard_map/all_to_all | solution.py:314
  152.9 19.6 %all-gather.5.cloned.1.call-done.weight = bf16[768,2304]{1,0:T(8,128)(2,1)} async-done(((bf16[24,2304]{1,0:T(8,128)(2,1)}), bf16[768,2304]{1,0:T(8,128)(2,1)}) %all-gather.5.cloned.1.call-update) | async-done | bytes 3538960 | tf_op jit(solution)/shard_map/all_gather | solution.py:804
  172.5 1.1 fusion.2
  173.9 3.9 %collective-permute-start.17 = (bf16[24,3456]{1,0:T(8,128)(2,1)S(1)}, bf16[24,3456]{1,0:T(8,128)(2,1)S(1)}, u32[]{:S(2)}, u32[]{:S(2)}) collective-permute-start(bf16[24,3456]{1,0:T(8,128)(2,1)S(1)} %pad_maximum_fusion.5), channel_id=1, source_target_pairs={{0,24},{4,28},{8,16},{12,20},{16,8},{20,12},{24,0},{28,4},{1,25},{... | collective-permute-start | bytes 497672 | tf_op jit(solution)/shard_map/ppermute | solution.py:261
  178.5 14.1 %all-to-all-done.3.got = bf16[32,136,128]{2,1,0:T(8,128)(2,1)S(1)} async-done(((bf16[32,136,128]{2,1,0:T(8,128)(2,1)}), bf16[32,136,128]{2,1,0:T(8,128)(2,1)S(1)}, u32[]{:S(2)}, u32[]{:S(2)}) %all-to-all-start.3) | async-done | bytes 1114144 | tf_op jit(solution)/shard_map/all_to_all | solution.py:314
  192.6 1.1 copy-done.1
  193.7 4.7 %last_part.1 = (bf16[128,768]{1,0:T(8,128)(2,1)}, f32[24,2304]{1,0:T(8,128)}, f32[8,24]{1,0:T(8,128)}) custom-call(bf16[32,136,128]{2,1,0:T(8,128)(2,1)} %copy-done.1, bf16[768,2304]{1,0:T(8,128)(2,1)} %all-gather.5.cloned.1.call-done.weight, bf16[128,768]{1,0:T(8,128)(2,1)} %bitcast.116, f32[1,768]{1,0:T(1,128)} %reshape.705.gain, ...), custom_call_target="tpu_custom_call" | custom-call | tf_op jit(solution)/shard_map/last_part/pallas_call | solution.py:724
  198.4 1.0 collective-permute-done.16
  199.5 0.8 multiply_reduce_fusion
  201.5 1.2 slice_bitcast_fusion.4
  202.7 1.5 convert_add_fusion.5
  (100 shorter events, 9.0 us)
Async XLA Ops:
  7.2 9.9 %copy-start.15 = (bf16[24]{0:T(256)(128)(2,1)S(1)}, bf16[24]{0:T(256)(128)(2,1)}, u32[]{:S(2)}) copy-start(bf16[24]{0:T(256)(128)(2,1)} %param.9) | copy-start | bytes 148
  7.2 9.9 %copy-start.16 = (bf16[24]{0:T(256)(128)(2,1)S(1)}, bf16[24]{0:T(256)(128)(2,1)}, u32[]{:S(2)}) copy-start(bf16[24]{0:T(256)(128)(2,1)} %param.12) | copy-start | bytes 148
  7.2 87.5 %all-gather.3.cloned.1.call-start = ((), (), s32[]{:S(2)}) async-start(), calls=%async_computation.4 | async-start | bytes 6690816 | tf_op jit(solution)/shard_map/all_gather | solution.py:749
  9.9 13.5 %collective-permute-start.1 = (bf16[64,768]{1,0:T(8,128)(2,1)S(1)}, bf16[64,768]{1,0:T(8,128)(2,1)S(1)}, u32[]{:S(2)}, u32[]{:S(2)}) collective-permute-start(bf16[64,768]{1,0:T(8,128)(2,1)S(1)} %get-tuple-element.135), channel_id=1, source_target_pairs={{0,16},{4,20},{8,24},{12,28},{16,0},{20,4},{24,8},{28,12},{1,17},{... | collective-permute-start | bytes 294920 | tf_op jit(solution)/shard_map/ppermute | solution.py:261
  14.0 9.4 %collective-permute-start.2 = (bf16[64,768]{1,0:T(8,128)(2,1)S(1)}, bf16[64,768]{1,0:T(8,128)(2,1)S(1)}, u32[]{:S(2)}, u32[]{:S(2)}) collective-permute-start(bf16[64,768]{1,0:T(8,128)(2,1)S(1)} %get-tuple-element.135), channel_id=1, source_target_pairs={{0,24},{4,28},{8,16},{12,20},{16,8},{20,12},{24,0},{28,4},{1,25},{... | collective-permute-start | bytes 294920 | tf_op jit(solution)/shard_map/ppermute | solution.py:261
  15.4 8.0 %collective-permute-start = (bf16[64,768]{1,0:T(8,128)(2,1)S(1)}, bf16[64,768]{1,0:T(8,128)(2,1)S(1)}, u32[]{:S(2)}, u32[]{:S(2)}) collective-permute-start(bf16[64,768]{1,0:T(8,128)(2,1)S(1)} %bitcast.129), channel_id=1, source_target_pairs={{0,8},{4,12},{8,0},{12,4},{16,24},{20,28},{24,16},{28,20},{1,9},{5... | collective-permute-start | bytes 294920 | tf_op jit(solution)/shard_map/ppermute | solution.py:261
  18.1 32.2 %all-to-all-start = ((bf16[32,24,256]{2,1,0:T(8,128)(2,1)}), bf16[32,24,256]{2,1,0:T(8,128)(2,1)S(1)}, u32[]{:S(2)}, u32[]{:S(2)}) async-start(bf16[32,24,256]{2,1,0:T(8,128)(2,1)} %bitcast.25), calls=%async_computation | async-start | bytes 786432 | tf_op jit(solution)/shard_map/all_to_all | solution.py:314
  23.3 149.2 %all-gather.5.cloned.1.call-start = ((), (), s32[]{:S(2)}) async-start(), calls=%async_computation.5 | async-start | bytes 3649536 | tf_op jit(solution)/shard_map/all_gather | solution.py:804
  23.7 10.9 %collective-permute-start.3 = (bf16[2,2,32,768]{3,2,1,0:T(8,128)(2,1)S(1)}, bf16[2,2,32,768]{3,2,1,0:T(8,128)(2,1)S(1)}, u32[]{:S(2)}, u32[]{:S(2)}) collective-permute-start(bf16[2,2,32,768]{3,2,1,0:T(8,128)(2,1)S(1)} %get-tuple-element.120), channel_id=1, source_target_pairs={{0,4},{4,0},{8,12},{12,8},{16,20},{20,16},{24,28},{28,24},{1,5},{5... | collective-permute-start | bytes 589832 | tf_op jit(solution)/shard_map/ppermute | solution.py:261
  25.5 10.2 %collective-permute-start.5 = (bf16[2,2,32,768]{3,2,1,0:T(8,128)(2,1)S(1)}, bf16[2,2,32,768]{3,2,1,0:T(8,128)(2,1)S(1)}, u32[]{:S(2)}, u32[]{:S(2)}) collective-permute-start(bf16[2,2,32,768]{3,2,1,0:T(8,128)(2,1)S(1)} %get-tuple-element.123), channel_id=1, source_target_pairs={{0,2},{1,3},{2,0},{3,1},{4,6},{5,7},{6,4},{7,5},{8,10},{9,11},{10,... | collective-permute-start | bytes 589832 | tf_op jit(solution)/shard_map/ppermute | solution.py:261
  34.7 15.3 %collective-permute-start.4 = (bf16[2,2,2,32,768]{4,3,2,1,0:T(8,128)(2,1)S(1)}, bf16[2,2,2,32,768]{4,3,2,1,0:T(8,128)(2,1)S(1)}, u32[]{:S(2)}, u32[]{:S(2)}) collective-permute-start(bf16[2,2,2,32,768]{4,3,2,1,0:T(8,128)(2,1)S(1)} %maximum_select_fusion.4), channel_id=1, source_target_pairs={{0,2},{1,3},{2,0},{3,1},{4,6},{5,7},{6,4},{7,5},{8,10},{9,11},{10,... | collective-permute-start | bytes 1179656 | tf_op jit(solution)/shard_map/ppermute | solution.py:261
  35.7 14.2 %collective-permute-start.6 = (bf16[2,2,2,32,768]{4,3,2,1,0:T(8,128)(2,1)S(1)}, bf16[2,2,2,32,768]{4,3,2,1,0:T(8,128)(2,1)S(1)}, u32[]{:S(2)}, u32[]{:S(2)}) collective-permute-start(bf16[2,2,2,32,768]{4,3,2,1,0:T(8,128)(2,1)S(1)} %maximum_select_fusion.6), channel_id=1, source_target_pairs={{0,4},{4,0},{8,12},{12,8},{16,20},{20,16},{24,28},{28,24},{1,5},{5... | collective-permute-start | bytes 1179656 | tf_op jit(solution)/shard_map/ppermute | solution.py:261
  50.3 3.5 %copy-start = (bf16[2,2,2,2,2,32,768]{6,5,4,3,2,1,0:T(8,128)(2,1)}, bf16[2,2,2,2,2,32,768]{6,5,4,3,2,1,0:T(8,128)(2,1)S(1)}, u32[]{:S(2)}) copy-start(bf16[2,2,2,2,2,32,768]{6,5,4,3,2,1,0:T(8,128)(2,1)S(1)} %pad_maximum_fusion) | copy-start | bytes 4718596
  50.3 3.5 %copy-start.2 = (bf16[32,24,256]{2,1,0:T(8,128)(2,1)}, bf16[32,24,256]{2,1,0:T(8,128)(2,1)S(1)}, u32[]{:S(2)}) copy-start(bf16[32,24,256]{2,1,0:T(8,128)(2,1)S(1)} %all-to-all-done) | copy-start | bytes 1179652
  50.3 3.5 %collective-permute-start.7 = (bf16[1024,768]{1,0:T(8,128)(2,1)S(1)}, bf16[1024,768]{1,0:T(8,128)(2,1)S(1)}, u32[]{:S(2)}, u32[]{:S(2)}) collective-permute-start(bf16[1024,768]{1,0:T(8,128)(2,1)S(1)} %bitcast.109), channel_id=1, source_target_pairs={{0,1},{1,0},{2,3},{3,2},{4,5},{5,4},{6,7},{7,6},{8,9},{9,8},{10,11... | collective-permute-start | bytes 4718600 | tf_op jit(solution)/shard_map/ppermute | solution.py:261
  53.8 1.1 copy-start.3
  73.8 19.0 %all-to-all-start.1 = ((bf16[32,32,128]{2,1,0:T(8,128)(2,1)}), bf16[32,32,128]{2,1,0:T(8,128)(2,1)S(1)}, u32[]{:S(2)}, u32[]{:S(2)}) async-start(bf16[32,32,128]{2,1,0:T(8,128)(2,1)} %bitcast.133), calls=%async_computation.1 | async-start | bytes 524288 | tf_op jit(solution)/shard_map/all_to_all | solution.py:314
  92.8 1.9 copy-start.4
  103.2 4.3 %collective-permute-start.8 = (bf16[128,6528]{1,0:T(8,128)(2,1)}, bf16[128,6528]{1,0:T(8,128)(2,1)S(1)}, u32[]{:S(2)}, u32[]{:S(2)}) collective-permute-start(bf16[128,6528]{1,0:T(8,128)(2,1)} %get-tuple-element.70.acts), channel_id=1, source_target_pairs={{0,1},{1,0},{2,3},{3,2},{4,5},{5,4},{6,7},{7,6},{8,9},{9,8},{10,11... | collective-permute-start | bytes 5013512 | tf_op jit(solution)/shard_map/ppermute | solution.py:261
  103.5 15.0 %all-to-all-start.2 = ((bf16[32,32,128]{2,1,0:T(8,128)(2,1)}), bf16[32,32,128]{2,1,0:T(8,128)(2,1)S(1)}, u32[]{:S(2)}, u32[]{:S(2)}) async-start(bf16[32,32,128]{2,1,0:T(8,128)(2,1)} %get-tuple-element.69), calls=%async_computation.2 | async-start | bytes 524288 | tf_op jit(solution)/shard_map/all_to_all | solution.py:314
  107.5 1.2 copy-start.14
  118.5 7.2 %copy-start.8 = (bf16[32,32,128]{2,1,0:T(8,128)(2,1)}, bf16[32,32,128]{2,1,0:T(8,128)(2,1)S(1)}, u32[]{:S(2)}) copy-start(bf16[32,32,128]{2,1,0:T(8,128)(2,1)S(1)} %all-to-all-done.2) | copy-start | bytes 786436
  118.5 24.4 %collective-permute-start.9 = (bf16[2,2,2,24,1920]{4,3,2,1,0:T(8,128)(2,1)}, bf16[2,2,2,24,1920]{4,3,2,1,0:T(8,128)(2,1)S(1)}, u32[]{:S(2)}, u32[]{:S(2)}) collective-permute-start(bf16[2,2,2,24,1920]{4,3,2,1,0:T(8,128)(2,1)} %bitcast.140), channel_id=1, source_target_pairs={{0,4},{4,0},{8,12},{12,8},{16,20},{20,16},{24,28},{28,24},{1,5},{5... | collective-permute-start | bytes 2211848 | tf_op jit(solution)/shard_map/ppermute | solution.py:261
  120.3 22.5 %collective-permute-start.11 = (bf16[2,2,24,768]{3,2,1,0:T(8,128)(2,1)S(1)}, bf16[2,2,24,768]{3,2,1,0:T(8,128)(2,1)S(1)}, u32[]{:S(2)}, u32[]{:S(2)}) collective-permute-start(bf16[2,2,24,768]{3,2,1,0:T(8,128)(2,1)S(1)} %get-tuple-element.118), channel_id=1, source_target_pairs={{0,8},{4,12},{8,0},{12,4},{16,24},{20,28},{24,16},{28,20},{1,9},{5... | collective-permute-start | bytes 442376 | tf_op jit(solution)/shard_map/ppermute | solution.py:261
  121.0 21.8 %collective-permute-start.12 = (bf16[2,2,24,768]{3,2,1,0:T(8,128)(2,1)S(1)}, bf16[2,2,24,768]{3,2,1,0:T(8,128)(2,1)S(1)}, u32[]{:S(2)}, u32[]{:S(2)}) collective-permute-start(bf16[2,2,24,768]{3,2,1,0:T(8,128)(2,1)S(1)} %get-tuple-element.117), channel_id=1, source_target_pairs={{0,16},{4,20},{8,24},{12,28},{16,0},{20,4},{24,8},{28,12},{1,17},{... | collective-permute-start | bytes 442376 | tf_op jit(solution)/shard_map/ppermute | solution.py:261
  121.8 21.0 %collective-permute-start.13 = (bf16[2,2,24,768]{3,2,1,0:T(8,128)(2,1)S(1)}, bf16[2,2,24,768]{3,2,1,0:T(8,128)(2,1)S(1)}, u32[]{:S(2)}, u32[]{:S(2)}) collective-permute-start(bf16[2,2,24,768]{3,2,1,0:T(8,128)(2,1)S(1)} %get-tuple-element.116), channel_id=1, source_target_pairs={{0,24},{4,28},{8,16},{12,20},{16,8},{20,12},{24,0},{28,4},{1,25},{... | collective-permute-start | bytes 442376 | tf_op jit(solution)/shard_map/ppermute | solution.py:261
  124.8 18.1 %collective-permute-start.10 = (bf16[2,2,2,24,1536]{4,3,2,1,0:T(8,128)(2,1)}, bf16[2,2,2,24,1536]{4,3,2,1,0:T(8,128)(2,1)S(1)}, u32[]{:S(2)}, u32[]{:S(2)}) collective-permute-start(bf16[2,2,2,24,1536]{4,3,2,1,0:T(8,128)(2,1)} %bitcast.141), channel_id=1, source_target_pairs={{0,2},{1,3},{2,0},{3,1},{4,6},{5,7},{6,4},{7,5},{8,10},{9,11},{10,... | collective-permute-start | bytes 1769480 | tf_op jit(solution)/shard_map/ppermute | solution.py:261
  125.6 17.9 %copy-start.5 = (bf16[4,2,24,1920]{3,2,1,0:T(8,128)(2,1)S(1)}, bf16[4,2,24,1920]{3,2,1,0:T(8,128)(2,1)}, u32[]{:S(2)}) copy-start(bf16[4,2,24,1920]{3,2,1,0:T(8,128)(2,1)} %get-tuple-element.86) | copy-start | bytes 2211844
  142.8 2.2 %copy-start.6 = (bf16[4,2,24,1536]{3,2,1,0:T(8,128)(2,1)S(1)}, bf16[4,2,24,1536]{3,2,1,0:T(8,128)(2,1)}, u32[]{:S(2)}) copy-start(bf16[4,2,24,1536]{3,2,1,0:T(8,128)(2,1)} %get-tuple-element.88) | copy-start | bytes 1769476
  142.8 0.7 copy-start.10
  142.8 0.7 copy-start.12
  143.7 2.8 %copy-start.9 = (bf16[2,2,24,768]{3,2,1,0:T(8,128)(2,1)S(1)}, bf16[2,2,24,768]{3,2,1,0:T(8,128)(2,1)}, u32[]{:S(2)}) copy-start(bf16[2,2,24,768]{3,2,1,0:T(8,128)(2,1)} %get-tuple-element.97) | copy-start | bytes 442372
  143.7 2.8 %copy-start.11 = (bf16[2,2,24,768]{3,2,1,0:T(8,128)(2,1)S(1)}, bf16[2,2,24,768]{3,2,1,0:T(8,128)(2,1)}, u32[]{:S(2)}) copy-start(bf16[2,2,24,768]{3,2,1,0:T(8,128)(2,1)} %copy-done.10) | copy-start | bytes 442372
  143.7 2.8 %copy-start.13 = (bf16[2,2,24,768]{3,2,1,0:T(8,128)(2,1)S(1)}, bf16[2,2,24,768]{3,2,1,0:T(8,128)(2,1)}, u32[]{:S(2)}) copy-start(bf16[2,2,24,768]{3,2,1,0:T(8,128)(2,1)} %copy-done.12) | copy-start | bytes 442372
  143.8 28.7 %collective-permute-start.14 = (bf16[2,2,24,1920]{3,2,1,0:T(8,128)(2,1)S(1)}, bf16[2,2,24,1920]{3,2,1,0:T(8,128)(2,1)}, u32[]{:S(2)}, u32[]{:S(2)}) collective-permute-start(bf16[2,2,24,1920]{3,2,1,0:T(8,128)(2,1)S(1)} %dynamic-slice_bitcast_fusion), channel_id=1, source_target_pairs={{0,2},{1,3},{2,0},{3,1},{4,6},{5,7},{6,4},{7,5},{8,10},{9,11},{10,... | collective-permute-start | bytes 1105928 | tf_op jit(solution)/shard_map/ppermute | solution.py:261
  145.2 27.3 %collective-permute-start.15 = (bf16[2,2,24,1536]{3,2,1,0:T(8,128)(2,1)S(1)}, bf16[2,2,24,1536]{3,2,1,0:T(8,128)(2,1)S(1)}, u32[]{:S(2)}, u32[]{:S(2)}) collective-permute-start(bf16[2,2,24,1536]{3,2,1,0:T(8,128)(2,1)S(1)} %dynamic-slice_bitcast_fusion.1), channel_id=1, source_target_pairs={{0,4},{4,0},{8,12},{12,8},{16,20},{20,16},{24,28},{28,24},{1,5},{5... | collective-permute-start | bytes 884744 | tf_op jit(solution)/shard_map/ppermute | solution.py:261
  146.6 31.2 %collective-permute-start.19 = (bf16[24,768]{1,0:T(8,128)(2,1)S(1)}, bf16[24,768]{1,0:T(8,128)(2,1)}, u32[]{:S(2)}, u32[]{:S(2)}) collective-permute-start(bf16[24,768]{1,0:T(8,128)(2,1)S(1)} %get-tuple-element.138), channel_id=1, source_target_pairs={{0,4},{4,0},{8,12},{12,8},{16,20},{20,16},{24,28},{28,24},{1,5},{5... | collective-permute-start | bytes 110600 | tf_op jit(solution)/shard_map/ppermute | solution.py:261
  147.5 50.9 %collective-permute-start.20 = (bf16[24,768]{1,0:T(8,128)(2,1)S(1)}, bf16[24,768]{1,0:T(8,128)(2,1)}, u32[]{:S(2)}, u32[]{:S(2)}) collective-permute-start(bf16[24,768]{1,0:T(8,128)(2,1)S(1)} %get-tuple-element.137), channel_id=1, source_target_pairs={{0,2},{1,3},{2,0},{3,1},{4,6},{5,7},{6,4},{7,5},{8,10},{9,11},{10,... | collective-permute-start | bytes 110600 | tf_op jit(solution)/shard_map/ppermute | solution.py:261
  148.3 50.0 %collective-permute-start.21 = (bf16[24,768]{1,0:T(8,128)(2,1)S(1)}, bf16[24,768]{1,0:T(8,128)(2,1)}, u32[]{:S(2)}, u32[]{:S(2)}) collective-permute-start(bf16[24,768]{1,0:T(8,128)(2,1)S(1)} %get-tuple-element.136), channel_id=1, source_target_pairs={{0,6},{1,7},{2,4},{3,5},{4,2},{5,3},{6,0},{7,1},{8,14},{9,15},{10,... | collective-permute-start | bytes 110600 | tf_op jit(solution)/shard_map/ppermute | solution.py:261
  150.2 42.4 %all-to-all-start.3 = ((bf16[32,136,128]{2,1,0:T(8,128)(2,1)}), bf16[32,136,128]{2,1,0:T(8,128)(2,1)S(1)}, u32[]{:S(2)}, u32[]{:S(2)}) async-start(bf16[32,136,128]{2,1,0:T(8,128)(2,1)} %bitcast.47), calls=%async_computation.3 | async-start | bytes 2228224 | tf_op jit(solution)/shard_map/all_to_all | solution.py:314
  173.8 24.6 %collective-permute-start.18 = (bf16[24,3456]{1,0:T(8,128)(2,1)S(1)}, bf16[24,3456]{1,0:T(8,128)(2,1)S(1)}, u32[]{:S(2)}, u32[]{:S(2)}) collective-permute-start(bf16[24,3456]{1,0:T(8,128)(2,1)S(1)} %pad_maximum_fusion.6), channel_id=1, source_target_pairs={{0,8},{4,12},{8,0},{12,4},{16,24},{20,28},{24,16},{28,20},{1,9},{5... | collective-permute-start | bytes 497672 | tf_op jit(solution)/shard_map/ppermute | solution.py:261
  173.9 24.5 %collective-permute-start.17 = (bf16[24,3456]{1,0:T(8,128)(2,1)S(1)}, bf16[24,3456]{1,0:T(8,128)(2,1)S(1)}, u32[]{:S(2)}, u32[]{:S(2)}) collective-permute-start(bf16[24,3456]{1,0:T(8,128)(2,1)S(1)} %pad_maximum_fusion.5), channel_id=1, source_target_pairs={{0,24},{4,28},{8,16},{12,20},{16,8},{20,12},{24,0},{28,4},{1,25},{... | collective-permute-start | bytes 497672 | tf_op jit(solution)/shard_map/ppermute | solution.py:261
  177.8 21.6 %collective-permute-start.16 = (bf16[24,3456]{1,0:T(8,128)(2,1)S(1)}, bf16[24,3456]{1,0:T(8,128)(2,1)S(1)}, u32[]{:S(2)}, u32[]{:S(2)}) collective-permute-start(bf16[24,3456]{1,0:T(8,128)(2,1)S(1)} %pad_maximum_fusion.4), channel_id=1, source_target_pairs={{0,16},{4,20},{8,24},{12,28},{16,0},{20,4},{24,8},{28,12},{1,17},{... | collective-permute-start | bytes 497672 | tf_op jit(solution)/shard_map/ppermute | solution.py:261
  192.6 1.1 copy-start.1
  193.7 5.8 %copy-start.7 = (bf16[24,2304]{1,0:T(8,128)(2,1)S(1)}, bf16[24,2304]{1,0:T(8,128)(2,1)}, u32[]{:S(2)}) copy-start(bf16[24,2304]{1,0:T(8,128)(2,1)} %param.13) | copy-start | bytes 331780
Sparse Core Ops, SparseCore 0:
  11.4 83.2 all-gather.2
  97.6 74.7 all-gather.4

commit v5 on v4

--- a/solution.py
+++ b/solution.py
@@ -250,10 +250,6 @@
 SENT = 136
 BY_COLUMN = (((1,), (1,)), ((), ()))
 BY_ROW = (((0,), (0,)), ((), ()))
-
-
-def pick(value, index):
-    return lax.dynamic_index_in_dim(value, index, 0, keepdims=False)
 
 
 def swap(value, axis, bit):
@@ -503,69 +499,52 @@
 
 
 def weight_grads_kernel(
-    place, acts, acts_too, keep_a, give_a, keep_b, give_b, own_c, give_c, total, turned, *,
-    width, hidden_units
+    place, acts, acts_too, keep_a, give_a, keep_b, give_b, total, turned, *, width, hidden_units
 ):
-    x, y, core, z = place[0], place[1], place[2], place[3]
+    x, y, core = place[0], place[1], place[2]
     rows = acts.shape[0]
-    joint = 3 * width
-    active = joint + 2 * hidden_units
-    branch = active + hidden_units
+    cut = 3 * width + 2 * hidden_units
 
     def turn_rows(i):
         columns = slice(i * width, (i + 1) * width)
         turned[:, :rows] = jnp.transpose(acts[:, columns])
         turned[:, rows:] = jnp.transpose(acts_too[:, columns])
 
-    def multiply(start):
+    def multiply(start, count):
         right = jnp.concatenate(
-            [acts[:, start : start + TILE], acts_too[:, start : start + TILE]], axis=0
+            [acts[:, start : start + count], acts_too[:, start : start + count]], axis=0
         )
         product = jnp.dot(turned[...], right, preferred_element_type=F32)
-        total[...] = product.reshape(total.shape)
-
-    def write_b(i):
+        total[..., :count] = product.reshape(*total.shape[:-1], count)
+
+    turn_rows(1)
+    for i in range(2 * hidden_units // TILE):
         columns = slice(i * TILE, (i + 1) * TILE)
+        multiply(3 * width + i * TILE, TILE)
+        keep_a[..., columns] = total[:, x, :, core].astype(BF)
+        give_a[..., columns] = total[:, 1 - x, :, core].astype(BF)
+    turn_rows(0)
+    for i in range((width + hidden_units) // TILE):
+        columns = slice(i * TILE, (i + 1) * TILE)
+        if i == width // TILE:
+            turn_rows(2)
+        if i < width // TILE:
+            multiply(cut + hidden_units + i * TILE, TILE)
+        else:
+            multiply(cut - width + i * TILE, TILE)
         keep_b[..., columns] = total[:, :, y, core].astype(BF)
         give_b[..., columns] = total[:, :, 1 - y, core].astype(BF)
-
-    turn_rows(0)
-    for i in range(width // TILE):
-        columns = slice(i * TILE, (i + 1) * TILE)
-        multiply(branch + i * TILE)
-        own_c[..., columns] = total[z, :, :, core].astype(BF)
-        for k in (1, 2, 3):
-            other = z + k - 2 * ((z % 2) * (k % 2) + (z // 2) * (k // 2) * 2)
-            give_c[k - 1, ..., columns] = total[other, :, :, core].astype(BF)
-    turn_rows(1)
-    tiles_a = keep_a.shape[-1] // TILE
-    for i in range(2 * hidden_units // TILE):
-        columns = slice(i * TILE, (i + 1) * TILE)
-        multiply(joint + i * TILE)
-        if i < tiles_a:
-            keep_a[..., columns] = total[:, x, :, core].astype(BF)
-            give_a[..., columns] = total[:, 1 - x, :, core].astype(BF)
-        else:
-            write_b(i - tiles_a)
-    turn_rows(2)
-    for i in range(hidden_units // TILE):
-        multiply(active + i * TILE)
-        write_b(2 * hidden_units // TILE - tiles_a + i)
 
 
 def weight_grads(place, acts, acts_too, width, hidden_units, rows_here):
     rows = acts.shape[0]
     zs = width // (8 * rows_here)
+    shape = lambda columns: jax.ShapeDtypeStruct((zs, 2, rows_here, columns), BF)
     columns = 3 * hidden_units + width
-    columns_a = 5 * (2 * hidden_units // TILE) // 6 * TILE
-    columns_b = 3 * hidden_units - columns_a
-    full = lambda *dims: jax.ShapeDtypeStruct(dims, BF)
     return pl.pallas_call(
         functools.partial(weight_grads_kernel, width=width, hidden_units=hidden_units),
         in_specs=[smem()] + [pl.BlockSpec(memory_space=pltpu.VMEM)] * 2,
-        out_shape=[full(zs, 2, rows_here, columns_a)] * 2
-        + [full(zs, 2, rows_here, columns_b)] * 2
-        + [full(2, 2, rows_here, width), full(3, 2, 2, rows_here, width)],
+        out_shape=[shape(2 * hidden_units)] * 2 + [shape(width + hidden_units)] * 2,
         scratch_shapes=[
             pltpu.VMEM((zs, 2, 2, 2, rows_here, TILE), F32),
             pltpu.VMEM((width, 2 * rows), BF),
@@ -609,18 +588,18 @@
         grad_scores, key_rows[...], preferred_element_type=F32
     )
     grad_value[...] += lax.dot_general(
-        low, (wide * inverse).astype(BF), BY_ROW, preferred_element_type=F32
+        (wide * inverse).astype(BF), low, BY_ROW, preferred_element_type=F32
     )
     grad_key[...] += lax.dot_general(
-        grad_scores, queries[...], BY_ROW, preferred_element_type=F32
+        queries[...], grad_scores, BY_ROW, preferred_element_type=F32
     )
 
     @pl.when(step == pl.num_programs(0) - 1)
     def _():
-        length = grad_key.shape[0]
-        both = side_by_side(grad_query[...], grad_key[...])
+        length = grad_query.shape[0]
+        both = side_by_side(grad_query[...], jnp.transpose(grad_key[...]))
         both = (both * cosine[...] - turn(both) * sine[...]).astype(BF)
-        low = grad_value[...].astype(BF)
+        low = jnp.transpose(grad_value[...]).astype(BF)
         copy.wait()
         head_grad = jnp.transpose(
             lax.dot_general(
@@ -666,7 +645,8 @@
         ],
         out_specs=whole(*send),
         out_shape=jax.ShapeDtypeStruct(send, BF),
-        scratch_shapes=[pltpu.VMEM((length, HEAD), F32)] * 3
+        scratch_shapes=[pltpu.VMEM((length, HEAD), F32)]
+        + [pltpu.VMEM((HEAD, length), F32)] * 2
         + [pltpu.VMEM(hidden.shape, BF), pltpu.SemaphoreType.DMA],
         cost_estimate=pl.CostEstimate(
             flops=14 * length * length * HEAD * 4,
@@ -717,7 +697,7 @@
         grad_weight[16:, place(2, h)] = side_by_side(left[:8, HEAD:], right[:8, HEAD:])
     sums = jnp.sum(grad_weight[...] * own_weight[...].astype(F32), axis=1, keepdims=True)
     sums = jnp.transpose(jnp.broadcast_to(sums, (sums.shape[0], LANES)))[:8]
-    gain_grad[...] = sums / own_gain[...]
+    gain_grad[...] = (sums / own_gain[...])[0]
 
 
 def last_part(got, weight, tokens, gain, grad_middle, own_weight, own_gain):
@@ -726,7 +706,7 @@
         out_shape=[
             jax.ShapeDtypeStruct(tokens.shape, BF),
             jax.ShapeDtypeStruct(own_weight.shape, F32),
-            jax.ShapeDtypeStruct((8, own_weight.shape[0]), F32),
+            jax.ShapeDtypeStruct((own_weight.shape[0],), F32),
         ],
         scratch_shapes=[pltpu.VMEM((tokens.shape[0], weight.shape[1]), BF)],
         name="last_part",
@@ -742,9 +722,8 @@
     rows = sequences * per_device
     length = per_device * 32
     core = my_bit("ulysses", 1).astype(jnp.int32).reshape(1)
-    x, y = my_bit("blk", 1), my_bit("ulysses", 2)
-    z = lax.axis_index("blk") // 2
-    place = jnp.stack([x, y, my_bit("ulysses", 1), z]).astype(jnp.int32)
+    place = jnp.stack([my_bit("blk", 1), my_bit("ulysses", 2), my_bit("ulysses", 1)])
+    place = place.astype(jnp.int32)
     late = jnp.concatenate([in_weight, attn_out_weight, jnp.transpose(out_weight)], axis=1)
     late_full = lax.all_gather(late, AXES, axis=0, tiled=True)
     by_head = qkv_weight.reshape(rows_here, 3, HEADS, HEAD).transpose(2, 0, 1, 3)
@@ -783,12 +762,10 @@
     acts_too = swap(acts, "ulysses", 1)
     parts = weight_grads(place, acts, acts_too, model_width, hidden_units, rows_here)
     got, parts = lax.optimization_barrier((got, parts))
-    *parts, own_c, give_c = parts
     keep_a, give_a, keep_b, give_b = (
         part.reshape(2, 2, *part.shape[1:]) for part in parts
     )
     came_a, came_b = swap(give_a, "blk", 1), swap(give_b, "ulysses", 2)
-    came_c = [swap(give_c[k - 1], "blk", 2 * k) for k in (1, 2, 3)]
     send = attend_back(
         got.reshape(length // 128, 2, 32, LANES),
         attn32,
@@ -802,30 +779,21 @@
         hidden_one.reshape(length, model_width),
     )
     qkv_full = lax.all_gather(qkv_weight, AXES, axis=0, tiled=True)
-    send, came_a, came_b, came_c = lax.optimization_barrier((send, came_a, came_b, came_c))
+    send, came_a, came_b = lax.optimization_barrier((send, came_a, came_b))
     got = exchange(send.reshape(32, SENT, LANES))
     keep_a, give_a = halve(keep_a, came_a, "ulysses", 2, 2)
     keep_b, give_b = halve(keep_b, came_b, "blk", 1, 2)
     came_a, came_b = swap(give_a, "ulysses", 2), swap(give_b, "blk", 1)
-    total_c = own_c.astype(F32)
-    for part in came_c:
-        total_c = total_c + part.astype(F32)
-    total_c = total_c.astype(BF).reshape(4, rows_here, model_width)
-    side = x * 2 + y
-    shard_attn = [pick(total_c, side)]
-    shard_attn.append(swap(pick(total_c, side ^ 2), "blk", 1))
-    shard_attn.append(swap(pick(total_c, side ^ 1), "ulysses", 2))
-    shard_attn.append(swap(pick(total_c, side ^ 3), AXES, 6))
-    came_a, came_b, qkv_full = lax.optimization_barrier((came_a, came_b, qkv_full))
-    total = [
-        (keep.astype(F32) + came.astype(F32)).astype(BF).reshape(4, rows_here, -1)
-        for keep, came in ((keep_a, came_a), (keep_b, came_b))
-    ]
-
-    def rows_of(owner):
-        return jnp.concatenate([pick(part, owner) for part in total], axis=1)
-
-    shards = [rows_of(z)] + [swap(rows_of(z ^ k), "blk", 2 * k) for k in (2, 3, 1)]
+    z = lax.axis_index("blk") // 2
+
+    def spread(keep, came):
+        total = (keep.astype(F32) + came.astype(F32)).astype(BF).reshape(4, rows_here, -1)
+        row = lambda owner: lax.dynamic_index_in_dim(total, owner, 0, keepdims=False)
+        return [row(z)] + [swap(row(z ^ k), "blk", 2 * k) for k in (2, 3, 1)]
+
+    parts_a = spread(keep_a, came_a)
+    came_b, qkv_full = lax.optimization_barrier((came_b, qkv_full))
+    parts_b = spread(keep_b, came_b)
     last = last_part(
         got,
         qkv_full,
@@ -835,19 +803,19 @@
         qkv_weight,
         attn_gain.astype(F32).reshape(1, rows_here),
     )
-    (input_grad, shard_qkv, shard_one), shards, shard_attn = lax.optimization_barrier(
-        (last, shards, shard_attn)
+    (input_grad, shard_qkv, shard_one), parts_a, parts_b = lax.optimization_barrier(
+        (last, parts_a, parts_b)
     )
     input_grad = input_grad.reshape(sequences, per_device, model_width)
-    shard_attn = sum(part.astype(F32) for part in shard_attn)
-    shards = sum(part.astype(F32) for part in shards)
-    shard_in = shards[:, : 2 * hidden_units]
-    shard_out = jnp.transpose(shards[:, 2 * hidden_units :])
+    shard_in = sum(part.astype(F32) for part in parts_a)
+    shards = sum(part.astype(F32) for part in parts_b)
+    shard_attn = shards[:, :model_width]
+    shard_out = jnp.transpose(shards[:, model_width:])
     shard_two = jnp.sum(shard_in * in_weight.astype(F32), axis=1) / mlp_gain.astype(F32)
     return (
         layer_output.reshape(sequences, per_device, model_width),
         input_grad,
-        shard_one[0],
+        shard_one,
         shard_qkv,
         shard_attn,
         shard_two,

time: 212 us -> 208 us (0.981)
  starting transfers between devices: 43.5 us -> 40.1 us
    ppermute x22 -> x19, waiting for transfers between devices: 18.4 us -> 36.5 us  [swap(): return lax.ppermute(value, axis, [(i, i ^ bit) for i in range(size)])]
    all_to_all x4, waiting for transfers between devices: 31.6 us -> 18 us  [exchange(): return lax.all_to_all(value, AXES, split_axis=0, concat_axis=0, tiled=True)]
    ppermute x22 -> x19, starting transfers between devices: 28.1 us -> 24 us  [swap(): return lax.ppermute(value, axis, [(i, i ^ bit) for i in range(size)])]
    all_gather x1, waiting for transfers between devices: 19.6 us -> 16.1 us  [owner_body(): qkv_full = lax.all_gather(qkv_weight, AXES, axis=0, tiled=True)]
    convert_element_type x2, other arithmetic: 0.32 us -> 3.25 us  [halve(): total = (keep.astype(F32) + got.astype(F32)).astype(BF)]
    squeeze x5 -> x2, local copies, waits for them, and re-layouts: 2.39 us -> 0.1 us  [spread(): lax.dynamic_index_in_dim(total, owner, 0, keepdims=False)]
  transfers between devices with their start and end apart: 28 -> 25, of which waited for: 9 -> 10; matrix products, arithmetic and copies ran while one was open for 7% -> 9% of each run, Pallas kernels for 26% -> 26%
where the time goes in v5:
time: 208 us; the launch traced here: 207 us
  waiting for transfers between devices  72.6 us (35%)
  Pallas kernels  54.5 us (26%)
  starting transfers between devices  40.1 us (19%)
  other arithmetic  15.3 us (7%)
  between operations  14.5 us (7%)
  local copies, waits for them, and re-layouts  10.5 us (5%)
    ppermute x19, waiting for transfers between devices, swap(): return lax.ppermute(value, axis, [(i, i ^ bit) for i in range(size)])  36.5 us
    ppermute x19, starting transfers between devices, swap(): return lax.ppermute(value, axis, [(i, i ^ bit) for i in range(size)])  24 us
    all_to_all x4, waiting for transfers between devices, exchange(): return lax.all_to_all(value, AXES, split_axis=0, concat_axis=0, tiled=True)  18 us
    pallas_call x1, Pallas kernels, attend_back(): pl.pallas_call(attend_back_kernel, grid=(steps,), in_specs=[pl.BlockSpec(...  16.3 us
    all_gather x1, waiting for transfers between devices, owner_body(): qkv_full = lax.all_gather(qkv_weight, AXES, axis=0, tiled=True)  16.1 us
    all_to_all x4, starting transfers between devices, exchange(): return lax.all_to_all(value, AXES, split_axis=0, concat_axis=0, tiled=True)  15.9 us
    pallas_call x1, Pallas kernels, attend(): pl.pallas_call(attend_kernel, grid=(steps,), in_specs=[by_row(HEAD), whol...  11.7 us
    pallas_call x1, Pallas kernels, middle_part(): pl.pallas_call(middle_kernel, out_shape=[jax.ShapeDtypeStruct(shape, kind...  8.51 us
  transfers between devices with their start and end apart: 25, of which 10 were waited for; matrix products, arithmetic and copies ran while one was open for 9% of the time, Pallas kernels for 26%

profile of v5, /device:TPU:0, one launch (start us, length us, event | category | flops | bytes accessed | tf_op | source)
XLA Modules:
  0.0 207.4 jit_solution(1353235172482595128)
XLA Ops:
  7.2 1.6 pad_maximum_fusion.2
  8.9 1.0 constant_dynamic-slice_fusion
  9.9 4.1 %collective-permute-start.1 = (bf16[64,768]{1,0:T(8,128)(2,1)S(1)}, bf16[64,768]{1,0:T(8,128)(2,1)S(1)}, u32[]{:S(2)}, u32[]{:S(2)}) collective-permute-start(bf16[64,768]{1,0:T(8,128)(2,1)S(1)} %get-tuple-element.116), channel_id=1, source_target_pairs={{0,16},{4,20},{8,24},{12,28},{16,0},{20,4},{24,8},{28,12},{1,17},{... | collective-permute-start | bytes 294920 | tf_op jit(solution)/shard_map/ppermute | solution.py:257
  14.0 1.3 collective-permute-start.2
  15.6 1.1 reshape.679
  17.3 0.8 broadcast_in_dim.5
  18.1 5.2 %all-to-all-start = ((bf16[32,24,256]{2,1,0:T(8,128)(2,1)}), bf16[32,24,256]{2,1,0:T(8,128)(2,1)S(1)}, u32[]{:S(2)}, u32[]{:S(2)}) async-start(bf16[32,24,256]{2,1,0:T(8,128)(2,1)} %bitcast.25), calls=%async_computation | async-start | bytes 786432 | tf_op jit(solution)/shard_map/all_to_all | solution.py:310
  23.7 1.8 collective-permute-start.3
  25.5 1.5 collective-permute-start.5
  27.1 7.5 %collective-permute-done.3 = bf16[2,2,32,768]{3,2,1,0:T(8,128)(2,1)S(1)} collective-permute-done((bf16[2,2,32,768]{3,2,1,0:T(8,128)(2,1)S(1)}, bf16[2,2,32,768]{3,2,1,0:T(8,128)(2,1)S(1)}, u32[]{:S(2)}, u32[]{:S(2)}) %collective-permute-start.3) | collective-permute-done | bytes 196640 | tf_op jit(solution)/shard_map/ppermute | solution.py:257
  34.7 1.0 collective-permute-start.4
  35.7 0.9 collective-permute-start.6
  36.6 5.5 %multiply_sine_fusion = (f32[2048,128]{1,0:T(8,128)}, f32[2048,128]{1,0:T(8,128)}) fusion(f32[128]{0:T(128)S(1)} %fusion.35, f32[2048]{0:T(1024)S(1)} %fusion.23), kind=kLoop, calls=%fused_computation.3 | loop fusion | flops 262144 | bytes 2105856 | tf_op jit(solution)/shard_map/sin | solution.py:306
  42.3 7.6 %collective-permute-done.6 = bf16[2,2,2,32,768]{4,3,2,1,0:T(8,128)(2,1)S(1)} collective-permute-done((bf16[2,2,2,32,768]{4,3,2,1,0:T(8,128)(2,1)S(1)}, bf16[2,2,2,32,768]{4,3,2,1,0:T(8,128)(2,1)S(1)}, u32[]{:S(2)}, u32[]{:S(2)}) %collective-permute-start.6) | collective-permute-done | bytes 393248 | tf_op jit(solution)/shard_map/ppermute | solution.py:257
  50.7 0.8 reshape.701.gain
  51.5 2.3 %collective-permute-done.7.other = bf16[1024,768]{1,0:T(8,128)(2,1)S(1)} collective-permute-done((bf16[1024,768]{1,0:T(8,128)(2,1)S(1)}, bf16[1024,768]{1,0:T(8,128)(2,1)S(1)}, u32[]{:S(2)}, u32[]{:S(2)}) %collective-permute-start.7) | collective-permute-done | bytes 1572896 | tf_op jit(solution)/shard_map/ppermute | solution.py:257
  53.8 1.1 copy-done.3
  54.9 7.2 %project.1 = (bf16[2,1024,768]{2,1,0:T(8,128)(2,1)}, bf16[2,1024,64]{2,1,0:T(8,128)(2,1)}, bf16[2,1024,64]{2,1,0:T(8,128)(2,1)}, bf16[2,1024,64]{2,1,0:T(8,128)(2,1)}) custom-call(s32[1]{0:T(128)} %bitcast.core, bf16[1024,768]{1,0:T(8,128)(2,1)} %bitcast.92, bf16[1024,768]{1,0:T(8,128)(2,1)} %copy-done.3, f32[1,768]{1,0:T(1,128)} %reshape.701.gain, ...), custom_call_target="tpu_custom_call" | custom-call | tf_op jit(solution)/shard_map/project/pallas_call | solution.py:357
  62.1 11.7 %attend.1 = (bf16[2048,2048]{1,0:T(8,128)(2,1)}, f32[2048,64]{1,0:T(8,128)}, f32[2048,1]{1,0:T(8,128)}, bf16[16,2,32,128]{3,2,1,0:T(8,128)(2,1)}) custom-call(bf16[2048,64]{1,0:T(8,128)(2,1)} %bitcast.124, bf16[2048,64]{1,0:T(8,128)(2,1)} %bitcast.126, bf16[2048,64]{1,0:T(8,128)(2,1)} %bitcast.128), custom_call_target="tpu_custom_call" | custom-call | flops 4294967296 | bytes 8388608 | tf_op jit(solution)/shard_map/attend/pallas_call | solution.py:399
  73.8 4.7 %all-to-all-start.1 = ((bf16[32,32,128]{2,1,0:T(8,128)(2,1)}), bf16[32,32,128]{2,1,0:T(8,128)(2,1)S(1)}, u32[]{:S(2)}, u32[]{:S(2)}) async-start(bf16[32,32,128]{2,1,0:T(8,128)(2,1)} %bitcast.115), calls=%async_computation.1 | async-start | bytes 524288 | tf_op jit(solution)/shard_map/all_to_all | solution.py:310
  79.0 13.8 %all-to-all-done.1.got = bf16[32,32,128]{2,1,0:T(8,128)(2,1)S(1)} async-done(((bf16[32,32,128]{2,1,0:T(8,128)(2,1)}), bf16[32,32,128]{2,1,0:T(8,128)(2,1)S(1)}, u32[]{:S(2)}, u32[]{:S(2)}) %all-to-all-start.1) | async-done | bytes 262176 | tf_op jit(solution)/shard_map/all_to_all | solution.py:310
  92.9 1.9 all-gather.3.cloned.1.call-done.late
  94.7 8.5 %middle_part.1 = (bf16[128,768]{1,0:T(8,128)(2,1)}, bf16[32,32,128]{2,1,0:T(8,128)(2,1)}, bf16[128,6528]{1,0:T(8,128)(2,1)}, f32[128,768]{1,0:T(8,128)}) custom-call(bf16[32,32,128]{2,1,0:T(8,128)(2,1)} %copy-done.4, bf16[128,768]{1,0:T(8,128)(2,1)} %bitcast.97, bf16[768,4224]{1,0:T(8,128)(2,1)} %all-gather.3.cloned.1.call-done.late, ...), custom_call_target="tpu_custom_call" | custom-call | tf_op jit(solution)/shard_map/middle_part/pallas_call | solution.py:494
  103.5 2.9 %all-to-all-start.2 = ((bf16[32,32,128]{2,1,0:T(8,128)(2,1)}), bf16[32,32,128]{2,1,0:T(8,128)(2,1)S(1)}, u32[]{:S(2)}, u32[]{:S(2)}) async-start(bf16[32,32,128]{2,1,0:T(8,128)(2,1)} %get-tuple-element.61), calls=%async_computation.2 | async-start | bytes 524288 | tf_op jit(solution)/shard_map/all_to_all | solution.py:310
  107.1 1.2 copy-done.10
  108.3 6.1 %weight_grads.1 = (bf16[4,2,24,2304]{3,2,1,0:T(8,128)(2,1)}, bf16[4,2,24,2304]{3,2,1,0:T(8,128)(2,1)}, bf16[4,2,24,1920]{3,2,1,0:T(8,128)(2,1)}, bf16[4,2,24,1920]{3,2,1,0:T(8,128)(2,1)}) custom-call(s32[3]{0:T(128)} %pad_add_fusion.place, bf16[128,6528]{1,0:T(8,128)(2,1)} %get-tuple-element.62.acts, bf16[128,6528]{1,0:T(8,128)(2,1)} %copy-done.10), custom_call_target="tpu_custom_call" | custom-call | flops 1660944384 | bytes 9830400 | tf_op jit(solution)/shard_map/weight_grads/pallas_call | solution.py:544
  114.4 4.2 %all-to-all-done.2 = bf16[32,32,128]{2,1,0:T(8,128)(2,1)S(1)} async-done(((bf16[32,32,128]{2,1,0:T(8,128)(2,1)}), bf16[32,32,128]{2,1,0:T(8,128)(2,1)S(1)}, u32[]{:S(2)}, u32[]{:S(2)}) %all-to-all-start.2) | async-done | bytes 262176 | tf_op jit(solution)/shard_map/all_to_all | solution.py:310
  118.5 0.8 collective-permute-start.9
  119.3 0.9 collective-permute-start.10
  120.2 16.3 %attend_back.1 = bf16[16,2,136,128]{3,2,1,0:T(8,128)(2,1)} custom-call(bf16[16,2,32,128]{3,2,1,0:T(8,128)(2,1)} %bitcast.114, f32[2048,64]{1,0:T(8,128)} %get-tuple-element.68.attn32, f32[2048,1]{1,0:T(8,128)} %get-tuple-element.69.total, bf16[2048,2048]{1,0:T(8,128)(2,1)} %get-tuple-element.70.weights, bf16[2048,64]{1,0:T(8,128)(2,1)} %bitcast.125, ...), custom_call_target="tpu_custom_call" | custom-call | flops 15032385536 | bytes 8388608 | tf_op jit(solution)/shard_map/attend_back/pallas_call | solution.py:629
  136.5 2.0 collective-permute-done.10
  138.5 4.3 %collective-permute-done.9 = bf16[2,2,2,24,2304]{4,3,2,1,0:T(8,128)(2,1)S(1)} collective-permute-done((bf16[2,2,2,24,2304]{4,3,2,1,0:T(8,128)(2,1)}, bf16[2,2,2,24,2304]{4,3,2,1,0:T(8,128)(2,1)S(1)}, u32[]{:S(2)}, u32[]{:S(2)}) %collective-permute-start.9) | collective-permute-done | bytes 884768 | tf_op jit(solution)/shard_map/ppermute | solution.py:257
  142.8 1.6 fusion.1
  144.4 0.8 collective-permute-start.11
  145.2 3.2 %all-to-all-start.3 = ((bf16[32,136,128]{2,1,0:T(8,128)(2,1)}), bf16[32,136,128]{2,1,0:T(8,128)(2,1)S(1)}, u32[]{:S(2)}, u32[]{:S(2)}) async-start(bf16[32,136,128]{2,1,0:T(8,128)(2,1)} %bitcast.105), calls=%async_computation.3 | async-start | bytes 2228224 | tf_op jit(solution)/shard_map/all_to_all | solution.py:310
  148.4 1.6 fusion
  150.0 0.8 dynamic-slice_bitcast_fusion
  150.9 1.8 collective-permute-start.12
  152.6 16.1 %all-gather.5.cloned.1.call-done.weight = bf16[768,2304]{1,0:T(8,128)(2,1)} async-done(((bf16[24,2304]{1,0:T(8,128)(2,1)}), bf16[768,2304]{1,0:T(8,128)(2,1)}) %all-gather.5.cloned.1.call-update) | async-done | bytes 3538960 | tf_op jit(solution)/shard_map/all_gather | solution.py:781
  168.9 2.3 %collective-permute-start.16 = (bf16[24,1920]{1,0:T(8,128)(2,1)S(1)}, bf16[24,1920]{1,0:T(8,128)(2,1)S(1)}, u32[]{:S(2)}, u32[]{:S(2)}) collective-permute-start(bf16[24,1920]{1,0:T(8,128)(2,1)S(1)} %get-tuple-element.113), channel_id=1, source_target_pairs={{0,16},{4,20},{8,24},{12,28},{16,0},{20,4},{24,8},{28,12},{1,17},{... | collective-permute-start | bytes 276488 | tf_op jit(solution)/shard_map/ppermute | solution.py:257
  171.2 1.8 collective-permute-start.17
  173.0 1.1 fusion.2
  174.2 2.6 %collective-permute-start.13 = (bf16[24,2304]{1,0:T(8,128)(2,1)S(1)}, bf16[24,2304]{1,0:T(8,128)(2,1)S(1)}, u32[]{:S(2)}, u32[]{:S(2)}) collective-permute-start(bf16[24,2304]{1,0:T(8,128)(2,1)S(1)} %get-tuple-element.102), channel_id=1, source_target_pairs={{0,16},{4,20},{8,24},{12,28},{16,0},{20,4},{24,8},{28,12},{1,17},{... | collective-permute-start | bytes 331784 | tf_op jit(solution)/shard_map/ppermute | solution.py:257
  176.9 1.8 collective-permute-start.14
  178.7 12.9 %collective-permute-done.16 = bf16[24,1920]{1,0:T(8,128)(2,1)S(1)} collective-permute-done((bf16[24,1920]{1,0:T(8,128)(2,1)S(1)}, bf16[24,1920]{1,0:T(8,128)(2,1)S(1)}, u32[]{:S(2)}, u32[]{:S(2)}) %collective-permute-start.16) | collective-permute-done | bytes 92192 | tf_op jit(solution)/shard_map/ppermute | solution.py:257
  192.0 1.0 copy-done.1
  193.1 4.7 %last_part.1 = (bf16[128,768]{1,0:T(8,128)(2,1)}, f32[24,2304]{1,0:T(8,128)}, f32[24]{0:T(128)}) custom-call(bf16[32,136,128]{2,1,0:T(8,128)(2,1)} %copy-done.1, bf16[768,2304]{1,0:T(8,128)(2,1)} %all-gather.5.cloned.1.call-done.weight, bf16[128,768]{1,0:T(8,128)(2,1)} %bitcast.98, f32[1,768]{1,0:T(1,128)} %reshape.701.gain, ...), custom_call_target="tpu_custom_call" | custom-call | tf_op jit(solution)/shard_map/last_part/pallas_call | solution.py:704
  199.2 0.9 multiply_reduce_fusion
  (78 shorter events, 6.2 us)
Async XLA Ops:
  7.2 9.9 %copy-start.11 = (bf16[24]{0:T(256)(128)(2,1)S(1)}, bf16[24]{0:T(256)(128)(2,1)}, u32[]{:S(2)}) copy-start(bf16[24]{0:T(256)(128)(2,1)} %param.9) | copy-start | bytes 148
  7.2 9.9 %copy-start.12 = (bf16[24]{0:T(256)(128)(2,1)S(1)}, bf16[24]{0:T(256)(128)(2,1)}, u32[]{:S(2)}) copy-start(bf16[24]{0:T(256)(128)(2,1)} %param.12) | copy-start | bytes 148
  7.2 87.5 %all-gather.3.cloned.1.call-start = ((), (), s32[]{:S(2)}) async-start(), calls=%async_computation.4 | async-start | bytes 6690816 | tf_op jit(solution)/shard_map/all_gather | solution.py:728
  9.9 13.5 %collective-permute-start.1 = (bf16[64,768]{1,0:T(8,128)(2,1)S(1)}, bf16[64,768]{1,0:T(8,128)(2,1)S(1)}, u32[]{:S(2)}, u32[]{:S(2)}) collective-permute-start(bf16[64,768]{1,0:T(8,128)(2,1)S(1)} %get-tuple-element.116), channel_id=1, source_target_pairs={{0,16},{4,20},{8,24},{12,28},{16,0},{20,4},{24,8},{28,12},{1,17},{... | collective-permute-start | bytes 294920 | tf_op jit(solution)/shard_map/ppermute | solution.py:257
  14.0 9.4 %collective-permute-start.2 = (bf16[64,768]{1,0:T(8,128)(2,1)S(1)}, bf16[64,768]{1,0:T(8,128)(2,1)S(1)}, u32[]{:S(2)}, u32[]{:S(2)}) collective-permute-start(bf16[64,768]{1,0:T(8,128)(2,1)S(1)} %get-tuple-element.116), channel_id=1, source_target_pairs={{0,24},{4,28},{8,16},{12,20},{16,8},{20,12},{24,0},{28,4},{1,25},{... | collective-permute-start | bytes 294920 | tf_op jit(solution)/shard_map/ppermute | solution.py:257
  15.4 8.0 %collective-permute-start = (bf16[64,768]{1,0:T(8,128)(2,1)S(1)}, bf16[64,768]{1,0:T(8,128)(2,1)S(1)}, u32[]{:S(2)}, u32[]{:S(2)}) collective-permute-start(bf16[64,768]{1,0:T(8,128)(2,1)S(1)} %bitcast.111), channel_id=1, source_target_pairs={{0,8},{4,12},{8,0},{12,4},{16,24},{20,28},{24,16},{28,20},{1,9},{5... | collective-permute-start | bytes 294920 | tf_op jit(solution)/shard_map/ppermute | solution.py:257
  18.1 32.2 %all-to-all-start = ((bf16[32,24,256]{2,1,0:T(8,128)(2,1)}), bf16[32,24,256]{2,1,0:T(8,128)(2,1)S(1)}, u32[]{:S(2)}, u32[]{:S(2)}) async-start(bf16[32,24,256]{2,1,0:T(8,128)(2,1)} %bitcast.25), calls=%async_computation | async-start | bytes 786432 | tf_op jit(solution)/shard_map/all_to_all | solution.py:310
  23.2 145.5 %all-gather.5.cloned.1.call-start = ((), (), s32[]{:S(2)}) async-start(), calls=%async_computation.5 | async-start | bytes 3649536 | tf_op jit(solution)/shard_map/all_gather | solution.py:781
  23.7 10.9 %collective-permute-start.3 = (bf16[2,2,32,768]{3,2,1,0:T(8,128)(2,1)S(1)}, bf16[2,2,32,768]{3,2,1,0:T(8,128)(2,1)S(1)}, u32[]{:S(2)}, u32[]{:S(2)}) collective-permute-start(bf16[2,2,32,768]{3,2,1,0:T(8,128)(2,1)S(1)} %get-tuple-element.105), channel_id=1, source_target_pairs={{0,4},{4,0},{8,12},{12,8},{16,20},{20,16},{24,28},{28,24},{1,5},{5... | collective-permute-start | bytes 589832 | tf_op jit(solution)/shard_map/ppermute | solution.py:257
  25.5 10.2 %collective-permute-start.5 = (bf16[2,2,32,768]{3,2,1,0:T(8,128)(2,1)S(1)}, bf16[2,2,32,768]{3,2,1,0:T(8,128)(2,1)S(1)}, u32[]{:S(2)}, u32[]{:S(2)}) collective-permute-start(bf16[2,2,32,768]{3,2,1,0:T(8,128)(2,1)S(1)} %get-tuple-element.108), channel_id=1, source_target_pairs={{0,2},{1,3},{2,0},{3,1},{4,6},{5,7},{6,4},{7,5},{8,10},{9,11},{10,... | collective-permute-start | bytes 589832 | tf_op jit(solution)/shard_map/ppermute | solution.py:257
  34.7 15.3 %collective-permute-start.4 = (bf16[2,2,2,32,768]{4,3,2,1,0:T(8,128)(2,1)S(1)}, bf16[2,2,2,32,768]{4,3,2,1,0:T(8,128)(2,1)S(1)}, u32[]{:S(2)}, u32[]{:S(2)}) collective-permute-start(bf16[2,2,2,32,768]{4,3,2,1,0:T(8,128)(2,1)S(1)} %maximum_select_fusion.4), channel_id=1, source_target_pairs={{0,2},{1,3},{2,0},{3,1},{4,6},{5,7},{6,4},{7,5},{8,10},{9,11},{10,... | collective-permute-start | bytes 1179656 | tf_op jit(solution)/shard_map/ppermute | solution.py:257
  35.7 14.2 %collective-permute-start.6 = (bf16[2,2,2,32,768]{4,3,2,1,0:T(8,128)(2,1)S(1)}, bf16[2,2,2,32,768]{4,3,2,1,0:T(8,128)(2,1)S(1)}, u32[]{:S(2)}, u32[]{:S(2)}) collective-permute-start(bf16[2,2,2,32,768]{4,3,2,1,0:T(8,128)(2,1)S(1)} %maximum_select_fusion.6), channel_id=1, source_target_pairs={{0,4},{4,0},{8,12},{12,8},{16,20},{20,16},{24,28},{28,24},{1,5},{5... | collective-permute-start | bytes 1179656 | tf_op jit(solution)/shard_map/ppermute | solution.py:257
  50.3 3.5 %copy-start = (bf16[2,2,2,2,2,32,768]{6,5,4,3,2,1,0:T(8,128)(2,1)}, bf16[2,2,2,2,2,32,768]{6,5,4,3,2,1,0:T(8,128)(2,1)S(1)}, u32[]{:S(2)}) copy-start(bf16[2,2,2,2,2,32,768]{6,5,4,3,2,1,0:T(8,128)(2,1)S(1)} %pad_maximum_fusion) | copy-start | bytes 4718596
  50.3 3.5 %copy-start.2 = (bf16[32,24,256]{2,1,0:T(8,128)(2,1)}, bf16[32,24,256]{2,1,0:T(8,128)(2,1)S(1)}, u32[]{:S(2)}) copy-start(bf16[32,24,256]{2,1,0:T(8,128)(2,1)S(1)} %all-to-all-done) | copy-start | bytes 1179652
  50.3 3.5 %collective-permute-start.7 = (bf16[1024,768]{1,0:T(8,128)(2,1)S(1)}, bf16[1024,768]{1,0:T(8,128)(2,1)S(1)}, u32[]{:S(2)}, u32[]{:S(2)}) collective-permute-start(bf16[1024,768]{1,0:T(8,128)(2,1)S(1)} %bitcast.91), channel_id=1, source_target_pairs={{0,1},{1,0},{2,3},{3,2},{4,5},{5,4},{6,7},{7,6},{8,9},{9,8},{10,11... | collective-permute-start | bytes 4718600 | tf_op jit(solution)/shard_map/ppermute | solution.py:257
  53.8 1.2 copy-start.3
  73.8 19.1 %all-to-all-start.1 = ((bf16[32,32,128]{2,1,0:T(8,128)(2,1)}), bf16[32,32,128]{2,1,0:T(8,128)(2,1)S(1)}, u32[]{:S(2)}, u32[]{:S(2)}) async-start(bf16[32,32,128]{2,1,0:T(8,128)(2,1)} %bitcast.115), calls=%async_computation.1 | async-start | bytes 524288 | tf_op jit(solution)/shard_map/all_to_all | solution.py:310
  92.9 1.9 copy-start.4
  103.3 3.8 %collective-permute-start.8 = (bf16[128,6528]{1,0:T(8,128)(2,1)}, bf16[128,6528]{1,0:T(8,128)(2,1)S(1)}, u32[]{:S(2)}, u32[]{:S(2)}) collective-permute-start(bf16[128,6528]{1,0:T(8,128)(2,1)} %get-tuple-element.62.acts), channel_id=1, source_target_pairs={{0,1},{1,0},{2,3},{3,2},{4,5},{5,4},{6,7},{7,6},{8,9},{9,8},{10,11... | collective-permute-start | bytes 5013512 | tf_op jit(solution)/shard_map/ppermute | solution.py:257
  103.5 15.0 %all-to-all-start.2 = ((bf16[32,32,128]{2,1,0:T(8,128)(2,1)}), bf16[32,32,128]{2,1,0:T(8,128)(2,1)S(1)}, u32[]{:S(2)}, u32[]{:S(2)}) async-start(bf16[32,32,128]{2,1,0:T(8,128)(2,1)} %get-tuple-element.61), calls=%async_computation.2 | async-start | bytes 524288 | tf_op jit(solution)/shard_map/all_to_all | solution.py:310
  107.1 1.2 copy-start.10
  118.5 1.7 copy-start.9
  118.5 24.2 %collective-permute-start.9 = (bf16[2,2,2,24,2304]{4,3,2,1,0:T(8,128)(2,1)}, bf16[2,2,2,24,2304]{4,3,2,1,0:T(8,128)(2,1)S(1)}, u32[]{:S(2)}, u32[]{:S(2)}) collective-permute-start(bf16[2,2,2,24,2304]{4,3,2,1,0:T(8,128)(2,1)} %bitcast.122), channel_id=1, source_target_pairs={{0,4},{4,0},{8,12},{12,8},{16,20},{20,16},{24,28},{28,24},{1,5},{5... | collective-permute-start | bytes 2654216 | tf_op jit(solution)/shard_map/ppermute | solution.py:257
  119.3 19.2 %collective-permute-start.10 = (bf16[2,2,2,24,1920]{4,3,2,1,0:T(8,128)(2,1)}, bf16[2,2,2,24,1920]{4,3,2,1,0:T(8,128)(2,1)S(1)}, u32[]{:S(2)}, u32[]{:S(2)}) collective-permute-start(bf16[2,2,2,24,1920]{4,3,2,1,0:T(8,128)(2,1)} %bitcast.123), channel_id=1, source_target_pairs={{0,2},{1,3},{2,0},{3,1},{4,6},{5,7},{6,4},{7,5},{8,10},{9,11},{10,... | collective-permute-start | bytes 2211848 | tf_op jit(solution)/shard_map/ppermute | solution.py:257
  120.2 22.6 %copy-start.6 = (bf16[4,2,24,1920]{3,2,1,0:T(8,128)(2,1)S(1)}, bf16[4,2,24,1920]{3,2,1,0:T(8,128)(2,1)}, u32[]{:S(2)}) copy-start(bf16[4,2,24,1920]{3,2,1,0:T(8,128)(2,1)} %get-tuple-element.75) | copy-start | bytes 2211844
  138.5 4.3 %copy-start.7 = (bf16[2,2,2,24,1920]{4,3,2,1,0:T(8,128)(2,1)}, bf16[2,2,2,24,1920]{4,3,2,1,0:T(8,128)(2,1)S(1)}, u32[]{:S(2)}) copy-start(bf16[2,2,2,24,1920]{4,3,2,1,0:T(8,128)(2,1)S(1)} %collective-permute-done.10) | copy-start | bytes 2211844
  142.8 2.5 %copy-start.5 = (bf16[2,2,2,24,2304]{4,3,2,1,0:T(8,128)(2,1)}, bf16[2,2,2,24,2304]{4,3,2,1,0:T(8,128)(2,1)S(1)}, u32[]{:S(2)}) copy-start(bf16[2,2,2,24,2304]{4,3,2,1,0:T(8,128)(2,1)S(1)} %collective-permute-done.9) | copy-start | bytes 2654212
  144.4 24.4 %collective-permute-start.11 = (bf16[2,2,24,1920]{3,2,1,0:T(8,128)(2,1)S(1)}, bf16[2,2,24,1920]{3,2,1,0:T(8,128)(2,1)S(1)}, u32[]{:S(2)}, u32[]{:S(2)}) collective-permute-start(bf16[2,2,24,1920]{3,2,1,0:T(8,128)(2,1)S(1)} %dynamic-slice_bitcast_fusion.1), channel_id=1, source_target_pairs={{0,4},{4,0},{8,12},{12,8},{16,20},{20,16},{24,28},{28,24},{1,5},{5... | collective-permute-start | bytes 1105928 | tf_op jit(solution)/shard_map/ppermute | solution.py:257
  145.2 46.8 %all-to-all-start.3 = ((bf16[32,136,128]{2,1,0:T(8,128)(2,1)}), bf16[32,136,128]{2,1,0:T(8,128)(2,1)S(1)}, u32[]{:S(2)}, u32[]{:S(2)}) async-start(bf16[32,136,128]{2,1,0:T(8,128)(2,1)} %bitcast.105), calls=%async_computation.3 | async-start | bytes 2228224 | tf_op jit(solution)/shard_map/all_to_all | solution.py:310
  150.9 22.2 %collective-permute-start.12 = (bf16[2,2,24,2304]{3,2,1,0:T(8,128)(2,1)}, bf16[2,2,24,2304]{3,2,1,0:T(8,128)(2,1)}, u32[]{:S(2)}, u32[]{:S(2)}) collective-permute-start(bf16[2,2,24,2304]{3,2,1,0:T(8,128)(2,1)} %dynamic-slice_bitcast_fusion), channel_id=1, source_target_pairs={{0,2},{1,3},{2,0},{3,1},{4,6},{5,7},{6,4},{7,5},{8,10},{9,11},{10,... | collective-permute-start | bytes 1327112 | tf_op jit(solution)/shard_map/ppermute | solution.py:257
  168.9 22.6 %collective-permute-start.16 = (bf16[24,1920]{1,0:T(8,128)(2,1)S(1)}, bf16[24,1920]{1,0:T(8,128)(2,1)S(1)}, u32[]{:S(2)}, u32[]{:S(2)}) collective-permute-start(bf16[24,1920]{1,0:T(8,128)(2,1)S(1)} %get-tuple-element.113), channel_id=1, source_target_pairs={{0,16},{4,20},{8,24},{12,28},{16,0},{20,4},{24,8},{28,12},{1,17},{... | collective-permute-start | bytes 276488 | tf_op jit(solution)/shard_map/ppermute | solution.py:257
  171.2 26.5 %collective-permute-start.17 = (bf16[24,1920]{1,0:T(8,128)(2,1)S(1)}, bf16[24,1920]{1,0:T(8,128)(2,1)S(1)}, u32[]{:S(2)}, u32[]{:S(2)}) collective-permute-start(bf16[24,1920]{1,0:T(8,128)(2,1)S(1)} %get-tuple-element.112), channel_id=1, source_target_pairs={{0,24},{4,28},{8,16},{12,20},{16,8},{20,12},{24,0},{28,4},{1,25},{... | collective-permute-start | bytes 276488 | tf_op jit(solution)/shard_map/ppermute | solution.py:257
  173.0 24.7 %collective-permute-start.18 = (bf16[24,1920]{1,0:T(8,128)(2,1)S(1)}, bf16[24,1920]{1,0:T(8,128)(2,1)S(1)}, u32[]{:S(2)}, u32[]{:S(2)}) collective-permute-start(bf16[24,1920]{1,0:T(8,128)(2,1)S(1)} %get-tuple-element.111), channel_id=1, source_target_pairs={{0,8},{4,12},{8,0},{12,4},{16,24},{20,28},{24,16},{28,20},{1,9},{5... | collective-permute-start | bytes 276488 | tf_op jit(solution)/shard_map/ppermute | solution.py:257
  174.2 23.6 %collective-permute-start.13 = (bf16[24,2304]{1,0:T(8,128)(2,1)S(1)}, bf16[24,2304]{1,0:T(8,128)(2,1)S(1)}, u32[]{:S(2)}, u32[]{:S(2)}) collective-permute-start(bf16[24,2304]{1,0:T(8,128)(2,1)S(1)} %get-tuple-element.102), channel_id=1, source_target_pairs={{0,16},{4,20},{8,24},{12,28},{16,0},{20,4},{24,8},{28,12},{1,17},{... | collective-permute-start | bytes 331784 | tf_op jit(solution)/shard_map/ppermute | solution.py:257
  176.9 20.9 %collective-permute-start.14 = (bf16[24,2304]{1,0:T(8,128)(2,1)S(1)}, bf16[24,2304]{1,0:T(8,128)(2,1)S(1)}, u32[]{:S(2)}, u32[]{:S(2)}) collective-permute-start(bf16[24,2304]{1,0:T(8,128)(2,1)S(1)} %get-tuple-element.101), channel_id=1, source_target_pairs={{0,24},{4,28},{8,16},{12,20},{16,8},{20,12},{24,0},{28,4},{1,25},{... | collective-permute-start | bytes 331784 | tf_op jit(solution)/shard_map/ppermute | solution.py:257
  191.5 6.3 %collective-permute-start.15 = (bf16[24,2304]{1,0:T(8,128)(2,1)S(1)}, bf16[24,2304]{1,0:T(8,128)(2,1)S(1)}, u32[]{:S(2)}, u32[]{:S(2)}) collective-permute-start(bf16[24,2304]{1,0:T(8,128)(2,1)S(1)} %get-tuple-element.100), channel_id=1, source_target_pairs={{0,8},{4,12},{8,0},{12,4},{16,24},{20,28},{24,16},{28,20},{1,9},{5... | collective-permute-start | bytes 331784 | tf_op jit(solution)/shard_map/ppermute | solution.py:257
  192.0 1.0 copy-start.1
  193.1 6.1 %copy-start.8 = (bf16[24,2304]{1,0:T(8,128)(2,1)S(1)}, bf16[24,2304]{1,0:T(8,128)(2,1)}, u32[]{:S(2)}) copy-start(bf16[24,2304]{1,0:T(8,128)(2,1)} %param.13) | copy-start | bytes 331780
Sparse Core Ops, SparseCore 0:
  11.4 83.2 all-gather.2
  97.6 71.1 all-gather.4

commit v6 on v5

--- a/solution.py
+++ b/solution.py
@@ -779,7 +779,7 @@
         hidden_one.reshape(length, model_width),
     )
     qkv_full = lax.all_gather(qkv_weight, AXES, axis=0, tiled=True)
-    send, came_a, came_b = lax.optimization_barrier((send, came_a, came_b))
+    send, came_b = lax.optimization_barrier((send, came_b))
     got = exchange(send.reshape(32, SENT, LANES))
     keep_a, give_a = halve(keep_a, came_a, "ulysses", 2, 2)
     keep_b, give_b = halve(keep_b, came_b, "blk", 1, 2)

time: 208 us -> 205 us (0.986)
  starting transfers between devices: 40.1 us -> 36.2 us
    ppermute x19, waiting for transfers between devices: 36.5 us -> 25.3 us  [swap(): return lax.ppermute(value, axis, [(i, i ^ bit) for i in range(size)])]
    all_gather x1, waiting for transfers between devices: 16.1 us -> 25.6 us  [owner_body(): qkv_full = lax.all_gather(qkv_weight, AXES, axis=0, tiled=True)]
    ppermute x19, starting transfers between devices: 24 us -> 20.2 us  [swap(): return lax.ppermute(value, axis, [(i, i ^ bit) for i in range(size)])]
  transfers between devices with their start and end apart: 25 -> 25, of which waited for: 10 -> 12; matrix products, arithmetic and copies ran while one was open for 9% -> 9% of each run, Pallas kernels for 26% -> 27%
where the time goes in v6:
time: 205 us; the launch traced here: 203 us
  waiting for transfers between devices  70.8 us (35%)
  Pallas kernels  54.5 us (27%)
  starting transfers between devices  36.2 us (18%)
  other arithmetic  15 us (7%)
  between operations  14.5 us (7%)
  local copies, waits for them, and re-layouts  12.3 us (6%)
    all_gather x1, waiting for transfers between devices, owner_body(): qkv_full = lax.all_gather(qkv_weight, AXES, axis=0, tiled=True)  25.6 us
    ppermute x19, waiting for transfers between devices, swap(): return lax.ppermute(value, axis, [(i, i ^ bit) for i in range(size)])  25.3 us
    ppermute x19, starting transfers between devices, swap(): return lax.ppermute(value, axis, [(i, i ^ bit) for i in range(size)])  20.2 us
    all_to_all x4, waiting for transfers between devices, exchange(): return lax.all_to_all(value, AXES, split_axis=0, concat_axis=0, tiled=True)  18 us
    pallas_call x1, Pallas kernels, attend_back(): pl.pallas_call(attend_back_kernel, grid=(steps,), in_specs=[pl.BlockSpec(...  16.3 us
    all_to_all x4, starting transfers between devices, exchange(): return lax.all_to_all(value, AXES, split_axis=0, concat_axis=0, tiled=True)  15.8 us
    pallas_call x1, Pallas kernels, attend(): pl.pallas_call(attend_kernel, grid=(steps,), in_specs=[by_row(HEAD), whol...  11.7 us
    pallas_call x1, Pallas kernels, middle_part(): pl.pallas_call(middle_kernel, out_shape=[jax.ShapeDtypeStruct(shape, kind...  8.51 us
  transfers between devices with their start and end apart: 25, of which 12 were waited for; matrix products, arithmetic and copies ran while one was open for 9% of the time, Pallas kernels for 27%

profile of v6, /device:TPU:0, one launch (start us, length us, event | category | flops | bytes accessed | tf_op | source)
XLA Modules:
  0.0 203.2 jit_solution(6549304883484471384)
XLA Ops:
  7.2 1.6 pad_maximum_fusion.2
  8.9 1.0 constant_dynamic-slice_fusion
  9.9 4.1 %collective-permute-start.1 = (bf16[64,768]{1,0:T(8,128)(2,1)S(1)}, bf16[64,768]{1,0:T(8,128)(2,1)S(1)}, u32[]{:S(2)}, u32[]{:S(2)}) collective-permute-start(bf16[64,768]{1,0:T(8,128)(2,1)S(1)} %get-tuple-element.114), channel_id=1, source_target_pairs={{0,16},{4,20},{8,24},{12,28},{16,0},{20,4},{24,8},{28,12},{1,17},{... | collective-permute-start | bytes 294920 | tf_op jit(solution)/shard_map/ppermute | solution.py:257
  14.0 1.3 collective-permute-start.2
  15.6 1.1 reshape.679
  18.1 5.2 %all-to-all-start = ((bf16[32,24,256]{2,1,0:T(8,128)(2,1)}), bf16[32,24,256]{2,1,0:T(8,128)(2,1)S(1)}, u32[]{:S(2)}, u32[]{:S(2)}) async-start(bf16[32,24,256]{2,1,0:T(8,128)(2,1)} %bitcast.25), calls=%async_computation | async-start | bytes 786432 | tf_op jit(solution)/shard_map/all_to_all | solution.py:310
  23.7 1.8 collective-permute-start.3
  25.5 1.5 collective-permute-start.5
  27.1 7.5 %collective-permute-done.3 = bf16[2,2,32,768]{3,2,1,0:T(8,128)(2,1)S(1)} collective-permute-done((bf16[2,2,32,768]{3,2,1,0:T(8,128)(2,1)S(1)}, bf16[2,2,32,768]{3,2,1,0:T(8,128)(2,1)S(1)}, u32[]{:S(2)}, u32[]{:S(2)}) %collective-permute-start.3) | collective-permute-done | bytes 196640 | tf_op jit(solution)/shard_map/ppermute | solution.py:257
  34.7 1.0 collective-permute-start.4
  35.7 0.9 collective-permute-start.6
  36.6 5.5 %multiply_sine_fusion = (f32[2048,128]{1,0:T(8,128)}, f32[2048,128]{1,0:T(8,128)}) fusion(f32[128]{0:T(128)S(1)} %fusion.35, f32[2048]{0:T(1024)S(1)} %fusion.23), kind=kLoop, calls=%fused_computation.3 | loop fusion | flops 262144 | bytes 2105856 | tf_op jit(solution)/shard_map/sin | solution.py:306
  42.3 7.6 %collective-permute-done.6 = bf16[2,2,2,32,768]{4,3,2,1,0:T(8,128)(2,1)S(1)} collective-permute-done((bf16[2,2,2,32,768]{4,3,2,1,0:T(8,128)(2,1)S(1)}, bf16[2,2,2,32,768]{4,3,2,1,0:T(8,128)(2,1)S(1)}, u32[]{:S(2)}, u32[]{:S(2)}) %collective-permute-start.6) | collective-permute-done | bytes 393248 | tf_op jit(solution)/shard_map/ppermute | solution.py:257
  50.7 0.8 reshape.701.gain
  51.5 2.3 %collective-permute-done.7.other = bf16[1024,768]{1,0:T(8,128)(2,1)S(1)} collective-permute-done((bf16[1024,768]{1,0:T(8,128)(2,1)S(1)}, bf16[1024,768]{1,0:T(8,128)(2,1)S(1)}, u32[]{:S(2)}, u32[]{:S(2)}) %collective-permute-start.7) | collective-permute-done | bytes 1572896 | tf_op jit(solution)/shard_map/ppermute | solution.py:257
  53.8 1.1 copy-done.3
  54.9 7.2 %project.1 = (bf16[2,1024,768]{2,1,0:T(8,128)(2,1)}, bf16[2,1024,64]{2,1,0:T(8,128)(2,1)}, bf16[2,1024,64]{2,1,0:T(8,128)(2,1)}, bf16[2,1024,64]{2,1,0:T(8,128)(2,1)}) custom-call(s32[1]{0:T(128)} %bitcast.core, bf16[1024,768]{1,0:T(8,128)(2,1)} %bitcast.92, bf16[1024,768]{1,0:T(8,128)(2,1)} %copy-done.3, f32[1,768]{1,0:T(1,128)} %reshape.701.gain, ...), custom_call_target="tpu_custom_call" | custom-call | tf_op jit(solution)/shard_map/project/pallas_call | solution.py:357
  62.1 11.7 %attend.1 = (bf16[2048,2048]{1,0:T(8,128)(2,1)}, f32[2048,64]{1,0:T(8,128)}, f32[2048,1]{1,0:T(8,128)}, bf16[16,2,32,128]{3,2,1,0:T(8,128)(2,1)}) custom-call(bf16[2048,64]{1,0:T(8,128)(2,1)} %bitcast.124, bf16[2048,64]{1,0:T(8,128)(2,1)} %bitcast.126, bf16[2048,64]{1,0:T(8,128)(2,1)} %bitcast.128), custom_call_target="tpu_custom_call" | custom-call | flops 4294967296 | bytes 8388608 | tf_op jit(solution)/shard_map/attend/pallas_call | solution.py:399
  73.8 4.7 %all-to-all-start.1 = ((bf16[32,32,128]{2,1,0:T(8,128)(2,1)}), bf16[32,32,128]{2,1,0:T(8,128)(2,1)S(1)}, u32[]{:S(2)}, u32[]{:S(2)}) async-start(bf16[32,32,128]{2,1,0:T(8,128)(2,1)} %bitcast.115), calls=%async_computation.1 | async-start | bytes 524288 | tf_op jit(solution)/shard_map/all_to_all | solution.py:310
  79.0 13.8 %all-to-all-done.1.got = bf16[32,32,128]{2,1,0:T(8,128)(2,1)S(1)} async-done(((bf16[32,32,128]{2,1,0:T(8,128)(2,1)}), bf16[32,32,128]{2,1,0:T(8,128)(2,1)S(1)}, u32[]{:S(2)}, u32[]{:S(2)}) %all-to-all-start.1) | async-done | bytes 262176 | tf_op jit(solution)/shard_map/all_to_all | solution.py:310
  92.9 1.9 all-gather.3.cloned.1.call-done.late
  94.7 8.5 %middle_part.1 = (bf16[128,768]{1,0:T(8,128)(2,1)}, bf16[32,32,128]{2,1,0:T(8,128)(2,1)}, bf16[128,6528]{1,0:T(8,128)(2,1)}, f32[128,768]{1,0:T(8,128)}) custom-call(bf16[32,32,128]{2,1,0:T(8,128)(2,1)} %copy-done.4, bf16[128,768]{1,0:T(8,128)(2,1)} %bitcast.97, bf16[768,4224]{1,0:T(8,128)(2,1)} %all-gather.3.cloned.1.call-done.late, ...), custom_call_target="tpu_custom_call" | custom-call | tf_op jit(solution)/shard_map/middle_part/pallas_call | solution.py:494
  103.5 2.9 %all-to-all-start.2 = ((bf16[32,32,128]{2,1,0:T(8,128)(2,1)}), bf16[32,32,128]{2,1,0:T(8,128)(2,1)S(1)}, u32[]{:S(2)}, u32[]{:S(2)}) async-start(bf16[32,32,128]{2,1,0:T(8,128)(2,1)} %get-tuple-element.60), calls=%async_computation.2 | async-start | bytes 524288 | tf_op jit(solution)/shard_map/all_to_all | solution.py:310
  107.1 1.2 copy-done.10
  108.3 6.1 %weight_grads.1 = (bf16[4,2,24,2304]{3,2,1,0:T(8,128)(2,1)}, bf16[4,2,24,2304]{3,2,1,0:T(8,128)(2,1)}, bf16[4,2,24,1920]{3,2,1,0:T(8,128)(2,1)}, bf16[4,2,24,1920]{3,2,1,0:T(8,128)(2,1)}) custom-call(s32[3]{0:T(128)} %pad_add_fusion.place, bf16[128,6528]{1,0:T(8,128)(2,1)} %get-tuple-element.61.acts, bf16[128,6528]{1,0:T(8,128)(2,1)} %copy-done.10), custom_call_target="tpu_custom_call" | custom-call | flops 1660944384 | bytes 9830400 | tf_op jit(solution)/shard_map/weight_grads/pallas_call | solution.py:544
  114.4 4.2 %all-to-all-done.2 = bf16[32,32,128]{2,1,0:T(8,128)(2,1)S(1)} async-done(((bf16[32,32,128]{2,1,0:T(8,128)(2,1)}), bf16[32,32,128]{2,1,0:T(8,128)(2,1)S(1)}, u32[]{:S(2)}, u32[]{:S(2)}) %all-to-all-start.2) | async-done | bytes 262176 | tf_op jit(solution)/shard_map/all_to_all | solution.py:310
  118.7 1.5 collective-permute-start.11
  120.2 16.3 %attend_back.1 = bf16[16,2,136,128]{3,2,1,0:T(8,128)(2,1)} custom-call(bf16[16,2,32,128]{3,2,1,0:T(8,128)(2,1)} %bitcast.114, f32[2048,64]{1,0:T(8,128)} %get-tuple-element.67.attn32, f32[2048,1]{1,0:T(8,128)} %get-tuple-element.68.total, bf16[2048,2048]{1,0:T(8,128)(2,1)} %get-tuple-element.69.weights, bf16[2048,64]{1,0:T(8,128)(2,1)} %bitcast.125, ...), custom_call_target="tpu_custom_call" | custom-call | flops 15032385536 | bytes 8388608 | tf_op jit(solution)/shard_map/attend_back/pallas_call | solution.py:629
  136.5 1.5 collective-permute-done.9
  138.0 0.9 copy-done.7
  138.9 1.3 fusion.1
  140.2 0.8 collective-permute-start.10
  141.0 3.1 %all-to-all-start.3 = ((bf16[32,136,128]{2,1,0:T(8,128)(2,1)}), bf16[32,136,128]{2,1,0:T(8,128)(2,1)S(1)}, u32[]{:S(2)}, u32[]{:S(2)}) async-start(bf16[32,136,128]{2,1,0:T(8,128)(2,1)} %bitcast.105), calls=%async_computation.3 | async-start | bytes 2228224 | tf_op jit(solution)/shard_map/all_to_all | solution.py:310
  144.1 1.9 collective-permute-done.11
  146.0 0.9 copy-done.5
  146.9 1.7 fusion
  148.6 0.8 dynamic-slice_bitcast_fusion
  149.4 25.6 %all-gather.5.cloned.1.call-done.weight = bf16[768,2304]{1,0:T(8,128)(2,1)} async-done(((bf16[24,2304]{1,0:T(8,128)(2,1)}), bf16[768,2304]{1,0:T(8,128)(2,1)}) %all-gather.5.cloned.1.call-update) | async-done | bytes 3538960 | tf_op jit(solution)/shard_map/all_gather | solution.py:781
  175.2 2.0 collective-permute-start.17
  177.2 1.5 collective-permute-start.18
  178.7 1.1 fusion.2
  179.9 1.0 collective-permute-start.13
  180.9 1.9 collective-permute-start.14
  182.8 1.8 collective-permute-done.16
  185.2 1.0 copy-done.1
  186.2 4.7 %last_part.1 = (bf16[128,768]{1,0:T(8,128)(2,1)}, f32[24,2304]{1,0:T(8,128)}, f32[24]{0:T(128)}) custom-call(bf16[32,136,128]{2,1,0:T(8,128)(2,1)} %copy-done.1, bf16[768,2304]{1,0:T(8,128)(2,1)} %all-gather.5.cloned.1.call-done.weight, bf16[128,768]{1,0:T(8,128)(2,1)} %bitcast.98, f32[1,768]{1,0:T(1,128)} %reshape.701.gain, ...), custom_call_target="tpu_custom_call" | custom-call | tf_op jit(solution)/shard_map/last_part/pallas_call | solution.py:704
  190.9 2.3 %collective-permute-done.13 = bf16[24,2304]{1,0:T(8,128)(2,1)S(1)} collective-permute-done((bf16[24,2304]{1,0:T(8,128)(2,1)S(1)}, bf16[24,2304]{1,0:T(8,128)(2,1)S(1)}, u32[]{:S(2)}, u32[]{:S(2)}) %collective-permute-start.13) | collective-permute-done | bytes 110624 | tf_op jit(solution)/shard_map/ppermute | solution.py:257
  194.9 0.9 multiply_reduce_fusion
  (78 shorter events, 7.6 us)
Async XLA Ops:
  7.2 9.9 %copy-start.11 = (bf16[24]{0:T(256)(128)(2,1)S(1)}, bf16[24]{0:T(256)(128)(2,1)}, u32[]{:S(2)}) copy-start(bf16[24]{0:T(256)(128)(2,1)} %param.9) | copy-start | bytes 148
  7.2 9.9 %copy-start.12 = (bf16[24]{0:T(256)(128)(2,1)S(1)}, bf16[24]{0:T(256)(128)(2,1)}, u32[]{:S(2)}) copy-start(bf16[24]{0:T(256)(128)(2,1)} %param.12) | copy-start | bytes 148
  7.2 87.5 %all-gather.3.cloned.1.call-start = ((), (), s32[]{:S(2)}) async-start(), calls=%async_computation.4 | async-start | bytes 6690816 | tf_op jit(solution)/shard_map/all_gather | solution.py:728
  9.9 13.5 %collective-permute-start.1 = (bf16[64,768]{1,0:T(8,128)(2,1)S(1)}, bf16[64,768]{1,0:T(8,128)(2,1)S(1)}, u32[]{:S(2)}, u32[]{:S(2)}) collective-permute-start(bf16[64,768]{1,0:T(8,128)(2,1)S(1)} %get-tuple-element.114), channel_id=1, source_target_pairs={{0,16},{4,20},{8,24},{12,28},{16,0},{20,4},{24,8},{28,12},{1,17},{... | collective-permute-start | bytes 294920 | tf_op jit(solution)/shard_map/ppermute | solution.py:257
  14.0 9.4 %collective-permute-start.2 = (bf16[64,768]{1,0:T(8,128)(2,1)S(1)}, bf16[64,768]{1,0:T(8,128)(2,1)S(1)}, u32[]{:S(2)}, u32[]{:S(2)}) collective-permute-start(bf16[64,768]{1,0:T(8,128)(2,1)S(1)} %get-tuple-element.114), channel_id=1, source_target_pairs={{0,24},{4,28},{8,16},{12,20},{16,8},{20,12},{24,0},{28,4},{1,25},{... | collective-permute-start | bytes 294920 | tf_op jit(solution)/shard_map/ppermute | solution.py:257
  15.4 8.0 %collective-permute-start = (bf16[64,768]{1,0:T(8,128)(2,1)S(1)}, bf16[64,768]{1,0:T(8,128)(2,1)S(1)}, u32[]{:S(2)}, u32[]{:S(2)}) collective-permute-start(bf16[64,768]{1,0:T(8,128)(2,1)S(1)} %bitcast.111), channel_id=1, source_target_pairs={{0,8},{4,12},{8,0},{12,4},{16,24},{20,28},{24,16},{28,20},{1,9},{5... | collective-permute-start | bytes 294920 | tf_op jit(solution)/shard_map/ppermute | solution.py:257
  18.1 32.2 %all-to-all-start = ((bf16[32,24,256]{2,1,0:T(8,128)(2,1)}), bf16[32,24,256]{2,1,0:T(8,128)(2,1)S(1)}, u32[]{:S(2)}, u32[]{:S(2)}) async-start(bf16[32,24,256]{2,1,0:T(8,128)(2,1)} %bitcast.25), calls=%async_computation | async-start | bytes 786432 | tf_op jit(solution)/shard_map/all_to_all | solution.py:310
  23.2 151.8 %all-gather.5.cloned.1.call-start = ((), (), s32[]{:S(2)}) async-start(), calls=%async_computation.5 | async-start | bytes 3649536 | tf_op jit(solution)/shard_map/all_gather | solution.py:781
  23.7 10.9 %collective-permute-start.3 = (bf16[2,2,32,768]{3,2,1,0:T(8,128)(2,1)S(1)}, bf16[2,2,32,768]{3,2,1,0:T(8,128)(2,1)S(1)}, u32[]{:S(2)}, u32[]{:S(2)}) collective-permute-start(bf16[2,2,32,768]{3,2,1,0:T(8,128)(2,1)S(1)} %get-tuple-element.103), channel_id=1, source_target_pairs={{0,4},{4,0},{8,12},{12,8},{16,20},{20,16},{24,28},{28,24},{1,5},{5... | collective-permute-start | bytes 589832 | tf_op jit(solution)/shard_map/ppermute | solution.py:257
  25.5 10.2 %collective-permute-start.5 = (bf16[2,2,32,768]{3,2,1,0:T(8,128)(2,1)S(1)}, bf16[2,2,32,768]{3,2,1,0:T(8,128)(2,1)S(1)}, u32[]{:S(2)}, u32[]{:S(2)}) collective-permute-start(bf16[2,2,32,768]{3,2,1,0:T(8,128)(2,1)S(1)} %get-tuple-element.106), channel_id=1, source_target_pairs={{0,2},{1,3},{2,0},{3,1},{4,6},{5,7},{6,4},{7,5},{8,10},{9,11},{10,... | collective-permute-start | bytes 589832 | tf_op jit(solution)/shard_map/ppermute | solution.py:257
  34.7 15.3 %collective-permute-start.4 = (bf16[2,2,2,32,768]{4,3,2,1,0:T(8,128)(2,1)S(1)}, bf16[2,2,2,32,768]{4,3,2,1,0:T(8,128)(2,1)S(1)}, u32[]{:S(2)}, u32[]{:S(2)}) collective-permute-start(bf16[2,2,2,32,768]{4,3,2,1,0:T(8,128)(2,1)S(1)} %maximum_select_fusion.4), channel_id=1, source_target_pairs={{0,2},{1,3},{2,0},{3,1},{4,6},{5,7},{6,4},{7,5},{8,10},{9,11},{10,... | collective-permute-start | bytes 1179656 | tf_op jit(solution)/shard_map/ppermute | solution.py:257
  35.7 14.2 %collective-permute-start.6 = (bf16[2,2,2,32,768]{4,3,2,1,0:T(8,128)(2,1)S(1)}, bf16[2,2,2,32,768]{4,3,2,1,0:T(8,128)(2,1)S(1)}, u32[]{:S(2)}, u32[]{:S(2)}) collective-permute-start(bf16[2,2,2,32,768]{4,3,2,1,0:T(8,128)(2,1)S(1)} %maximum_select_fusion.6), channel_id=1, source_target_pairs={{0,4},{4,0},{8,12},{12,8},{16,20},{20,16},{24,28},{28,24},{1,5},{5... | collective-permute-start | bytes 1179656 | tf_op jit(solution)/shard_map/ppermute | solution.py:257
  50.3 3.5 %copy-start = (bf16[2,2,2,2,2,32,768]{6,5,4,3,2,1,0:T(8,128)(2,1)}, bf16[2,2,2,2,2,32,768]{6,5,4,3,2,1,0:T(8,128)(2,1)S(1)}, u32[]{:S(2)}) copy-start(bf16[2,2,2,2,2,32,768]{6,5,4,3,2,1,0:T(8,128)(2,1)S(1)} %pad_maximum_fusion) | copy-start | bytes 4718596
  50.3 3.5 %copy-start.2 = (bf16[32,24,256]{2,1,0:T(8,128)(2,1)}, bf16[32,24,256]{2,1,0:T(8,128)(2,1)S(1)}, u32[]{:S(2)}) copy-start(bf16[32,24,256]{2,1,0:T(8,128)(2,1)S(1)} %all-to-all-done) | copy-start | bytes 1179652
  50.3 3.5 %collective-permute-start.7 = (bf16[1024,768]{1,0:T(8,128)(2,1)S(1)}, bf16[1024,768]{1,0:T(8,128)(2,1)S(1)}, u32[]{:S(2)}, u32[]{:S(2)}) collective-permute-start(bf16[1024,768]{1,0:T(8,128)(2,1)S(1)} %bitcast.91), channel_id=1, source_target_pairs={{0,1},{1,0},{2,3},{3,2},{4,5},{5,4},{6,7},{7,6},{8,9},{9,8},{10,11... | collective-permute-start | bytes 4718600 | tf_op jit(solution)/shard_map/ppermute | solution.py:257
  53.8 1.2 copy-start.3
  73.8 19.1 %all-to-all-start.1 = ((bf16[32,32,128]{2,1,0:T(8,128)(2,1)}), bf16[32,32,128]{2,1,0:T(8,128)(2,1)S(1)}, u32[]{:S(2)}, u32[]{:S(2)}) async-start(bf16[32,32,128]{2,1,0:T(8,128)(2,1)} %bitcast.115), calls=%async_computation.1 | async-start | bytes 524288 | tf_op jit(solution)/shard_map/all_to_all | solution.py:310
  92.9 1.9 copy-start.4
  103.3 3.8 %collective-permute-start.8 = (bf16[128,6528]{1,0:T(8,128)(2,1)}, bf16[128,6528]{1,0:T(8,128)(2,1)S(1)}, u32[]{:S(2)}, u32[]{:S(2)}) collective-permute-start(bf16[128,6528]{1,0:T(8,128)(2,1)} %get-tuple-element.61.acts), channel_id=1, source_target_pairs={{0,1},{1,0},{2,3},{3,2},{4,5},{5,4},{6,7},{7,6},{8,9},{9,8},{10,11... | collective-permute-start | bytes 5013512 | tf_op jit(solution)/shard_map/ppermute | solution.py:257
  103.5 15.0 %all-to-all-start.2 = ((bf16[32,32,128]{2,1,0:T(8,128)(2,1)}), bf16[32,32,128]{2,1,0:T(8,128)(2,1)S(1)}, u32[]{:S(2)}, u32[]{:S(2)}) async-start(bf16[32,32,128]{2,1,0:T(8,128)(2,1)} %get-tuple-element.60), calls=%async_computation.2 | async-start | bytes 524288 | tf_op jit(solution)/shard_map/all_to_all | solution.py:310
  107.1 1.2 copy-start.10
  118.5 1.7 copy-start.9
  118.5 19.5 %collective-permute-start.9 = (bf16[2,2,2,24,1920]{4,3,2,1,0:T(8,128)(2,1)}, bf16[2,2,2,24,1920]{4,3,2,1,0:T(8,128)(2,1)S(1)}, u32[]{:S(2)}, u32[]{:S(2)}) collective-permute-start(bf16[2,2,2,24,1920]{4,3,2,1,0:T(8,128)(2,1)} %bitcast.123), channel_id=1, source_target_pairs={{0,2},{1,3},{2,0},{3,1},{4,6},{5,7},{6,4},{7,5},{8,10},{9,11},{10,... | collective-permute-start | bytes 2211848 | tf_op jit(solution)/shard_map/ppermute | solution.py:257
  118.7 27.3 %collective-permute-start.11 = (bf16[2,2,2,24,2304]{4,3,2,1,0:T(8,128)(2,1)}, bf16[2,2,2,24,2304]{4,3,2,1,0:T(8,128)(2,1)S(1)}, u32[]{:S(2)}, u32[]{:S(2)}) collective-permute-start(bf16[2,2,2,24,2304]{4,3,2,1,0:T(8,128)(2,1)} %bitcast.122), channel_id=1, source_target_pairs={{0,4},{4,0},{8,12},{12,8},{16,20},{20,16},{24,28},{28,24},{1,5},{5... | collective-permute-start | bytes 2654216 | tf_op jit(solution)/shard_map/ppermute | solution.py:257
  120.2 18.7 %copy-start.6 = (bf16[4,2,24,1920]{3,2,1,0:T(8,128)(2,1)S(1)}, bf16[4,2,24,1920]{3,2,1,0:T(8,128)(2,1)}, u32[]{:S(2)}) copy-start(bf16[4,2,24,1920]{3,2,1,0:T(8,128)(2,1)} %get-tuple-element.73) | copy-start | bytes 2211844
  138.0 0.9 copy-start.7
  140.2 34.8 %collective-permute-start.10 = (bf16[2,2,24,1920]{3,2,1,0:T(8,128)(2,1)S(1)}, bf16[2,2,24,1920]{3,2,1,0:T(8,128)(2,1)S(1)}, u32[]{:S(2)}, u32[]{:S(2)}) collective-permute-start(bf16[2,2,24,1920]{3,2,1,0:T(8,128)(2,1)S(1)} %dynamic-slice_bitcast_fusion.1), channel_id=1, source_target_pairs={{0,4},{4,0},{8,12},{12,8},{16,20},{20,16},{24,28},{28,24},{1,5},{5... | collective-permute-start | bytes 1105928 | tf_op jit(solution)/shard_map/ppermute | solution.py:257
  141.0 44.2 %all-to-all-start.3 = ((bf16[32,136,128]{2,1,0:T(8,128)(2,1)}), bf16[32,136,128]{2,1,0:T(8,128)(2,1)S(1)}, u32[]{:S(2)}, u32[]{:S(2)}) async-start(bf16[32,136,128]{2,1,0:T(8,128)(2,1)} %bitcast.105), calls=%async_computation.3 | async-start | bytes 2228224 | tf_op jit(solution)/shard_map/all_to_all | solution.py:310
  146.0 0.9 copy-start.5
  149.4 29.3 %collective-permute-start.12 = (bf16[2,2,24,2304]{3,2,1,0:T(8,128)(2,1)}, bf16[2,2,24,2304]{3,2,1,0:T(8,128)(2,1)}, u32[]{:S(2)}, u32[]{:S(2)}) collective-permute-start(bf16[2,2,24,2304]{3,2,1,0:T(8,128)(2,1)} %dynamic-slice_bitcast_fusion), channel_id=1, source_target_pairs={{0,2},{1,3},{2,0},{3,1},{4,6},{5,7},{6,4},{7,5},{8,10},{9,11},{10,... | collective-permute-start | bytes 1327112 | tf_op jit(solution)/shard_map/ppermute | solution.py:257
  175.2 9.5 %collective-permute-start.16 = (bf16[24,1920]{1,0:T(8,128)(2,1)S(1)}, bf16[24,1920]{1,0:T(8,128)(2,1)S(1)}, u32[]{:S(2)}, u32[]{:S(2)}) collective-permute-start(bf16[24,1920]{1,0:T(8,128)(2,1)S(1)} %get-tuple-element.111), channel_id=1, source_target_pairs={{0,16},{4,20},{8,24},{12,28},{16,0},{20,4},{24,8},{28,12},{1,17},{... | collective-permute-start | bytes 276488 | tf_op jit(solution)/shard_map/ppermute | solution.py:257
  175.2 15.7 %collective-permute-start.17 = (bf16[24,1920]{1,0:T(8,128)(2,1)S(1)}, bf16[24,1920]{1,0:T(8,128)(2,1)S(1)}, u32[]{:S(2)}, u32[]{:S(2)}) collective-permute-start(bf16[24,1920]{1,0:T(8,128)(2,1)S(1)} %get-tuple-element.110), channel_id=1, source_target_pairs={{0,24},{4,28},{8,16},{12,20},{16,8},{20,12},{24,0},{28,4},{1,25},{... | collective-permute-start | bytes 276488 | tf_op jit(solution)/shard_map/ppermute | solution.py:257
  177.2 13.7 %collective-permute-start.18 = (bf16[24,1920]{1,0:T(8,128)(2,1)S(1)}, bf16[24,1920]{1,0:T(8,128)(2,1)S(1)}, u32[]{:S(2)}, u32[]{:S(2)}) collective-permute-start(bf16[24,1920]{1,0:T(8,128)(2,1)S(1)} %get-tuple-element.109), channel_id=1, source_target_pairs={{0,8},{4,12},{8,0},{12,4},{16,24},{20,28},{24,16},{28,20},{1,9},{5... | collective-permute-start | bytes 276488 | tf_op jit(solution)/shard_map/ppermute | solution.py:257
  179.9 13.3 %collective-permute-start.13 = (bf16[24,2304]{1,0:T(8,128)(2,1)S(1)}, bf16[24,2304]{1,0:T(8,128)(2,1)S(1)}, u32[]{:S(2)}, u32[]{:S(2)}) collective-permute-start(bf16[24,2304]{1,0:T(8,128)(2,1)S(1)} %get-tuple-element.100), channel_id=1, source_target_pairs={{0,16},{4,20},{8,24},{12,28},{16,0},{20,4},{24,8},{28,12},{1,17},{... | collective-permute-start | bytes 331784 | tf_op jit(solution)/shard_map/ppermute | solution.py:257
  180.9 12.3 %collective-permute-start.14 = (bf16[24,2304]{1,0:T(8,128)(2,1)S(1)}, bf16[24,2304]{1,0:T(8,128)(2,1)S(1)}, u32[]{:S(2)}, u32[]{:S(2)}) collective-permute-start(bf16[24,2304]{1,0:T(8,128)(2,1)S(1)} %get-tuple-element.99), channel_id=1, source_target_pairs={{0,24},{4,28},{8,16},{12,20},{16,8},{20,12},{24,0},{28,4},{1,25},{... | collective-permute-start | bytes 331784 | tf_op jit(solution)/shard_map/ppermute | solution.py:257
  184.7 8.9 %collective-permute-start.15 = (bf16[24,2304]{1,0:T(8,128)(2,1)S(1)}, bf16[24,2304]{1,0:T(8,128)(2,1)S(1)}, u32[]{:S(2)}, u32[]{:S(2)}) collective-permute-start(bf16[24,2304]{1,0:T(8,128)(2,1)S(1)} %get-tuple-element.98), channel_id=1, source_target_pairs={{0,8},{4,12},{8,0},{12,4},{16,24},{20,28},{24,16},{28,20},{1,9},{5... | collective-permute-start | bytes 331784 | tf_op jit(solution)/shard_map/ppermute | solution.py:257
  185.2 1.0 copy-start.1
  186.2 8.7 %copy-start.8 = (bf16[24,2304]{1,0:T(8,128)(2,1)S(1)}, bf16[24,2304]{1,0:T(8,128)(2,1)}, u32[]{:S(2)}) copy-start(bf16[24,2304]{1,0:T(8,128)(2,1)} %param.13) | copy-start | bytes 331780
Sparse Core Ops, SparseCore 0:
  11.4 83.2 all-gather.2
  97.6 77.3 all-gather.4
